TPU v7x, 256 devices: a whole 4x4x8 slice. The times are simulated.
256 devices in a mesh: group: 4 (over y), dom: 64 (over z, x, core).
Axes of the slice: x: 4, y: 4, z: 8, core: 2. Of those that a mesh axis runs over, the one named last changes fastest.
Arguments:
- node_lat: bfloat16 [524288, 256], P(('group', 'dom')), may hold values from -6 to 6
- edge_lat: bfloat16 [2097152, 256], P(('group', 'dom')), may hold values from -6 to 6
- edge_send: int32 [2097152], P(('group', 'dom')), may hold values from 0 to 3071, as said below
- halo_list: int32 [262144], P(('group', 'dom')), may hold values from 0 to 2047
- pool_id: int32 [524288], P(('group', 'dom')), may hold values from 0 to 1023
- coarse_lat: bfloat16 [65536, 256], P(('group', 'dom')), may hold values from -6 to 6
- cedge_lat: bfloat16 [262144, 256], P(('group', 'dom')), may hold values from -6 to 6
- cedge_send: int32 [262144], P(('group', 'dom')), may hold values from 0 to 511, as said below
- chalo_list: int32 [65536], P(('group', 'dom')), may hold values from 0 to 255
- fine_edge_in: bfloat16 [3, 256, 256], replicated, may hold values from -0.21875 to 0.21875
- fine_edge_out: bfloat16 [256, 256], replicated, may hold values from -0.375 to 0.375
- fine_node_in: bfloat16 [2, 256, 256], replicated, may hold values from -0.25 to 0.25
- fine_node_out: bfloat16 [256, 256], replicated, may hold values from -0.375 to 0.375
- fine_bias: float32 [4, 256], replicated, may hold values from -3 to 3
- fine_gain: float32 [2, 256], replicated, may hold values from 0.1 to 1.9
- coarse_edge_in: bfloat16 [3, 256, 256], replicated, may hold values from -0.21875 to 0.21875
- coarse_edge_out: bfloat16 [256, 256], replicated, may hold values from -0.375 to 0.375
- coarse_node_in: bfloat16 [2, 256, 256], replicated, may hold values from -0.25 to 0.25
- coarse_node_out: bfloat16 [256, 256], replicated, may hold values from -0.375 to 0.375
- coarse_bias: float32 [4, 256], replicated, may hold values from -3 to 3
- coarse_gain: float32 [2, 256], replicated, may hold values from 0.1 to 1.9
Outputs:
- fine_out: bfloat16 [524288, 256], P(('group', 'dom'))
- coarse_out: bfloat16 [65536, 256], P(('group', 'dom'))
Inputs may be any that keep to these rules, and one draw needn't show every extreme that they name: `edge_send`: indices into the block's extended rows: below 512 the lower neighbour's rows, from 2560 on the upper neighbour's; a block never names the rows of a neighbour it lacks. `cedge_send`: indices into the block's extended coarse rows: below 128 the lower neighbour's rows, from 384 on the upper neighbour's; a block never names the rows of a neighbour it lacks.
All inputs are finite; a program needn't handle non-finite values.
Results may differ from a plain program's by a relative error of at most 0.012.
Values may be sent and summed in bfloat16 or wider, within the bound.
No kernel may reach another device: no remote copies, remote signals or barrier semaphores. Data moves between devices by JAX's collectives and lax.ppermute only.
A program may use at most 128 MiB of HBM per device.

v0:
```python
import jax
import jax.numpy as jnp
from jax import lax
from jax.sharding import PartitionSpec as P

EPSILON = 1e-05


def padded(block, sides, width):
    for axis, dim in sides:
        count = lax.axis_size(axis)
        forward = [(i, i + 1) for i in range(count - 1)]
        backward = [(target, source) for source, target in forward]
        low = lax.ppermute(
            lax.slice_in_dim(block, block.shape[dim] - width, None, axis=dim), axis, forward
        )
        high = lax.ppermute(lax.slice_in_dim(block, 0, width, axis=dim), axis, backward)
        block = jnp.concatenate([low, block, high], axis=dim)
    return block


def cut_along(x, dim, count):
    before, after = (x.shape[:dim], x.shape[dim + 1 :])
    return jnp.moveaxis(x.reshape(*before, count, -1, *after), dim, 0)


def sum_at_owner(x, axis, dim):
    count = lax.axis_size(axis)
    blocks = lax.all_to_all(cut_along(x, dim, count), axis, 0, 0, tiled=True)
    return jnp.sum(blocks.astype(jnp.float32), axis=0)


def in_one_piece(arrays, axis, dim, along):
    columns = [a.reshape(*a.shape[:along], -1) for a in arrays]
    both = jnp.concatenate(columns, axis=along)
    result, at, gathered = (sum_at_owner(both, axis, dim), 0, [])
    for a, column in zip(arrays, columns):
        share = result[..., at : at + column.shape[along]]
        gathered.append(share.reshape(*share.shape[:along], *a.shape[along:]))
        at += column.shape[along]
    return tuple(gathered)


def layer_norm_rows(values):
    row_mean = jnp.mean(values, axis=-1, keepdims=True)
    centred = values - row_mean
    variance = jnp.mean(centred * centred, axis=-1, keepdims=True)
    return centred * lax.rsqrt(variance + EPSILON)


def edge_node(
    sender_proj, own_rows, edge_rows, senders, edge_in, edge_out, node_in, node_out, biases, gains
):
    node_count = own_rows.shape[0]
    width = own_rows.shape[1]
    fanin = edge_rows.shape[0] // node_count
    receiver_proj = jnp.dot(own_rows, edge_in[1], preferred_element_type=jnp.float32)
    edge_pre = jnp.dot(edge_rows, edge_in[2], preferred_element_type=jnp.float32)
    edge_pre = edge_pre + sender_proj[senders].astype(jnp.float32) + biases[0]
    edge_pre = (edge_pre.reshape(node_count, fanin, width) + receiver_proj[:, None, :]).reshape(
        node_count * fanin, width
    )
    edge_hidden = jnp.maximum(edge_pre, 0.0).astype(jnp.bfloat16)
    message = (
        layer_norm_rows(
            jnp.dot(edge_hidden, edge_out, preferred_element_type=jnp.float32) + biases[1]
        )
        * gains[0]
    )
    message = message.astype(jnp.bfloat16)
    summed = jnp.sum(message.astype(jnp.float32).reshape(node_count, fanin, width), axis=1).astype(
        jnp.bfloat16
    )
    node_pre = jnp.dot(own_rows, node_in[0], preferred_element_type=jnp.float32)
    node_pre = (
        node_pre + jnp.dot(summed, node_in[1], preferred_element_type=jnp.float32) + biases[2]
    )
    node_hidden = jnp.maximum(node_pre, 0.0).astype(jnp.bfloat16)
    update = (
        layer_norm_rows(
            jnp.dot(node_hidden, node_out, preferred_element_type=jnp.float32) + biases[3]
        )
        * gains[1]
    )
    return (own_rows.astype(jnp.float32) + update).astype(jnp.bfloat16)


def project(rows_in, weight):
    return jnp.dot(rows_in, weight, preferred_element_type=jnp.float32).astype(jnp.bfloat16)


def join_rim(extended_rows, own_rows, rim_rows):
    return jnp.concatenate(
        [extended_rows[:rim_rows], own_rows, extended_rows[3 * rim_rows :]], axis=0
    )


def body(
    node_lat,
    edge_lat,
    edge_send,
    halo_list,
    pool_id,
    coarse_lat,
    cedge_lat,
    cedge_send,
    chalo_list,
    fine_edge_in,
    fine_edge_out,
    fine_node_in,
    fine_node_out,
    fine_bias,
    fine_gain,
    coarse_edge_in,
    coarse_edge_out,
    coarse_node_in,
    coarse_node_out,
    coarse_bias,
    coarse_gain,
):
    rim_rows = halo_list.shape[0] // 2
    extended_rows = padded(node_lat[halo_list], (("dom", 0),), rim_rows)
    sender_proj = project(join_rim(extended_rows, node_lat, rim_rows), fine_edge_in[0])
    fine_out = edge_node(
        sender_proj,
        node_lat,
        edge_lat,
        edge_send,
        fine_edge_in,
        fine_edge_out,
        fine_node_in,
        fine_node_out,
        fine_bias,
        fine_gain,
    )
    groups = lax.axis_size("group")
    cluster_rows = coarse_lat.shape[0]
    columns = groups * cluster_rows
    member_table = (pool_id[:, None] == jnp.arange(columns, dtype=jnp.int32)[None, :]).astype(
        jnp.bfloat16
    )
    cluster_sum = jnp.einsum(
        "nc,nh->ch", member_table, fine_out, preferred_element_type=jnp.float32
    )
    member_count = jnp.sum(member_table, axis=0, dtype=jnp.float32)
    cluster_sum, member_count = in_one_piece(
        (cluster_sum.astype(jnp.bfloat16), member_count.astype(jnp.bfloat16)), "group", 0, 1
    )
    pooled_mean = cluster_sum / jnp.maximum(member_count, 1.0)[:, None]
    coarse_in = (coarse_lat.astype(jnp.float32) + pooled_mean).astype(jnp.bfloat16)
    coarse_rim = chalo_list.shape[0] // 2
    coarse_ext = padded(coarse_in[chalo_list], (("dom", 0),), coarse_rim)
    coarse_sender = project(join_rim(coarse_ext, coarse_in, coarse_rim), coarse_edge_in[0])
    coarse_out = edge_node(
        coarse_sender,
        coarse_in,
        cedge_lat,
        cedge_send,
        coarse_edge_in,
        coarse_edge_out,
        coarse_node_in,
        coarse_node_out,
        coarse_bias,
        coarse_gain,
    )
    return (fine_out, coarse_out)


def solution(mesh):
    placed = (
        P(("group", "dom"), None),
        P(("group", "dom"), None),
        P(("group", "dom")),
        P(("group", "dom")),
        P(("group", "dom")),
        P(("group", "dom"), None),
        P(("group", "dom"), None),
        P(("group", "dom")),
        P(("group", "dom")),
        P(),
        P(),
        P(),
        P(),
        P(),
        P(),
        P(),
        P(),
        P(),
        P(),
        P(),
        P(),
    )
    return jax.shard_map(
        body,
        mesh=mesh,
        in_specs=placed,
        out_specs=(P(("group", "dom"), None), P(("group", "dom"), None)),
        check_vma=False,
    )
```

profile of v0, /device:TPU:103, one launch (start us, length us, event | category | flops | bytes accessed | tf_op | source)
XLA Modules:
  0.0 167.8 jit_solution(10681137921550769504)
XLA Ops:
  0.7 0.8 fusion.74
  1.5 4.9 %gather_fusion = bf16[1024,256]{1,0:T(8,128)(2,1)S(1)} fusion(bf16[2048,256]{1,0:T(8,128)(2,1)} %param.21, s32[1024]{0:T(1024)S(1)} %fusion.74), kind=kCustom, calls=%fused_computation | custom fusion | bytes 1052672 | tf_op jit(solution)/shard_map/gather | solution.py:122
  6.4 5.2 %collective-permute-start = (bf16[512,256]{1,0:T(8,128)(2,1)S(1)}, bf16[512,256]{1,0:T(8,128)(2,1)S(1)}, u32[]{:S(2)}, u32[]{:S(2)}) collective-permute-start(bf16[512,256]{1,0:T(8,128)(2,1)S(1)} %get-tuple-element.12), channel_id=1, source_target_pairs={{0,1},{1,2},{2,3},{3,4},{4,5},{5,6},{6,7},{7,8},{8,9},{9,10},{10,1... | collective-permute-start | bytes 786440 | tf_op jit(solution)/shard_map/ppermute | solution.py:14
  11.7 1.9 %collective-permute-start.1 = (bf16[512,256]{1,0:T(8,128)(2,1)S(1)}, bf16[512,256]{1,0:T(8,128)(2,1)}, u32[]{:S(2)}, u32[]{:S(2)}) collective-permute-start(bf16[512,256]{1,0:T(8,128)(2,1)S(1)} %get-tuple-element.13), channel_id=1, source_target_pairs={{1,0},{2,1},{3,2},{4,3},{5,4},{6,5},{7,6},{8,7},{9,8},{10,9},{11,1... | collective-permute-start | bytes 786440 | tf_op jit(solution)/shard_map/ppermute | solution.py:17
  13.6 0.6 fusion.85
  14.2 2.7 %fusion.50 = f32[2048,256]{1,0:T(8,128)} fusion(bf16[2048,256]{1,0:T(8,128)(2,1)S(1)} %copy-done.2, bf16[3,256,256]{2,1,0:T(8,128)(2,1)} %param.30), kind=kOutput, calls=%fused_computation.70 | convolution fusion | flops 268435456 | bytes 3276800 | tf_op jit(solution)/shard_map/dot_general | solution.py:57
  16.9 0.6 fusion.87
  17.5 1.8 %fusion.55 = f32[2048,256]{1,0:T(8,128)} fusion(bf16[2048,256]{1,0:T(8,128)(2,1)S(1)} %copy-done.2, bf16[2,256,256]{2,1,0:T(8,128)(2,1)S(1)} %copy-done.4), kind=kOutput, calls=%fused_computation.74 | convolution fusion | flops 268435456 | bytes 3276800 | tf_op jit(solution)/shard_map/dot_general | solution.py:74
  19.2 1.0 fusion.5
  20.3 1.4 copy.60
  21.7 5.7 %add.199 = f32[2048,4,256]{2,1,0:T(4,128)} broadcast(f32[2048,256]{1,0:T(8,128)} %fusion.50), dimensions={0,2} | broadcast | bytes 10485760 | tf_op jit(solution)/shard_map/add | solution.py:60
  27.5 10.0 %add.200 = f32[8192,256]{1,0:T(8,128)} reshape(f32[2048,4,256]{2,1,0:T(4,128)} %add.199) | data formatting | bytes 16777216 | tf_op jit(solution)/shard_map/add | solution.py:60
  37.6 0.6 fusion.73
  38.2 0.7 copy-done.25
  38.9 1.6 convolution_convert_fusion
  40.6 35.8 %gather_fusion.1 = bf16[8192,256]{1,0:T(8,128)(2,1)} fusion(bf16[3072,256]{1,0:T(8,128)(2,1)S(1)} %convolution_convert_fusion, s32[8192]{0:T(1024)} %fusion.73), kind=kCustom, calls=%fused_computation.1 | custom fusion | bytes 8421376 | tf_op jit(solution)/shard_map/gather | solution.py:59
  76.4 11.6 %fusion.88 = (f32[8192]{0:T(1024)S(1)}, f32[8192,256]{1,0:T(8,128)}) fusion(f32[256]{0:T(256)S(1)} %bitcast.76, bf16[256,256]{1,0:T(8,128)(2,1)S(1)} %copy-done.7, f32[8192,256]{1,0:T(8,128)} %add.200, bf16[8192,256]{1,0:T(8,128)(2,1)} %param.22, bf16[8192,256]{1,0:T(8,128)(2,1)} %gather_fusion.1, f32[256]{0:T(256)S(1)} %bitcast.77, ...), kind=kOutput, calls=%fused_computation.117 | convolution fusion | flops 2164252672 | bytes 25462784 | tf_op jit(solution)/shard_map/dot_general | solution.py:66
  88.0 5.4 %multiply_reduce_fusion = f32[8192]{0:T(1024)S(1)} fusion(f32[8192,256]{1,0:T(8,128)} %get-tuple-element.29, f32[8192]{0:T(1024)S(1)} %broadcast_multiply_fusion), kind=kLoop, calls=%fused_computation.12 | loop fusion | flops 6283264 | bytes 8454144 | tf_op jit(solution)/shard_map/reduce_sum | solution.py:47
  93.5 0.4 copy-done.1
  93.9 5.4 %multiply_convert_fusion = bf16[8192,256]{1,0:T(8,128)(2,1)} fusion(f32[8192,256]{1,0:T(8,128)S(1)} %copy-done.1, f32[256]{0:T(256)S(1)} %bitcast.71, f32[8192]{0:T(1024)S(1)} %add_rsqrt_fusion, f32[8192]{0:T(1024)S(1)} %broadcast_multiply_fusion), kind=kLoop, calls=%fused_computation.11 | loop fusion | flops 8388608 | bytes 12649472 | tf_op jit(solution)/shard_map/convert_element_type | solution.py:70
  99.2 6.9 %reshape.79 = bf16[2048,4,256]{2,1,0:T(4,128)(2,1)} reshape(bf16[8192,256]{1,0:T(8,128)(2,1)} %multiply_convert_fusion) | data formatting | bytes 8388608 | tf_op jit(solution)/shard_map/reshape | solution.py:71
  106.1 12.3 %reduce.1 = bf16[2048,256]{1,0:T(8,128)(2,1)} reduce(bf16[2048,4,256]{2,1,0:T(4,128)(2,1)} %reshape.79, bf16[]{:T(256)} %constant.16.clone.1), dimensions={1}, to_apply=%region_2.0.clone | reduce | flops 1572864 | bytes 5242882 | tf_op jit(solution)/shard_map/reduce_sum | solution.py:71
  118.5 2.8 %fusion.91 = (f32[2048]{0:T(1024)S(1)}, f32[2048,256]{0,1:T(8,128)S(1)}) fusion(f32[256]{0:T(256)S(1)} %bitcast.75, bf16[256,256]{1,0:T(8,128)(2,1)S(1)} %copy-done.8, f32[2048,256]{1,0:T(8,128)} %fusion.55, bf16[2048,256]{1,0:T(8,128)(2,1)} %reduce.1, f32[256]{0:T(256)S(1)} %bitcast.74, bf16[2,256,256]{2,1,0:T(8,128)(2,1)S(1)} %copy-done.4), kind=kOutput, calls=%fused_computation.118 | convolution fusion | flops 540014592 | bytes 5515264 | tf_op jit(solution)/shard_map/dot_general | solution.py:81
  121.3 0.2 multiply_reduce_fusion.1
  121.6 1.7 %add_convert_fusion = bf16[2048,256]{0,1:T(8,128)(2,1)S(1)} fusion(bf16[2048,256]{0,1:T(8,128)(2,1)} %copy.60, f32[2048,256]{0,1:T(8,128)S(1)} %get-tuple-element.31, f32[256]{0:T(256)S(1)} %bitcast.70, f32[2048]{0:T(1024)S(1)} %add_rsqrt_fusion.1, f32[2048]{0:T(1024)S(1)} %broadcast_multiply_fusion.1), kind=kLoop, calls=%fused_computation.23 | loop fusion | flops 3145728 | bytes 4211712 | tf_op jit(solution)/shard_map/convert_element_type | solution.py:85
  123.3 1.0 copy-done.3
  124.3 1.7 %fusion.21 = bf16[1024,256]{1,0:T(8,128)(2,1)S(1)} fusion(bf16[2048,256]{0,1:T(8,128)(2,1)S(1)} %add_convert_fusion, s32[2048]{0:T(1024)S(1)} %copy-done.27), kind=kOutput, calls=%fused_computation.36 | convolution fusion | flops 1078198272 | bytes 1581056 | tf_op jit(solution)/shard_map/nc,nh->ch/dot_general | solution.py:142
  126.2 0.8 pad_maximum_fusion
  127.0 4.2 %all-to-all-start = ((bf16[4,256,257]{1,2,0:T(8,128)(2,1)}), bf16[4,256,257]{1,2,0:T(8,128)(2,1)S(1)}, u32[]{:S(2)}, u32[]{:S(2)}) async-start(bf16[4,256,257]{1,2,0:T(8,128)(2,1)} %pad_maximum_fusion), calls=%async_computation | async-start | bytes 1081344 | tf_op jit(solution)/shard_map/all_to_all | solution.py:29
  131.2 0.6 fusion.86
  131.8 0.6 fusion.84
  132.4 2.3 %copy.69 = bf16[2048,256]{1,0:T(8,128)(2,1)} copy(bf16[2048,256]{0,1:T(8,128)(2,1)} %copy-done.3) | data formatting | bytes 2097152
  134.6 6.4 %all-to-all-done = bf16[4,256,257]{1,2,0:T(8,128)(2,1)S(1)} async-done(((bf16[4,256,257]{1,2,0:T(8,128)(2,1)}), bf16[4,256,257]{1,2,0:T(8,128)(2,1)S(1)}, u32[]{:S(2)}, u32[]{:S(2)}) %all-to-all-start) | async-done | bytes 526368 | tf_op jit(solution)/shard_map/all_to_all | solution.py:29
  141.6 1.2 gather_fusion.2
  142.8 5.5 %collective-permute-start.2 = (bf16[128,256]{0,1:T(8,128)(2,1)S(1)}, bf16[128,256]{0,1:T(8,128)(2,1)S(1)}, u32[]{:S(2)}, u32[]{:S(2)}) collective-permute-start(bf16[128,256]{0,1:T(8,128)(2,1)S(1)} %copy.73), channel_id=1, source_target_pairs={{0,1},{1,2},{2,3},{3,4},{4,5},{5,6},{6,7},{7,8},{8,9},{9,10},{10,1... | collective-permute-start | bytes 196616 | tf_op jit(solution)/shard_map/ppermute | solution.py:14
  148.5 1.9 %collective-permute-start.3 = (bf16[128,256]{0,1:T(8,128)(2,1)S(1)}, bf16[128,256]{0,1:T(8,128)(2,1)S(1)}, u32[]{:S(2)}, u32[]{:S(2)}) collective-permute-start(bf16[128,256]{0,1:T(8,128)(2,1)S(1)} %copy.74), channel_id=1, source_target_pairs={{1,0},{2,1},{3,2},{4,3},{5,4},{6,5},{7,6},{8,7},{9,8},{10,9},{11,1... | collective-permute-start | bytes 196616 | tf_op jit(solution)/shard_map/ppermute | solution.py:17
  150.4 1.1 fusion.41
  151.6 0.2 fusion.46
  152.0 0.4 add.227
  152.4 5.0 %collective-permute-done.3 = bf16[128,256]{0,1:T(8,128)(2,1)S(1)} collective-permute-done((bf16[128,256]{0,1:T(8,128)(2,1)S(1)}, bf16[128,256]{0,1:T(8,128)(2,1)S(1)}, u32[]{:S(2)}, u32[]{:S(2)}) %collective-permute-start.3) | collective-permute-done | bytes 65568 | tf_op jit(solution)/shard_map/ppermute | solution.py:17
  157.4 1.2 convolution_convert_fusion.1
  158.6 3.9 %gather_fusion.3 = bf16[1024,256]{1,0:T(8,128)(2,1)S(1)} fusion(bf16[512,256]{1,0:T(8,128)(2,1)S(1)} %convolution_convert_fusion.1, s32[1024]{0:T(1024)S(1)} %fusion.75), kind=kCustom, calls=%fused_computation.3 | custom fusion | bytes 1052672 | tf_op jit(solution)/shard_map/gather | solution.py:59
  162.6 1.6 fusion.94
  164.2 0.4 multiply_reduce_fusion.2
  164.6 0.3 multiply_convert_fusion.1
  165.1 0.7 reduce.2
  165.8 1.1 fusion.97
  167.1 0.8 copy.70
  (84 shorter events, 1.7 us)
Async XLA Ops:
  0.6 161.9 %copy-start = (bf16[1024,256]{1,0:T(8,128)(2,1)S(1)}, bf16[1024,256]{1,0:T(8,128)(2,1)}, u32[]{:S(2)}) copy-start(bf16[1024,256]{1,0:T(8,128)(2,1)} %param.27) | copy-start | bytes 1572868
  0.6 13.6 %copy-start.2 = (bf16[2048,256]{1,0:T(8,128)(2,1)S(1)}, bf16[2048,256]{1,0:T(8,128)(2,1)}, u32[]{:S(2)}) copy-start(bf16[2048,256]{1,0:T(8,128)(2,1)} %param.21) | copy-start | bytes 3145732
  0.7 13.0 %copy-start.18 = (f32[4,256]{1,0:T(4,128)S(1)}, f32[4,256]{1,0:T(4,128)}, u32[]{:S(2)}) copy-start(f32[4,256]{1,0:T(4,128)} %param.34) | copy-start | bytes 12292
  1.5 15.4 %copy-start.22 = (f32[2,256]{1,0:T(2,128)S(1)}, f32[2,256]{1,0:T(2,128)}, u32[]{:S(2)}) copy-start(f32[2,256]{1,0:T(2,128)} %param.35) | copy-start | bytes 6148
  1.5 16.0 %copy-start.4 = (bf16[2,256,256]{2,1,0:T(8,128)(2,1)S(1)}, bf16[2,256,256]{2,1,0:T(8,128)(2,1)}, u32[]{:S(2)}) copy-start(bf16[2,256,256]{2,1,0:T(8,128)(2,1)} %param.32) | copy-start | bytes 786436
  6.4 12.9 %copy-start.26 = (s32[2048]{0:T(1024)S(1)}, s32[2048]{0:T(1024)}, u32[]{:S(2)}) copy-start(s32[2048]{0:T(1024)} %param.25) | copy-start | bytes 24580
  6.4 13.9 %copy-start.24 = (s32[256]{0:T(256)S(1)}, s32[256]{0:T(256)}, u32[]{:S(2)}) copy-start(s32[256]{0:T(256)} %param.29) | copy-start | bytes 3076
  6.4 13.9 %copy-start.19 = (s32[1024]{0:T(1024)S(1)}, s32[1024]{0:T(1024)}, u32[]{:S(2)}) copy-start(s32[1024]{0:T(1024)} %param.28) | copy-start | bytes 12292
  6.4 31.8 %collective-permute-start = (bf16[512,256]{1,0:T(8,128)(2,1)S(1)}, bf16[512,256]{1,0:T(8,128)(2,1)S(1)}, u32[]{:S(2)}, u32[]{:S(2)}) collective-permute-start(bf16[512,256]{1,0:T(8,128)(2,1)S(1)} %get-tuple-element.12), channel_id=1, source_target_pairs={{0,1},{1,2},{2,3},{3,4},{4,5},{5,6},{6,7},{7,8},{8,9},{9,10},{10,1... | collective-permute-start | bytes 786440 | tf_op jit(solution)/shard_map/ppermute | solution.py:14
  11.7 27.3 %collective-permute-start.1 = (bf16[512,256]{1,0:T(8,128)(2,1)S(1)}, bf16[512,256]{1,0:T(8,128)(2,1)}, u32[]{:S(2)}, u32[]{:S(2)}) collective-permute-start(bf16[512,256]{1,0:T(8,128)(2,1)S(1)} %get-tuple-element.13), channel_id=1, source_target_pairs={{1,0},{2,1},{3,2},{4,3},{5,4},{6,5},{7,6},{8,7},{9,8},{10,9},{11,1... | collective-permute-start | bytes 786440 | tf_op jit(solution)/shard_map/ppermute | solution.py:17
  27.4 10.1 %copy-start.9 = (bf16[256,256]{1,0:T(8,128)(2,1)S(1)}, bf16[256,256]{1,0:T(8,128)(2,1)}, u32[]{:S(2)}) copy-start(bf16[256,256]{1,0:T(8,128)(2,1)} %param.26) | copy-start | bytes 393220
  27.4 10.2 %copy-start.11 = (s32[8192]{0:T(1024)S(1)}, s32[8192]{0:T(1024)}, u32[]{:S(2)}) copy-start(s32[8192]{0:T(1024)} %param.23) | copy-start | bytes 98308
  38.2 0.7 copy-start.25
  40.6 35.8 %copy-start.7 = (bf16[256,256]{1,0:T(8,128)(2,1)S(1)}, bf16[256,256]{1,0:T(8,128)(2,1)}, u32[]{:S(2)}) copy-start(bf16[256,256]{1,0:T(8,128)(2,1)} %param.31) | copy-start | bytes 393220
  40.6 35.8 %copy-start.16 = (f32[1,256]{1,0:T(1,128)S(1)}, f32[1,256]{1,0:T(1,128)}, u32[]{:S(2)}) copy-start(f32[1,256]{1,0:T(1,128)} %get-tuple-element.21) | copy-start | bytes 3076
  40.6 35.8 %copy-start.17 = (f32[1,256]{1,0:T(1,128)S(1)}, f32[1,256]{1,0:T(1,128)}, u32[]{:S(2)}) copy-start(f32[1,256]{1,0:T(1,128)} %get-tuple-element.22) | copy-start | bytes 3076
  88.0 5.8 %copy-start.1 = (f32[8192,256]{1,0:T(8,128)S(1)}, f32[8192,256]{1,0:T(8,128)}, u32[]{:S(2)}) copy-start(f32[8192,256]{1,0:T(8,128)} %get-tuple-element.29) | copy-start | bytes 25165828
  88.0 5.8 %copy-start.12 = (f32[1,256]{1,0:T(1,128)S(1)}, f32[1,256]{1,0:T(1,128)}, u32[]{:S(2)}) copy-start(f32[1,256]{1,0:T(1,128)} %get-tuple-element.27) | copy-start | bytes 3076
  106.1 12.3 %copy-start.8 = (bf16[256,256]{1,0:T(8,128)(2,1)S(1)}, bf16[256,256]{1,0:T(8,128)(2,1)}, u32[]{:S(2)}) copy-start(bf16[256,256]{1,0:T(8,128)(2,1)} %param.33) | copy-start | bytes 393220
  106.1 12.3 %copy-start.14 = (f32[1,256]{1,0:T(1,128)S(1)}, f32[1,256]{1,0:T(1,128)}, u32[]{:S(2)}) copy-start(f32[1,256]{1,0:T(1,128)} %get-tuple-element.20) | copy-start | bytes 3076
  106.1 12.3 %copy-start.15 = (f32[1,256]{1,0:T(1,128)S(1)}, f32[1,256]{1,0:T(1,128)}, u32[]{:S(2)}) copy-start(f32[1,256]{1,0:T(1,128)} %get-tuple-element.23) | copy-start | bytes 3076
  121.3 3.0 %copy-start.27 = (s32[2048]{0:T(1024)S(1)}, s32[2048]{0:T(1024)}, u32[]{:S(2)}) copy-start(s32[2048]{0:T(1024)} %param.25) | copy-start | bytes 24580
  123.3 1.0 copy-start.3
  124.3 6.9 %copy-start.23 = (f32[2,256]{1,0:T(2,128)S(1)}, f32[2,256]{1,0:T(2,128)}, u32[]{:S(2)}) copy-start(f32[2,256]{1,0:T(2,128)} %param.41) | copy-start | bytes 6148
  124.3 7.5 %copy-start.20 = (f32[4,256]{1,0:T(4,128)S(1)}, f32[4,256]{1,0:T(4,128)}, u32[]{:S(2)}) copy-start(f32[4,256]{1,0:T(4,128)} %param.40) | copy-start | bytes 12292
  126.2 25.4 %copy-start.5 = (bf16[2,256,256]{2,1,0:T(8,128)(2,1)S(1)}, bf16[2,256,256]{2,1,0:T(8,128)(2,1)}, u32[]{:S(2)}) copy-start(bf16[2,256,256]{2,1,0:T(8,128)(2,1)} %param.38) | copy-start | bytes 786436
  127.0 14.0 %all-to-all-start = ((bf16[4,256,257]{1,2,0:T(8,128)(2,1)}), bf16[4,256,257]{1,2,0:T(8,128)(2,1)S(1)}, u32[]{:S(2)}, u32[]{:S(2)}) async-start(bf16[4,256,257]{1,2,0:T(8,128)(2,1)} %pad_maximum_fusion), calls=%async_computation | async-start | bytes 1081344 | tf_op jit(solution)/shard_map/all_to_all | solution.py:29
  142.8 9.5 %collective-permute-start.2 = (bf16[128,256]{0,1:T(8,128)(2,1)S(1)}, bf16[128,256]{0,1:T(8,128)(2,1)S(1)}, u32[]{:S(2)}, u32[]{:S(2)}) collective-permute-start(bf16[128,256]{0,1:T(8,128)(2,1)S(1)} %copy.73), channel_id=1, source_target_pairs={{0,1},{1,2},{2,3},{3,4},{4,5},{5,6},{6,7},{7,8},{8,9},{9,10},{10,1... | collective-permute-start | bytes 196616 | tf_op jit(solution)/shard_map/ppermute | solution.py:14
  148.5 8.9 %collective-permute-start.3 = (bf16[128,256]{0,1:T(8,128)(2,1)S(1)}, bf16[128,256]{0,1:T(8,128)(2,1)S(1)}, u32[]{:S(2)}, u32[]{:S(2)}) collective-permute-start(bf16[128,256]{0,1:T(8,128)(2,1)S(1)} %copy.74), channel_id=1, source_target_pairs={{1,0},{2,1},{3,2},{4,3},{5,4},{6,5},{7,6},{8,7},{9,8},{10,9},{11,1... | collective-permute-start | bytes 196616 | tf_op jit(solution)/shard_map/ppermute | solution.py:17
  152.0 10.6 %copy-start.13 = (f32[1,256]{1,0:T(1,128)S(1)}, f32[1,256]{1,0:T(1,128)}, u32[]{:S(2)}) copy-start(f32[1,256]{1,0:T(1,128)} %get-tuple-element.17) | copy-start | bytes 3076
  162.5 2.0 %copy-start.21 = (f32[1,256]{1,0:T(1,128)S(1)}, f32[1,256]{1,0:T(1,128)}, u32[]{:S(2)}) copy-start(f32[1,256]{1,0:T(1,128)} %get-tuple-element.25) | copy-start | bytes 3076
  164.2 1.6 copy-start.6
  164.2 1.6 copy-start.10
where the time goes:
time: 169 us; the launch traced here: 168 us
  local copies, waits for them, and re-layouts  78.9 us (47%)
  other arithmetic  30.1 us (18%)
  matrix products  27.3 us (16%)
  starting transfers between devices  18.8 us (11%)
  waiting for transfers between devices  11.4 us (7%)
    gather x2, local copies, waits for them, and re-layouts, edge_node(): edge_pre = edge_pre + sender_proj[senders].astype(jnp.float32) + biases[0]  39.7 us
    add x4, local copies, waits for them, and re-layouts, edge_node(): edge_pre.reshape(node_count, fanin, width) + receiver_proj[:, None, :]  16.3 us
    dot_general x2, matrix products, edge_node(): jnp.dot(edge_hidden, edge_out, preferred_element_type=jnp.float32)  13.2 us
    reduce_sum x2, other arithmetic, edge_node(): jnp.sum(message.astype(jnp.float32).reshape(node_count, fanin, width), ax...  13 us
    ppermute x2, starting transfers between devices, padded(): lax.ppermute(lax.slice_in_dim(block, block.shape[dim] - width, None, axis...  10.8 us
    unnamed x63, local copies, waits for them, and re-layouts  7.08 us
    reshape x2, local copies, waits for them, and re-layouts, edge_node(): message.astype(jnp.float32).reshape(node_count, fanin, width)  7.03 us
    all_to_all x1, waiting for transfers between devices, sum_at_owner(): blocks = lax.all_to_all(cut_along(x, dim, count), axis, 0, 0, tiled=True)  6.41 us
  transfers between devices with their start and end apart: 5, of which 2 were waited for; matrix products, arithmetic and copies ran while one was open for 18% of the time, Pallas kernels for 0%

commit v1 on v0

v1 whole, which is shorter than its diff:
```python
import jax
import jax.numpy as jnp
from jax import lax
from jax.experimental import pallas as pl
from jax.experimental.pallas import tpu as pltpu
from jax.sharding import PartitionSpec as P

EPSILON = 1e-05
F32 = jnp.float32
BF16 = jnp.bfloat16
CHUNK = 1024
TILE = 256
DEG = 4

VMEM_SPEC = pl.BlockSpec(memory_space=pltpu.VMEM)
ANY_SPEC = pl.BlockSpec(memory_space=pl.ANY)


def dot(a, b):
    return jnp.dot(a, b, preferred_element_type=F32)


def centred_weight(w):
    w = w.astype(F32)
    return (w - jnp.mean(w, axis=-1, keepdims=True)).astype(BF16)


def centred_row(b):
    return b - jnp.mean(b, axis=-1, keepdims=True)


def scaled_rows(z):
    mean_square = jnp.mean(z * z, axis=-1, keepdims=True)
    return z * lax.rsqrt(mean_square + EPSILON)


def store_split(table, row, values):
    n = values.shape[0]
    table[pl.ds(2 * row, n, stride=2), :] = values[:, :128]
    table[pl.ds(2 * row + 1, n, stride=2), :] = values[:, 128:]


def load_split(table, row, n):
    return jnp.concatenate(
        [table[pl.ds(2 * row, n, stride=2), :], table[pl.ds(2 * row + 1, n, stride=2), :]],
        axis=1,
    )


def border_kernel(list_ref, node_ref, w_ref, a_ref, b_ref, table, rows, index, sem):
    rim = a_ref.shape[0]
    odd = lax.rem(lax.axis_index("dom"), 2)
    first = pl.multiple_of((1 - odd) * rim, rim)
    second = pl.multiple_of(odd * rim, rim)
    copies = [
        pltpu.make_async_copy(list_ref.at[pl.ds(first, rim)], index.at[pl.ds(0, rim)], sem.at[0]),
        pltpu.make_async_copy(
            list_ref.at[pl.ds(second, rim)], index.at[pl.ds(rim, rim)], sem.at[1]
        ),
    ]
    for c in copies:
        c.start()
    w = w_ref[0]
    for i in range(node_ref.shape[0] // TILE):
        p = dot(node_ref[i * TILE : (i + 1) * TILE, :], w)
        store_split(table, i * TILE, p.astype(BF16).astype(F32))
    for c in copies:
        c.wait()
    for part, out in enumerate((a_ref, b_ref)):
        for u in range(rim):
            at = part * rim + u
            row = pl.multiple_of(index[at] * 2, 2)
            rows[pl.ds(2 * at, 2), :] = table[pl.ds(row, 2), :]
        for i in range(0, rim, TILE):
            out[i : i + TILE, :] = load_split(rows, part * rim + i, TILE).astype(BF16)


def border_rows(lists, nodes, edge_in, rim):
    shape = jax.ShapeDtypeStruct((rim, 256), BF16)
    return pl.pallas_call(
        border_kernel,
        out_shape=(shape, shape),
        in_specs=[ANY_SPEC, VMEM_SPEC, VMEM_SPEC],
        out_specs=(VMEM_SPEC, VMEM_SPEC),
        scratch_shapes=[
            pltpu.VMEM((2 * nodes.shape[0], 128), F32),
            pltpu.VMEM((4 * rim, 128), F32),
            pltpu.SMEM((2 * rim,), jnp.int32),
            pltpu.SemaphoreType.DMA((2,)),
        ],
        cost_estimate=pl.CostEstimate(flops=300_000_000, bytes_accessed=2_000_000, transcendentals=0),
        name="border_rows",
    )(lists, nodes, edge_in)


def fine_kernel(
    send_ref,
    edge_ref,
    node_ref,
    low_ref,
    high_ref,
    pool_ref,
    edge_in,
    edge_out,
    node_in,
    node_out,
    bias,
    gain,
    out_ref,
    pooled_ref,
    table,
    edges,
    rows0,
    rows1,
    index0,
    index1,
    w_edge,
    w_node,
    edge_sem,
    index_sem,
):
    nodes = node_ref.shape[0]
    chunks = edges.shape[0] // CHUNK
    rim = low_ref.shape[0]
    cnodes = CHUNK // DEG

    def edge_copy(c):
        at = pl.ds(pl.multiple_of(c * CHUNK, CHUNK), CHUNK)
        return pltpu.make_async_copy(edge_ref.at[at, :], edges.at[at, :], edge_sem.at[c])

    def index_copy(c, index, slot):
        at = pl.ds(pl.multiple_of(c * CHUNK, CHUNK), CHUNK)
        return pltpu.make_async_copy(send_ref.at[at], index, index_sem.at[slot])

    index_copy(0, index0, 0).start()
    index_copy(1, index1, 1).start()
    for c in range(chunks):
        edge_copy(c).start()

    w = edge_in[0]
    for i in range(nodes // TILE):
        p = dot(node_ref[i * TILE : (i + 1) * TILE, :], w)
        store_split(table, i * TILE, p.astype(BF16).astype(F32))
    for i in range(0, rim, TILE):
        store_split(table, nodes + i, low_ref[i : i + TILE, :].astype(F32))
        store_split(table, nodes + rim + i, high_ref[i : i + TILE, :].astype(F32))
    w_edge[...] = centred_weight(edge_out[...])
    w_node[...] = centred_weight(node_out[...])
    b_edge = bias[0:1, :]
    b_message = centred_row(bias[1:2, :])
    b_node = bias[2:3, :]
    b_update = centred_row(bias[3:4, :])
    g_message = gain[0:1, :]
    g_update = gain[1:2, :]
    tnodes = TILE // DEG
    spread = (
        lax.broadcasted_iota(jnp.int32, (TILE, tnodes), 0) // DEG
        == lax.broadcasted_iota(jnp.int32, (TILE, tnodes), 1)
    ).astype(F32).astype(BF16)
    collect = (
        lax.broadcasted_iota(jnp.int32, (tnodes, TILE), 1) // DEG
        == lax.broadcasted_iota(jnp.int32, (tnodes, TILE), 0)
    ).astype(F32).astype(BF16)

    def gather(index, rows, start, count):
        for u in range(start, start + count):
            row = pl.multiple_of(index[u], 2)
            rows[2 * u : 2 * u + 2, :] = table[pl.ds(row, 2), :]

    def compute(c, rows, fetch):
        edge_copy(c).wait()
        own = node_ref[pl.ds(pl.multiple_of(c * cnodes, cnodes), cnodes), :]
        receiver = (dot(own, edge_in[1]) + b_edge).astype(BF16)
        sums = []
        tiles = CHUNK // TILE
        for t in range(tiles):
            x = edges[pl.ds(pl.multiple_of(c * CHUNK + t * TILE, TILE), TILE), :]
            pre = dot(x, edge_in[2]) + dot(spread, receiver[t * tnodes : (t + 1) * tnodes, :])
            pre = pre + load_split(rows, t * TILE, TILE)
            hidden = jnp.maximum(pre, 0.0).astype(BF16)
            z = dot(hidden, w_edge[...]) + b_message
            sums.append(dot(collect, scaled_rows(z).astype(BF16)))
            fetch(t * TILE, TILE)
        summed = (jnp.concatenate(sums, axis=0) * g_message).astype(BF16)
        pre = dot(own, node_in[0]) + dot(summed, node_in[1]) + b_node
        hidden = jnp.maximum(pre, 0.0).astype(BF16)
        u = scaled_rows(dot(hidden, w_node[...]) + b_update) * g_update
        out_ref[pl.ds(pl.multiple_of(c * cnodes, cnodes), cnodes), :] = (
            own.astype(F32) + u
        ).astype(BF16)

    index_copy(0, index0, 0).wait()
    gather(index0, rows0, 0, CHUNK)
    index_copy(2, index0, 0).start()

    def pair(k, carry):
        c = 2 * k
        index_copy(c + 1, index1, 1).wait()
        compute(c, rows0, lambda s, n: gather(index1, rows1, s, n))
        index_copy(jnp.minimum(c + 3, chunks - 1), index1, 1).start()
        index_copy(jnp.minimum(c + 2, chunks - 1), index0, 0).wait()
        compute(c + 1, rows1, lambda s, n: gather(index0, rows0, s, n))
        index_copy(jnp.minimum(c + 4, chunks - 1), index0, 0).start()
        return carry

    lax.fori_loop(0, chunks // 2, pair, 0)
    index_copy(0, index0, 0).wait()
    index_copy(1, index1, 1).wait()

    ids = pool_ref[...]
    owners = pooled_ref.shape[0]
    cluster_rows = 256
    for g in range(owners):
        member = (
            lax.broadcasted_iota(jnp.int32, (cluster_rows, nodes), 0) + g * cluster_rows == ids
        ).astype(F32)
        pooled_ref[g, :cluster_rows, :] = dot(member.astype(BF16), out_ref[...]).astype(BF16)
        count = jnp.sum(member, axis=1, keepdims=True)
        high = jnp.floor(count * (1.0 / 256.0))
        low = count - high * 256.0
        both = jnp.where(
            lax.broadcasted_iota(jnp.int32, (cluster_rows, 128), 1) == 0,
            low,
            jnp.where(lax.broadcasted_iota(jnp.int32, (cluster_rows, 128), 1) == 1, high, 0.0),
        )
        flipped = both.T[:16, :]
        pooled_ref[g, cluster_rows:, :] = flipped.astype(BF16)


def fine_level(send, edges, nodes, low, high, pool, edge_in, edge_out, node_in, node_out, bias, gain, owners):
    n = nodes.shape[0]
    rim = low.shape[0]
    return pl.pallas_call(
        fine_kernel,
        out_shape=(
            jax.ShapeDtypeStruct((n, 256), BF16),
            jax.ShapeDtypeStruct((owners, 272, 256), BF16),
        ),
        in_specs=[ANY_SPEC, ANY_SPEC] + [VMEM_SPEC] * 10,
        out_specs=(VMEM_SPEC, VMEM_SPEC),
        scratch_shapes=[
            pltpu.VMEM((2 * (n + 2 * rim), 128), F32),
            pltpu.VMEM(edges.shape, BF16),
            pltpu.VMEM((2 * CHUNK, 128), F32),
            pltpu.VMEM((2 * CHUNK, 128), F32),
            pltpu.SMEM((CHUNK,), jnp.int32),
            pltpu.SMEM((CHUNK,), jnp.int32),
            pltpu.VMEM((256, 256), BF16),
            pltpu.VMEM((256, 256), BF16),
            pltpu.SemaphoreType.DMA((edges.shape[0] // CHUNK,)),
            pltpu.SemaphoreType.DMA((2,)),
        ],
        cost_estimate=pl.CostEstimate(flops=6_000_000_000, bytes_accessed=8_000_000, transcendentals=0),
        name="fine_level",
    )(send, edges, nodes, low, high, pool, edge_in, edge_out, node_in, node_out, bias, gain)


def one_hot_rows(index_col, count):
    return (
        index_col == lax.broadcasted_iota(jnp.int32, (index_col.shape[0], count), 1)
    ).astype(F32).astype(BF16)


def cluster_kernel(parts_ref, lat_ref, list_ref, w_ref, in_ref, proj_ref, border_ref):
    clusters = lat_ref.shape[0]
    total = parts_ref[0, :clusters, :].astype(F32)
    tail = parts_ref[0, clusters:, :].astype(F32)
    for g in range(1, parts_ref.shape[0]):
        total = total + parts_ref[g, :clusters, :].astype(F32)
        tail = tail + parts_ref[g, clusters:, :].astype(F32)
    count = tail[0:1, :] + 256.0 * tail[1:2, :]
    count = jnp.broadcast_to(count, (8, clusters)).T[:, :1]
    mean = total / jnp.maximum(count, 1.0)
    coarse_in = (lat_ref[...].astype(F32) + mean).astype(BF16)
    in_ref[...] = coarse_in
    proj = dot(coarse_in, w_ref[0]).astype(BF16)
    proj_ref[...] = proj
    picked = one_hot_rows(list_ref[...], clusters)
    border_ref[...] = dot(picked, proj).astype(BF16)


def cluster_level(parts, lat, lists, edge_in):
    n = lat.shape[0]
    shape = jax.ShapeDtypeStruct((n, 256), BF16)
    return pl.pallas_call(
        cluster_kernel,
        out_shape=(shape, shape, jax.ShapeDtypeStruct((lists.shape[0], 256), BF16)),
        in_specs=[VMEM_SPEC] * 4,
        out_specs=(VMEM_SPEC,) * 3,
        cost_estimate=pl.CostEstimate(flops=70_000_000, bytes_accessed=1_000_000, transcendentals=0),
        name="cluster_level",
    )(parts, lat, lists, edge_in)


def coarse_kernel(
    send_ref, edge_ref, node_ref, proj_ref, low_ref, high_ref, edge_in, edge_out, node_in, node_out, bias, gain, out_ref
):
    nodes = node_ref.shape[0]
    rim = low_ref.shape[0]
    count = edge_ref.shape[0]
    table = jnp.concatenate([proj_ref[...], low_ref[...], high_ref[...]], axis=0)
    w_edge = centred_weight(edge_out[...])
    w_node = centred_weight(node_out[...])
    b_message = centred_row(bias[1:2, :])
    b_update = centred_row(bias[3:4, :])
    tnodes = TILE // DEG
    spread = (
        lax.broadcasted_iota(jnp.int32, (TILE, tnodes), 0) // DEG
        == lax.broadcasted_iota(jnp.int32, (TILE, tnodes), 1)
    ).astype(F32).astype(BF16)
    collect = (
        lax.broadcasted_iota(jnp.int32, (tnodes, TILE), 1) // DEG
        == lax.broadcasted_iota(jnp.int32, (tnodes, TILE), 0)
    ).astype(F32).astype(BF16)
    own = node_ref[...]
    receiver = (dot(own, edge_in[1]) + bias[0:1, :]).astype(BF16)
    sums = []
    for t in range(count // TILE):
        x = edge_ref[t * TILE : (t + 1) * TILE, :]
        picked = one_hot_rows(send_ref[t * TILE : (t + 1) * TILE, :], nodes + 2 * rim)
        pre = dot(x, edge_in[2]) + dot(spread, receiver[t * tnodes : (t + 1) * tnodes, :])
        pre = pre + dot(picked, table)
        hidden = jnp.maximum(pre, 0.0).astype(BF16)
        z = dot(hidden, w_edge) + b_message
        sums.append(dot(collect, scaled_rows(z).astype(BF16)))
    summed = (jnp.concatenate(sums, axis=0) * gain[0:1, :]).astype(BF16)
    pre = dot(own, node_in[0]) + dot(summed, node_in[1]) + bias[2:3, :]
    hidden = jnp.maximum(pre, 0.0).astype(BF16)
    u = scaled_rows(dot(hidden, w_node) + b_update) * gain[1:2, :]
    out_ref[...] = (own.astype(F32) + u).astype(BF16)


def coarse_level(send, edges, nodes, proj, low, high, edge_in, edge_out, node_in, node_out, bias, gain):
    return pl.pallas_call(
        coarse_kernel,
        out_shape=jax.ShapeDtypeStruct(nodes.shape, BF16),
        in_specs=[VMEM_SPEC] * 12,
        out_specs=VMEM_SPEC,
        cost_estimate=pl.CostEstimate(flops=800_000_000, bytes_accessed=3_000_000, transcendentals=0),
        name="coarse_level",
    )(send, edges, nodes, proj, low, high, edge_in, edge_out, node_in, node_out, bias, gain)


def pair_swaps():
    count = lax.axis_size("dom")
    inner = [(i, i ^ 1) for i in range(count)]
    outer = [(i, ((i + 1) ^ 1) - 1) for i in range(1, count - 1)]
    return inner, outer


def body(
    node_lat,
    edge_lat,
    edge_send,
    halo_list,
    pool_id,
    coarse_lat,
    cedge_lat,
    cedge_send,
    chalo_list,
    fine_edge_in,
    fine_edge_out,
    fine_node_in,
    fine_node_out,
    fine_bias,
    fine_gain,
    coarse_edge_in,
    coarse_edge_out,
    coarse_node_in,
    coarse_node_out,
    coarse_bias,
    coarse_gain,
):
    inner, outer = pair_swaps()
    odd = lax.rem(lax.axis_index("dom"), 2)
    rim = halo_list.shape[0] // 2
    nodes = node_lat.shape[0]

    def table_row(send, count, rim_rows):
        lower = jnp.where(odd == 1, count, count + rim_rows)
        upper = jnp.where(odd == 1, count + rim_rows, count)
        return jnp.where(
            send < rim_rows,
            send + lower,
            jnp.where(
                send < rim_rows + count, send - rim_rows, send - (rim_rows + count) + upper
            ),
        )

    border_a, border_b = border_rows(halo_list, node_lat, fine_edge_in, rim)
    rim_a = lax.ppermute(border_a, "dom", inner)
    rim_b = lax.ppermute(border_b, "dom", outer)
    send = table_row(edge_send, nodes, rim) * 2
    groups = lax.axis_size("group")
    fine_out, pooled = fine_level(
        send,
        edge_lat,
        node_lat,
        rim_a,
        rim_b,
        pool_id.reshape(1, -1),
        fine_edge_in,
        fine_edge_out,
        fine_node_in,
        fine_node_out,
        fine_bias,
        fine_gain,
        groups,
    )
    parts = lax.all_to_all(pooled, "group", 0, 0, tiled=True)
    crim = chalo_list.shape[0] // 2
    clusters = coarse_lat.shape[0]
    lists = jnp.where(odd == 1, chalo_list, jnp.roll(chalo_list, crim))
    coarse_in, coarse_proj, border = cluster_level(
        parts, coarse_lat, lists.reshape(-1, 1), coarse_edge_in
    )
    crim_a = lax.ppermute(border[:crim], "dom", inner)
    crim_b = lax.ppermute(border[crim:], "dom", outer)
    coarse_out = coarse_level(
        table_row(cedge_send, clusters, crim).reshape(-1, 1),
        cedge_lat,
        coarse_in,
        coarse_proj,
        crim_a,
        crim_b,
        coarse_edge_in,
        coarse_edge_out,
        coarse_node_in,
        coarse_node_out,
        coarse_bias,
        coarse_gain,
    )
    return (fine_out, coarse_out)


def solution(mesh):
    rows = P(("group", "dom"), None)
    flat = P(("group", "dom"))
    placed = (rows, rows, flat, flat, flat, rows, rows, flat, flat) + (P(),) * 12
    return jax.shard_map(
        body,
        mesh=mesh,
        in_specs=placed,
        out_specs=(rows, rows),
        check_vma=False,
    )
```

time: 169 us -> 79.9 us (0.47)
  local copies, waits for them, and re-layouts: 78.9 us -> 4.84 us
  Pallas kernels: 0 us -> 42.7 us
  other arithmetic: 30.1 us -> 1.41 us
  matrix products: 27.3 us -> 0 us
  starting transfers between devices: 18.8 us -> 15.2 us
  waiting for transfers between devices: 11.4 us -> 14.2 us
    gather x4 -> x0, local copies, waits for them, and re-layouts: 45.7 us -> none  [the longest x2 39.7 us: edge_node(): edge_pre = edge_pre + sender_proj[senders].astype(jnp.float32) + biases[0]]
    pallas_call x0 -> x4, Pallas kernels: none -> 42.7 us  [the longest x1 31.1 us: fine_level(): pl.pallas_call(fine_kernel, out_shape=(jax.ShapeDtypeStruct((n, 256), BF1...]
    dot_general x11 -> x0, matrix products: 27.3 us -> none  [the longest x2 13.2 us: edge_node(): jnp.dot(edge_hidden, edge_out, preferred_element_type=jnp.float32)]
    reduce_sum x8 -> x0, other arithmetic: 20.1 us -> none  [the longest x2 13 us: edge_node(): jnp.sum(message.astype(jnp.float32).reshape(node_count, fanin, width), ax...]
    add x4 -> x0, local copies, waits for them, and re-layouts: 16.3 us -> none  [edge_node(): edge_pre.reshape(node_count, fanin, width) + receiver_proj[:, None, :]]
    convert_element_type x5 -> x0, other arithmetic: 7.59 us -> none  [the longest x2 5.72 us: edge_node(): message = message.astype(jnp.bfloat16)]
    reshape x2, local copies, waits for them, and re-layouts: 7.03 us -> 1.82 us  [the longest x1 1.02 us: body(): table_row(cedge_send, clusters, crim).reshape(-1, 1)]
    unnamed x63 -> x14, local copies, waits for them, and re-layouts: 7.08 us -> 2.13 us
  transfers between devices with their start and end apart: 5 -> 5, of which waited for: 2 -> 3; matrix products, arithmetic and copies ran while one was open for 18% -> 4% of each run, Pallas kernels for 0% -> 0%
where the time goes in v1:
time: 79.9 us; the launch traced here: 79 us
  Pallas kernels  42.7 us (53%)
  starting transfers between devices  15.2 us (19%)
  waiting for transfers between devices  14.2 us (18%)
  local copies, waits for them, and re-layouts  4.84 us (6%)
  other arithmetic  1.41 us (2%)
    pallas_call x1, Pallas kernels, fine_level(): pl.pallas_call(fine_kernel, out_shape=(jax.ShapeDtypeStruct((n, 256), BF1...  31.1 us
    all_to_all x1, waiting for transfers between devices, body(): parts = lax.all_to_all(pooled, 'group', 0, 0, tiled=True)  6.71 us
    ppermute x1, starting transfers between devices, body(): crim_b = lax.ppermute(border[crim:], 'dom', outer)  5.59 us
    pallas_call x1, Pallas kernels, coarse_level(): pl.pallas_call(coarse_kernel, out_shape=jax.ShapeDtypeStruct(nodes.shape,...  5.37 us
    ppermute x1, waiting for transfers between devices, body(): rim_b = lax.ppermute(border_b, 'dom', outer)  5.22 us
    ppermute x1, starting transfers between devices, body(): rim_b = lax.ppermute(border_b, 'dom', outer)  4.57 us
    all_to_all x1, starting transfers between devices, body(): parts = lax.all_to_all(pooled, 'group', 0, 0, tiled=True)  4.2 us
    pallas_call x1, Pallas kernels, border_rows(): pl.pallas_call(border_kernel, out_shape=(shape, shape), in_specs=[ANY_SPE...  3.68 us
  transfers between devices with their start and end apart: 5, of which 3 were waited for; matrix products, arithmetic and copies ran while one was open for 4% of the time, Pallas kernels for 0%

profile of v1, /device:TPU:103, one launch (start us, length us, event | category | flops | bytes accessed | tf_op | source)
XLA Modules:
  0.0 79.0 jit_solution(4084762623584423914)
XLA Ops:
  0.6 3.7 %border_rows.1 = (bf16[512,256]{1,0:T(8,128)(2,1)}, bf16[512,256]{1,0:T(8,128)(2,1)}) custom-call(s32[1024]{0:T(1024)} %list_ref.1, bf16[2048,256]{1,0:T(8,128)(2,1)} %node_ref.3, bf16[3,256,256]{2,1,0:T(8,128)(2,1)} %edge_in.2), custom_call_target="tpu_custom_call" | custom-call | flops 300000000 | bytes 2000000 | tf_op jit(solution)/shard_map/border_rows/pallas_call | solution.py:80
  4.3 0.8 collective-permute-start
  5.1 4.6 %collective-permute-start.1 = (bf16[512,256]{1,0:T(8,128)(2,1)}, bf16[512,256]{1,0:T(8,128)(2,1)S(1)}, u32[]{:S(2)}, u32[]{:S(2)}) collective-permute-start(bf16[512,256]{1,0:T(8,128)(2,1)} %get-tuple-element.10), channel_id=1, source_target_pairs={{1,2},{2,1},{3,4},{4,3},{5,6},{6,5},{7,8},{8,7},{9,10},{10,9},{11,... | collective-permute-start | bytes 786440 | tf_op jit(solution)/shard_map/ppermute | solution.py:392
  9.7 1.4 %select_multiply_fusion.send_ref = s32[8192]{0:T(1024)} fusion(s32[8192]{0:T(1024)} %param.23, s32[]{:T(128)S(6)} %select_n.36, s32[]{:T(128)S(6)} %select_n.35), kind=kLoop, calls=%fused_computation | loop fusion | flops 73728 | bytes 65544 | tf_op jit(solution)/shard_map/mul | solution.py:393
  11.1 0.0 collective-permute-done.low_ref
  11.1 0.0 copy-start.3
  11.1 5.2 %collective-permute-done.1.high_ref = bf16[512,256]{1,0:T(8,128)(2,1)S(1)} collective-permute-done((bf16[512,256]{1,0:T(8,128)(2,1)}, bf16[512,256]{1,0:T(8,128)(2,1)S(1)}, u32[]{:S(2)}, u32[]{:S(2)}) %collective-permute-start.1) | collective-permute-done | bytes 262176 | tf_op jit(solution)/shard_map/ppermute | solution.py:392
  16.3 0.0 copy-start.4
  16.3 0.0 copy-done.3
  16.3 0.7 copy-done.4
  17.0 0.0 copy-start.1
  17.0 0.0 copy-start.2
  17.0 31.1 %fine_level.1 = (bf16[2048,256]{1,0:T(8,128)(2,1)}, bf16[4,272,256]{2,1,0:T(8,128)(2,1)}) custom-call(s32[8192]{0:T(1024)} %select_multiply_fusion.send_ref, bf16[8192,256]{1,0:T(8,128)(2,1)} %edge_ref.2, bf16[2048,256]{1,0:T(8,128)(2,1)} %node_ref.3, bf16[512,256]{1,0:T(8,128)(2,1)} %copy-done.3, bf16[512,256]{1,0:T(8,128)(2,1)} %copy-done.4, ...), custom_call_target="tpu_custom_call" | custom-call | flops 6000000000 | bytes 8000000 | tf_op jit(solution)/shard_map/fine_level/pallas_call | solution.py:233
  48.1 4.2 %all-to-all-start = ((bf16[4,272,256]{2,1,0:T(8,128)(2,1)}), bf16[4,272,256]{2,1,0:T(8,128)(2,1)S(1)}, u32[]{:S(2)}, u32[]{:S(2)}) async-start(bf16[4,272,256]{2,1,0:T(8,128)(2,1)} %get-tuple-element.12), calls=%async_computation | async-start | bytes 1114112 | tf_op jit(solution)/shard_map/all_to_all | solution.py:410
  52.3 0.0 copy-done.1
  52.3 0.8 %copy.23.list_ref = s32[256,1]{1,0:T(8,128)} copy(s32[256,1]{0,1:T(1,128)S(1)} %bitcast.4) | data formatting | bytes 2048 | tf_op jit(solution)/shard_map/reshape | solution.py:415
  53.1 6.7 %all-to-all-done.parts_ref = bf16[4,272,256]{2,1,0:T(8,128)(2,1)S(1)} async-done(((bf16[4,272,256]{2,1,0:T(8,128)(2,1)}), bf16[4,272,256]{2,1,0:T(8,128)(2,1)S(1)}, u32[]{:S(2)}, u32[]{:S(2)}) %all-to-all-start) | async-done | bytes 557088 | tf_op jit(solution)/shard_map/all_to_all | solution.py:410
  59.8 0.0 copy-start
  59.8 0.8 %copy-done = bf16[4,272,256]{2,1,0:T(8,128)(2,1)} copy-done((bf16[4,272,256]{2,1,0:T(8,128)(2,1)}, bf16[4,272,256]{2,1,0:T(8,128)(2,1)S(1)}, u32[]{:S(2)}) %copy-start) | copy-done | bytes 557080
  60.6 2.5 %cluster_level.1 = (bf16[256,256]{1,0:T(8,128)(2,1)}, bf16[256,256]{1,0:T(8,128)(2,1)}, bf16[256,256]{1,0:T(8,128)(2,1)}) custom-call(bf16[4,272,256]{2,1,0:T(8,128)(2,1)} %copy-done, bf16[256,256]{1,0:T(8,128)(2,1)} %lat_ref.1, s32[256,1]{1,0:T(8,128)} %copy.23.list_ref, bf16[3,256,256]{2,1,0:T(8,128)(2,1)} %edge_in.3), custom_call_target="tpu_custom_call" | custom-call | flops 70000000 | bytes 1000000 | tf_op jit(solution)/shard_map/cluster_level/pallas_call | solution.py:285
  63.2 0.9 %fusion = (bf16[128,256]{1,0:T(8,128)(2,1)S(1)}, bf16[128,256]{1,0:T(8,128)(2,1)S(1)}) fusion(bf16[256,256]{1,0:T(8,128)(2,1)} %get-tuple-element.15), kind=kLoop, calls=%fused_computation.3 | loop fusion | bytes 262144 | tf_op jit(solution)/shard_map/slice | solution.py:418
  64.0 0.1 collective-permute-start.2
  64.1 5.6 %collective-permute-start.3 = (bf16[128,256]{1,0:T(8,128)(2,1)S(1)}, bf16[128,256]{1,0:T(8,128)(2,1)S(1)}, u32[]{:S(2)}, u32[]{:S(2)}) collective-permute-start(bf16[128,256]{1,0:T(8,128)(2,1)S(1)} %get-tuple-element.16), channel_id=1, source_target_pairs={{1,2},{2,1},{3,4},{4,3},{5,6},{6,5},{7,8},{8,7},{9,10},{10,9},{11,... | collective-permute-start | bytes 196616 | tf_op jit(solution)/shard_map/ppermute | solution.py:418
  69.7 0.0 copy-done.2
  69.8 1.0 %copy.24.send_ref = s32[1024,1]{1,0:T(8,128)} copy(s32[1024,1]{0,1:T(1,128)S(1)} %bitcast.3) | data formatting | bytes 8192 | tf_op jit(solution)/shard_map/reshape | solution.py:420
  70.8 0.0 collective-permute-done.2.low_ref
  70.8 0.0 copy-start.5
  70.8 2.3 %collective-permute-done.3.high_ref = bf16[128,256]{1,0:T(8,128)(2,1)S(1)} collective-permute-done((bf16[128,256]{1,0:T(8,128)(2,1)S(1)}, bf16[128,256]{1,0:T(8,128)(2,1)S(1)}, u32[]{:S(2)}, u32[]{:S(2)}) %collective-permute-start.3) | collective-permute-done | bytes 65568 | tf_op jit(solution)/shard_map/ppermute | solution.py:418
  73.0 0.0 copy-start.6
  73.1 0.0 copy-done.5
  73.1 0.6 copy-done.6
  73.7 5.4 %coarse_level.1 = bf16[256,256]{1,0:T(8,128)(2,1)} custom-call(s32[1024,1]{1,0:T(8,128)} %copy.24.send_ref, bf16[1024,256]{1,0:T(8,128)(2,1)} %edge_ref.3, bf16[256,256]{1,0:T(8,128)(2,1)} %get-tuple-element.13.node_ref, bf16[256,256]{1,0:T(8,128)(2,1)} %get-tuple-element.14.proj_ref, bf16[128,256]{1,0:T(8,128)(2,1)} %copy-done.5, ...), custom_call_target="tpu_custom_call" | custom-call | flops 800000000 | bytes 3000000 | tf_op jit(solution)/shard_map/coarse_level/pallas_call | solution.py:334
  (3 shorter events, 0.0 us)
Async XLA Ops:
  4.3 6.7 %collective-permute-start = (bf16[512,256]{1,0:T(8,128)(2,1)}, bf16[512,256]{1,0:T(8,128)(2,1)S(1)}, u32[]{:S(2)}, u32[]{:S(2)}) collective-permute-start(bf16[512,256]{1,0:T(8,128)(2,1)} %get-tuple-element.9), channel_id=1, source_target_pairs={{0,1},{1,0},{2,3},{3,2},{4,5},{5,4},{6,7},{7,6},{8,9},{9,8},{10,11... | collective-permute-start | bytes 786440 | tf_op jit(solution)/shard_map/ppermute | solution.py:391
  5.1 11.2 %collective-permute-start.1 = (bf16[512,256]{1,0:T(8,128)(2,1)}, bf16[512,256]{1,0:T(8,128)(2,1)S(1)}, u32[]{:S(2)}, u32[]{:S(2)}) collective-permute-start(bf16[512,256]{1,0:T(8,128)(2,1)} %get-tuple-element.10), channel_id=1, source_target_pairs={{1,2},{2,1},{3,4},{4,3},{5,6},{6,5},{7,8},{8,7},{9,10},{10,9},{11,... | collective-permute-start | bytes 786440 | tf_op jit(solution)/shard_map/ppermute | solution.py:392
  11.1 5.2 %copy-start.3 = (bf16[512,256]{1,0:T(8,128)(2,1)}, bf16[512,256]{1,0:T(8,128)(2,1)S(1)}, u32[]{:S(2)}) copy-start(bf16[512,256]{1,0:T(8,128)(2,1)S(1)} %collective-permute-done.low_ref) | copy-start | bytes 786436
  16.3 0.7 copy-start.4
  17.0 35.3 %copy-start.1 = (s32[256]{0:T(256)S(1)}, s32[256]{0:T(256)}, u32[]{:S(2)}) copy-start(s32[256]{0:T(256)} %param.29) | copy-start | bytes 3076
  17.0 52.8 %copy-start.2 = (s32[1024]{0:T(1024)S(1)}, s32[1024]{0:T(1024)}, u32[]{:S(2)}) copy-start(s32[1024]{0:T(1024)} %param.28) | copy-start | bytes 12292
  48.1 11.7 %all-to-all-start = ((bf16[4,272,256]{2,1,0:T(8,128)(2,1)}), bf16[4,272,256]{2,1,0:T(8,128)(2,1)S(1)}, u32[]{:S(2)}, u32[]{:S(2)}) async-start(bf16[4,272,256]{2,1,0:T(8,128)(2,1)} %get-tuple-element.12), calls=%async_computation | async-start | bytes 1114112 | tf_op jit(solution)/shard_map/all_to_all | solution.py:410
  59.8 0.8 %copy-start = (bf16[4,272,256]{2,1,0:T(8,128)(2,1)}, bf16[4,272,256]{2,1,0:T(8,128)(2,1)S(1)}, u32[]{:S(2)}) copy-start(bf16[4,272,256]{2,1,0:T(8,128)(2,1)S(1)} %all-to-all-done.parts_ref) | copy-start | bytes 1671172
  64.0 6.8 %collective-permute-start.2 = (bf16[128,256]{1,0:T(8,128)(2,1)S(1)}, bf16[128,256]{1,0:T(8,128)(2,1)S(1)}, u32[]{:S(2)}, u32[]{:S(2)}) collective-permute-start(bf16[128,256]{1,0:T(8,128)(2,1)S(1)} %get-tuple-element.17), channel_id=1, source_target_pairs={{0,1},{1,0},{2,3},{3,2},{4,5},{5,4},{6,7},{7,6},{8,9},{9,8},{10,11... | collective-permute-start | bytes 196616 | tf_op jit(solution)/shard_map/ppermute | solution.py:417
  64.1 8.9 %collective-permute-start.3 = (bf16[128,256]{1,0:T(8,128)(2,1)S(1)}, bf16[128,256]{1,0:T(8,128)(2,1)S(1)}, u32[]{:S(2)}, u32[]{:S(2)}) collective-permute-start(bf16[128,256]{1,0:T(8,128)(2,1)S(1)} %get-tuple-element.16), channel_id=1, source_target_pairs={{1,2},{2,1},{3,4},{4,3},{5,6},{6,5},{7,8},{8,7},{9,10},{10,9},{11,... | collective-permute-start | bytes 196616 | tf_op jit(solution)/shard_map/ppermute | solution.py:418
  70.8 2.3 %copy-start.5 = (bf16[128,256]{1,0:T(8,128)(2,1)}, bf16[128,256]{1,0:T(8,128)(2,1)S(1)}, u32[]{:S(2)}) copy-start(bf16[128,256]{1,0:T(8,128)(2,1)S(1)} %collective-permute-done.2.low_ref) | copy-start | bytes 196612
  73.0 0.6 copy-start.6

commit v2 on v1

v2 whole, which is shorter than its diff:
```python
import jax
import jax.numpy as jnp
from jax import lax
from jax.experimental import pallas as pl
from jax.experimental.pallas import tpu as pltpu
from jax.sharding import PartitionSpec as P

EPSILON = 1e-05
F32 = jnp.float32
BF16 = jnp.bfloat16
CHUNK = 1024
GATHER = 1024
TILE = 256
DEG = 4

VMEM_SPEC = pl.BlockSpec(memory_space=pltpu.VMEM)
HBM_SPEC = pl.BlockSpec(memory_space=pltpu.HBM)


def hbm(x):
    return pltpu.with_memory_space_constraint(x, pltpu.HBM)


def limit(mib):
    return pltpu.CompilerParams(vmem_limit_bytes=mib * 1024 * 1024)


def dot(a, b):
    return jnp.dot(a, b, preferred_element_type=F32)


def centred_weight(w):
    w = w.astype(F32)
    return (w - jnp.mean(w, axis=-1, keepdims=True)).astype(BF16)


def centred_row(b):
    return b - jnp.mean(b, axis=-1, keepdims=True)


def scaled_rows(z):
    mean_square = jnp.mean(z * z, axis=-1, keepdims=True)
    return z * lax.rsqrt(mean_square + EPSILON)


def store_split(table, row, values):
    n = values.shape[0]
    table[pl.ds(2 * row, n, stride=2), :] = values[:, :128]
    table[pl.ds(2 * row + 1, n, stride=2), :] = values[:, 128:]


def load_split(table, row, n):
    return jnp.concatenate(
        [table[pl.ds(2 * row, n, stride=2), :], table[pl.ds(2 * row + 1, n, stride=2), :]],
        axis=1,
    )


def border_kernel(
    list_ref, node_ref, w_ref, a_ref, b_ref, nodes, w, table, rows, index0, index1, list_sem, w_sem, node_sem
):
    rim = a_ref.shape[0]
    odd = lax.rem(lax.axis_index("dom"), 2)
    w_copy = pltpu.make_async_copy(w_ref.at[0], w, w_sem)
    w_copy.start()
    copies = [
        pltpu.make_async_copy(node_ref.at[i : i + TILE, :], nodes.at[i : i + TILE, :], node_sem.at[i // TILE])
        for i in range(0, nodes.shape[0], TILE)
    ]
    for c in copies:
        c.start()
    lists = []
    for part, (index, first) in enumerate(((index0, (1 - odd) * rim), (index1, odd * rim))):
        first = pl.multiple_of(first, rim)
        lists.append(
            pltpu.make_async_copy(list_ref.at[pl.ds(first, rim)], index, list_sem.at[part])
        )
        lists[-1].start()
    w_copy.wait()
    for i, c in enumerate(copies):
        c.wait()
        p = dot(nodes[i * TILE : (i + 1) * TILE, :], w[...])
        store_split(table, i * TILE, p.astype(BF16).astype(F32))
    for part, (index, out) in enumerate(((index1, b_ref), (index0, a_ref))):
        lists[1 - part].wait()
        for u in range(rim):
            row = pl.multiple_of(index[u] * 2, 2)
            rows[2 * u : 2 * u + 2, :] = table[pl.ds(row, 2), :]
        out[...] = load_split(rows, 0, rim).astype(BF16)


def border_rows(lists, nodes, edge_in, rim):
    shape = jax.ShapeDtypeStruct((rim, 256), BF16)
    return pl.pallas_call(
        border_kernel,
        out_shape=(shape, shape),
        in_specs=[HBM_SPEC] * 3,
        out_specs=(VMEM_SPEC, VMEM_SPEC),
        scratch_shapes=[
            pltpu.VMEM(nodes.shape, BF16),
            pltpu.VMEM((256, 256), BF16),
            pltpu.VMEM((2 * nodes.shape[0], 128), F32),
            pltpu.VMEM((2 * rim, 128), F32),
            pltpu.SMEM((rim,), jnp.int32),
            pltpu.SMEM((rim,), jnp.int32),
            pltpu.SemaphoreType.DMA((2,)),
            pltpu.SemaphoreType.DMA,
            pltpu.SemaphoreType.DMA((nodes.shape[0] // TILE,)),
        ],
        cost_estimate=pl.CostEstimate(flops=300_000_000, bytes_accessed=2_000_000, transcendentals=0),
        name="border_rows",
        compiler_params=limit(10),
    )(hbm(lists), hbm(nodes), hbm(edge_in))


def edges_kernel(
    send_hbm,
    pool_hbm,
    node_hbm,
    edge_in_hbm,
    edge_out_hbm,
    node_in_hbm,
    node_out_hbm,
    bias_hbm,
    edge_hbm,
    pre_ref,
    own_ref,
    table_ref,
    row_ref,
    w_ref,
    member_ref,
    count_ref,
    send,
    pool,
    node,
    edge_in,
    edge_out,
    node_in,
    node_out,
    bias,
    edges,
    rep0,
    rep1,
    small_sem,
    edge_sem,
):
    nodes = node.shape[0]
    chunks = edges.shape[0] // CHUNK
    cnodes = CHUNK // DEG
    rim = (table_ref.shape[0] // 2 - nodes) // 2
    small = [
        pltpu.make_async_copy(source, target, small_sem.at[i])
        for i, (source, target) in enumerate(
            (
                (send_hbm, send),
                (pool_hbm, pool),
                (node_hbm, node),
                (edge_in_hbm, edge_in),
                (edge_out_hbm, edge_out),
                (node_in_hbm, node_in),
                (node_out_hbm, node_out),
                (bias_hbm, bias),
            )
        )
    ]
    copies = [
        pltpu.make_async_copy(
            edge_hbm.at[c * CHUNK : (c + 1) * CHUNK, :],
            edges.at[c * CHUNK : (c + 1) * CHUNK, :],
            edge_sem.at[c],
        )
        for c in range(chunks)
    ]
    for c in small + copies:
        c.start()
    for c in small:
        c.wait()
    odd = lax.rem(lax.axis_index("dom"), 2)
    sent = send[...]
    lower = jnp.where(odd == 1, nodes, nodes + rim)
    upper = jnp.where(odd == 1, nodes + rim, nodes) - (rim + nodes)
    row_ref[...] = 2 * (
        sent + jnp.where(sent < rim, lower, jnp.where(sent < rim + nodes, -rim, upper))
    )
    w_ref[0] = centred_weight(edge_out[...])
    w_ref[1] = centred_weight(node_out[...])
    b_edge = bias[0:1, :]
    b_node = bias[2:3, :]

    def own_terms(k, carry):
        i = pl.multiple_of(k * CHUNK, CHUNK)
        own = node[pl.ds(i, CHUNK), :]
        store_split(table_ref, i, dot(own, edge_in[0]).astype(BF16).astype(F32))
        own_ref[pl.ds(i, CHUNK), :] = dot(own, node_in[0]) + b_node
        return carry

    lax.fori_loop(0, nodes // CHUNK, own_terms, 0, unroll=True)

    def edge_chunk(c, carry):
        own = node[pl.ds(pl.multiple_of(c * cnodes, cnodes), cnodes), :]
        receiver = dot(own, edge_in[1]) + b_edge
        for j in range(DEG):
            rep0[pl.ds(j, cnodes, stride=DEG), :] = receiver[:, :128]
            rep1[pl.ds(j, cnodes, stride=DEG), :] = receiver[:, 128:]
        at = pl.ds(pl.multiple_of(c * CHUNK, CHUNK), CHUNK)
        pltpu.make_async_copy(edge_hbm.at[at, :], edges.at[at, :], edge_sem.at[c]).wait()
        pre_ref[at, :] = dot(edges[at, :], edge_in[2]) + jnp.concatenate(
            [rep0[...], rep1[...]], axis=1
        )
        return carry

    lax.fori_loop(0, chunks, edge_chunk, 0, unroll=2)

    ids = pool[...]
    lane = lax.broadcasted_iota(jnp.int32, (256, 128), 1)

    def membership(g, carry):
        member = (
            lax.broadcasted_iota(jnp.int32, (256, nodes), 0) + g * 256 == ids
        ).astype(F32)
        member_ref[g] = member.astype(BF16)
        count = jnp.sum(member, axis=1, keepdims=True)
        high = jnp.floor(count * (1.0 / 256.0))
        low = count - high * 256.0
        both = jnp.where(lane == 0, low, jnp.where(lane == 1, high, 0.0))
        count_ref[g] = both.T[:16, :].astype(BF16)
        return carry

    lax.fori_loop(0, member_ref.shape[0], membership, 0)


def edge_terms(send, pool, edges, nodes, rim, owners, edge_in, edge_out, node_in, node_out, bias):
    n = nodes.shape[0]
    e = edges.shape[0]
    shape = jax.ShapeDtypeStruct
    operands = (send, pool, nodes, edge_in, edge_out, node_in, node_out, bias, edges)
    return pl.pallas_call(
        edges_kernel,
        out_shape=(
            shape((e, 256), F32),
            shape((n, 256), F32),
            shape((2 * (n + 2 * rim), 128), F32),
            shape(send.shape, jnp.int32),
            shape((2, 256, 256), BF16),
            shape((owners, 256, n), BF16),
            shape((owners, 16, 256), BF16),
        ),
        in_specs=[HBM_SPEC] * len(operands),
        out_specs=(VMEM_SPEC,) * 7,
        scratch_shapes=[pltpu.VMEM(x.shape, x.dtype) for x in operands]
        + [
            pltpu.VMEM((CHUNK, 128), F32),
            pltpu.VMEM((CHUNK, 128), F32),
            pltpu.SemaphoreType.DMA((8,)),
            pltpu.SemaphoreType.DMA((e // CHUNK,)),
        ],
        cost_estimate=pl.CostEstimate(flops=3_000_000_000, bytes_accessed=8_000_000, transcendentals=0),
        name="edge_terms",
        compiler_params=limit(14),
    )(*(hbm(x) for x in operands))


def fine_kernel(
    row_ref,
    pre_ref,
    own_ref,
    table_ref,
    w_ref,
    member_ref,
    count_ref,
    low_ref,
    high_ref,
    node_hbm,
    node_in,
    bias,
    gain,
    out_hbm,
    pooled_ref,
    table,
    rows,
    node,
    out,
    summed,
    index,
    index_sem,
    node_sem,
    out_sem,
):
    nodes = node.shape[0]
    chunks = pre_ref.shape[0] // GATHER
    rim = low_ref.shape[0]
    cnodes = GATHER // DEG
    lines = GATHER // 128

    def index_copy(c):
        at = pl.ds(pl.multiple_of(c * lines, lines), lines)
        return pltpu.make_async_copy(row_ref.at[at, :], index, index_sem)

    index_copy(0).start()
    node_copy = pltpu.make_async_copy(node_hbm, node, node_sem)
    node_copy.start()
    store_split(table, nodes, low_ref[...].astype(F32))
    store_split(table, nodes + rim, high_ref[...].astype(F32))
    b_message = centred_row(bias[1:2, :])
    b_update = centred_row(bias[3:4, :])
    g_message = gain[0:1, :]
    g_update = gain[1:2, :]
    tnodes = TILE // DEG
    collect = (
        lax.broadcasted_iota(jnp.int32, (tnodes, TILE), 1) // DEG
        == lax.broadcasted_iota(jnp.int32, (tnodes, TILE), 0)
    ).astype(F32).astype(BF16)

    def chunk(c, carry):
        index_copy(c).wait()
        for u in range(GATHER):
            row = pl.multiple_of(index[u // 128, u % 128], 2)
            rows[2 * u : 2 * u + 2, :] = table[pl.ds(row, 2), :]
        index_copy(jnp.minimum(c + 1, chunks - 1)).start()
        pre = pre_ref[pl.ds(pl.multiple_of(c * GATHER, GATHER), GATHER), :]
        hidden = jnp.maximum(pre + load_split(rows, 0, GATHER), 0.0).astype(BF16)
        m = scaled_rows(dot(hidden, w_ref[0]) + b_message).astype(BF16)
        sums = [dot(collect, m[q : q + TILE, :]) for q in range(0, GATHER, TILE)]
        summed[pl.ds(pl.multiple_of(c * cnodes, cnodes), cnodes), :] = (
            jnp.concatenate(sums, axis=0) * g_message
        ).astype(BF16)
        return carry

    lax.fori_loop(0, chunks, chunk, 0)
    index_copy(0).wait()
    node_copy.wait()
    hidden = jnp.maximum(own_ref[...] + dot(summed[...], node_in[1]), 0.0).astype(BF16)
    u = scaled_rows(dot(hidden, w_ref[1]) + b_update) * g_update
    out[...] = (node[...].astype(F32) + u).astype(BF16)
    out_copy = pltpu.make_async_copy(out, out_hbm, out_sem)
    out_copy.start()
    for g in range(pooled_ref.shape[0]):
        pooled_ref[g, :256, :] = dot(member_ref[g], out[...]).astype(BF16)
        pooled_ref[g, 256:, :] = count_ref[g]
    out_copy.wait()


def fine_level(terms, nodes, low, high, node_in, bias, gain):
    n = nodes.shape[0]
    pre, own, table, row, w, member, count = terms
    owners = member.shape[0]
    outs = pl.pallas_call(
        fine_kernel,
        out_shape=(
            jax.ShapeDtypeStruct((n, 256), BF16),
            jax.ShapeDtypeStruct((owners, 272, 256), BF16),
            jax.ShapeDtypeStruct(table.shape, F32),
        ),
        in_specs=[VMEM_SPEC] * 9 + [HBM_SPEC] + [VMEM_SPEC] * 3,
        out_specs=(HBM_SPEC, VMEM_SPEC, VMEM_SPEC),
        scratch_shapes=[
            pltpu.VMEM((2 * GATHER, 128), F32),
            pltpu.VMEM((n, 256), BF16),
            pltpu.VMEM((n, 256), BF16),
            pltpu.VMEM((n, 256), BF16),
            pltpu.SMEM((GATHER // 128, 128), jnp.int32),
            pltpu.SemaphoreType.DMA,
            pltpu.SemaphoreType.DMA,
            pltpu.SemaphoreType.DMA,
        ],
        input_output_aliases={3: 2},
        cost_estimate=pl.CostEstimate(flops=4_000_000_000, bytes_accessed=8_000_000, transcendentals=0),
        name="fine_level",
        compiler_params=limit(16),
    )(row, pre, own, table, w, member, count, low, high, hbm(nodes), node_in, bias, gain)
    return outs[0], outs[1]


def one_hot_rows(index_col, count):
    return (
        index_col == lax.broadcasted_iota(jnp.int32, (index_col.shape[0], count), 1)
    ).astype(F32).astype(BF16)


def cluster_kernel(parts_ref, lat_ref, list_ref, w_ref, in_ref, proj_ref, a_ref, b_ref):
    clusters = lat_ref.shape[0]
    rim = a_ref.shape[0]
    total = parts_ref[0, :clusters, :].astype(F32)
    tail = parts_ref[0, clusters:, :].astype(F32)
    for g in range(1, parts_ref.shape[0]):
        total = total + parts_ref[g, :clusters, :].astype(F32)
        tail = tail + parts_ref[g, clusters:, :].astype(F32)
    count = tail[0:1, :] + 256.0 * tail[1:2, :]
    count = jnp.broadcast_to(count, (8, clusters)).T[:, :1]
    mean = total / jnp.maximum(count, 1.0)
    coarse_in = (lat_ref[...].astype(F32) + mean).astype(BF16)
    in_ref[...] = coarse_in
    proj = dot(coarse_in, w_ref[0]).astype(BF16)
    proj_ref[...] = proj
    border = dot(one_hot_rows(list_ref[...], clusters), proj).astype(BF16)
    a_ref[...] = border[:rim, :]
    b_ref[...] = border[rim:, :]


def cluster_level(parts, lat, lists, edge_in):
    n = lat.shape[0]
    shape = jax.ShapeDtypeStruct((n, 256), BF16)
    rim = jax.ShapeDtypeStruct((lists.shape[0] // 2, 256), BF16)
    return pl.pallas_call(
        cluster_kernel,
        out_shape=(shape, shape, rim, rim),
        in_specs=[VMEM_SPEC] * 4,
        out_specs=(VMEM_SPEC,) * 4,
        cost_estimate=pl.CostEstimate(flops=70_000_000, bytes_accessed=1_000_000, transcendentals=0),
        name="cluster_level",
        compiler_params=limit(16),
    )(parts, lat, lists, edge_in)


def coarse_edges_kernel(send_ref, edge_ref, node_ref, proj_ref, edge_in, edge_out, node_in, node_out, bias, pre_ref, own_ref, w_ref):
    nodes = node_ref.shape[0]
    count = edge_ref.shape[0]
    own = node_ref[...]
    receiver = (dot(own, edge_in[1]) + bias[0:1, :]).astype(BF16)
    spread = (
        lax.broadcasted_iota(jnp.int32, (count, nodes), 0) // DEG
        == lax.broadcasted_iota(jnp.int32, (count, nodes), 1)
    ).astype(F32).astype(BF16)
    picked = one_hot_rows(send_ref[...], nodes)
    pre_ref[...] = dot(edge_ref[...], edge_in[2]) + (dot(spread, receiver) + dot(picked, proj_ref[...]))
    own_ref[...] = dot(own, node_in[0]) + bias[2:3, :]
    w_ref[0] = centred_weight(edge_out[...])
    w_ref[1] = centred_weight(node_out[...])


def coarse_edge_terms(send, edges, nodes, proj, edge_in, edge_out, node_in, node_out, bias):
    shape = jax.ShapeDtypeStruct
    return pl.pallas_call(
        coarse_edges_kernel,
        out_shape=(shape(edges.shape, F32), shape(nodes.shape, F32), shape((2, 256, 256), BF16)),
        in_specs=[VMEM_SPEC] * 9,
        out_specs=(VMEM_SPEC,) * 3,
        cost_estimate=pl.CostEstimate(flops=500_000_000, bytes_accessed=3_000_000, transcendentals=0),
        name="coarse_edge_terms",
        compiler_params=limit(16),
    )(send, edges, nodes, proj, edge_in, edge_out, node_in, node_out, bias)


def coarse_kernel(send_ref, pre_ref, own_ref, w_ref, node_ref, low_ref, high_ref, node_in, bias, gain, out_ref):
    nodes = node_ref.shape[0]
    rim = low_ref.shape[0]
    count = pre_ref.shape[0]
    rims = jnp.concatenate([low_ref[...], high_ref[...]], axis=0)
    b_message = centred_row(bias[1:2, :])
    b_update = centred_row(bias[3:4, :])
    tnodes = TILE // DEG
    collect = (
        lax.broadcasted_iota(jnp.int32, (tnodes, TILE), 1) // DEG
        == lax.broadcasted_iota(jnp.int32, (tnodes, TILE), 0)
    ).astype(F32).astype(BF16)
    picked = one_hot_rows(send_ref[...] - nodes, 2 * rim)
    hidden = jnp.maximum(pre_ref[...] + dot(picked, rims), 0.0).astype(BF16)
    m = scaled_rows(dot(hidden, w_ref[0]) + b_message).astype(BF16)
    sums = [dot(collect, m[q : q + TILE, :]) for q in range(0, count, TILE)]
    summed = (jnp.concatenate(sums, axis=0) * gain[0:1, :]).astype(BF16)
    hidden = jnp.maximum(own_ref[...] + dot(summed, node_in[1]), 0.0).astype(BF16)
    u = scaled_rows(dot(hidden, w_ref[1]) + b_update) * gain[1:2, :]
    out_ref[...] = (node_ref[...].astype(F32) + u).astype(BF16)


def coarse_level(send, terms, nodes, low, high, node_in, bias, gain):
    pre, own, w = terms
    return pl.pallas_call(
        coarse_kernel,
        out_shape=jax.ShapeDtypeStruct(nodes.shape, BF16),
        in_specs=[VMEM_SPEC] * 10,
        out_specs=VMEM_SPEC,
        cost_estimate=pl.CostEstimate(flops=500_000_000, bytes_accessed=3_000_000, transcendentals=0),
        name="coarse_level",
        compiler_params=limit(16),
    )(send, pre, own, w, nodes, low, high, node_in, bias, gain)


def pair_swaps():
    count = lax.axis_size("dom")
    inner = [(i, i ^ 1) for i in range(count)]
    outer = [(i, ((i + 1) ^ 1) - 1) for i in range(1, count - 1)]
    return inner, outer


def body(
    node_lat,
    edge_lat,
    edge_send,
    halo_list,
    pool_id,
    coarse_lat,
    cedge_lat,
    cedge_send,
    chalo_list,
    fine_edge_in,
    fine_edge_out,
    fine_node_in,
    fine_node_out,
    fine_bias,
    fine_gain,
    coarse_edge_in,
    coarse_edge_out,
    coarse_node_in,
    coarse_node_out,
    coarse_bias,
    coarse_gain,
):
    inner, outer = pair_swaps()
    odd = lax.rem(lax.axis_index("dom"), 2)
    rim = halo_list.shape[0] // 2

    def table_row(send, count, rim_rows):
        lower = jnp.where(odd == 1, count, count + rim_rows)
        upper = jnp.where(odd == 1, count + rim_rows, count)
        return jnp.where(
            send < rim_rows,
            send + lower,
            jnp.where(
                send < rim_rows + count, send - rim_rows, send - (rim_rows + count) + upper
            ),
        )

    border_a, border_b = border_rows(halo_list, node_lat, fine_edge_in, rim)
    rim_a = lax.ppermute(border_a, "dom", inner)
    rim_b = lax.ppermute(border_b, "dom", outer)
    groups = lax.axis_size("group")
    terms = edge_terms(
        edge_send.reshape(-1, 128),
        pool_id.reshape(1, -1),
        edge_lat,
        node_lat,
        rim,
        groups,
        fine_edge_in,
        fine_edge_out,
        fine_node_in,
        fine_node_out,
        fine_bias,
    )
    fine_out, pooled = fine_level(
        terms, node_lat, rim_a, rim_b, fine_node_in, fine_bias, fine_gain
    )
    parts = lax.all_to_all(pooled, "group", 0, 0, tiled=True)
    crim = chalo_list.shape[0] // 2
    clusters = coarse_lat.shape[0]
    lists = jnp.where(odd == 1, chalo_list, jnp.roll(chalo_list, crim))
    coarse_in, coarse_proj, cborder_a, cborder_b = cluster_level(
        parts, coarse_lat, lists.reshape(-1, 1), coarse_edge_in
    )
    crim_a = lax.ppermute(cborder_a, "dom", inner)
    crim_b = lax.ppermute(cborder_b, "dom", outer)
    csend = table_row(cedge_send, clusters, crim).reshape(-1, 1)
    cterms = coarse_edge_terms(
        csend,
        cedge_lat,
        coarse_in,
        coarse_proj,
        coarse_edge_in,
        coarse_edge_out,
        coarse_node_in,
        coarse_node_out,
        coarse_bias,
    )
    coarse_out = coarse_level(
        csend, cterms, coarse_in, crim_a, crim_b, coarse_node_in, coarse_bias, coarse_gain
    )
    return (fine_out, coarse_out)


def solution(mesh):
    rows = P(("group", "dom"), None)
    flat = P(("group", "dom"))
    placed = (rows, rows, flat, flat, flat, rows, rows, flat, flat) + (P(),) * 12
    return jax.shard_map(
        body,
        mesh=mesh,
        in_specs=placed,
        out_specs=(rows, rows),
        check_vma=False,
    )
```

time: 79.9 us -> 59.2 us (0.74)
  Pallas kernels: 42.7 us -> 31.3 us
  local copies, waits for them, and re-layouts: 4.84 us -> 0.44 us
  waiting for transfers between devices: 14.2 us -> 12 us
  other arithmetic: 1.41 us -> 0.02 us
  starting transfers between devices: 15.2 us -> 14.3 us
    pallas_call x1, Pallas kernels: 31.1 us -> 14.8 us  [fine_level(): pl.pallas_call(fine_kernel, out_shape=(jax.ShapeDtypeStruct((n, 256), BF1...]
    pallas_call x2 -> x4, Pallas kernels: 6.2 us -> 14.7 us  [the longest x1 9.28 us: edge_terms(): pl.pallas_call(edges_kernel, out_shape=(shape((e, 256), F32), shape((n, 2...]
    ppermute x1, waiting for transfers between devices: 5.22 us -> 0.01 us  [body(): rim_b = lax.ppermute(border_b, 'dom', outer)]
    pallas_call x1, Pallas kernels: 5.37 us -> 1.8 us  [coarse_level(): pl.pallas_call(coarse_kernel, out_shape=jax.ShapeDtypeStruct(nodes.shape,...]
    all_to_all x1, waiting for transfers between devices: 6.71 us -> 8.92 us  [body(): parts = lax.all_to_all(pooled, 'group', 0, 0, tiled=True)]
    unnamed x14 -> x26, local copies, waits for them, and re-layouts: 2.13 us -> 0.08 us
    mul x1 -> x0, other arithmetic: 1.39 us -> none  [body(): send = table_row(edge_send, nodes, rim) * 2]
    ppermute x2, starting transfers between devices: 5.68 us -> 4.79 us  [the longest x1 4.7 us: body(): crim_b = lax.ppermute(cborder_b, 'dom', outer)]
  transfers between devices with their start and end apart: 5 -> 5, of which waited for: 3 -> 2; matrix products, arithmetic and copies ran while one was open for 4% -> 1% of each run, Pallas kernels for 0% -> 17%
where the time goes in v2:
time: 59.2 us; the launch traced here: 59 us
  Pallas kernels  31.3 us (53%)
  starting transfers between devices  14.3 us (24%)
  waiting for transfers between devices  12 us (20%)
  between operations  0.94 us (2%)
    pallas_call x1, Pallas kernels, fine_level(): pl.pallas_call(fine_kernel, out_shape=(jax.ShapeDtypeStruct((n, 256), BF1...  14.8 us
    pallas_call x1, Pallas kernels, edge_terms(): pl.pallas_call(edges_kernel, out_shape=(shape((e, 256), F32), shape((n, 2...  9.28 us
    all_to_all x1, waiting for transfers between devices, body(): parts = lax.all_to_all(pooled, 'group', 0, 0, tiled=True)  8.92 us
    ppermute x1, starting transfers between devices, body(): crim_b = lax.ppermute(cborder_b, 'dom', outer)  4.7 us
    ppermute x1, starting transfers between devices, body(): rim_b = lax.ppermute(border_b, 'dom', outer)  4.58 us
    all_to_all x1, starting transfers between devices, body(): parts = lax.all_to_all(pooled, 'group', 0, 0, tiled=True)  4.21 us
    pallas_call x1, Pallas kernels, border_rows(): pl.pallas_call(border_kernel, out_shape=(shape, shape), in_specs=[HBM_SPE...  4 us
    ppermute x1, waiting for transfers between devices, body(): crim_b = lax.ppermute(cborder_b, 'dom', outer)  3.06 us
  transfers between devices with their start and end apart: 5, of which 2 were waited for; matrix products, arithmetic and copies ran while one was open for 1% of the time, Pallas kernels for 17%

profile of v2, /device:TPU:103, one launch (start us, length us, event | category | flops | bytes accessed | tf_op | source)
XLA Modules:
  0.0 59.0 jit_solution(13639234684748836852)
XLA Ops:
  0.6 4.0 %border_rows.1 = (bf16[512,256]{1,0:T(8,128)(2,1)S(1)}, bf16[512,256]{1,0:T(8,128)(2,1)S(1)}) custom-call(s32[1024]{0:T(1024)} %list_ref.1, bf16[2048,256]{1,0:T(8,128)(2,1)} %node_hbm.3, bf16[3,256,256]{2,1,0:T(8,128)(2,1)} %w_ref.2), custom_call_target="tpu_custom_call" | custom-call | flops 300000000 | bytes 2000000 | tf_op jit(solution)/shard_map/border_rows/pallas_call | solution.py:94
  4.6 0.8 %collective-permute-start = (bf16[512,256]{1,0:T(8,128)(2,1)S(1)}, bf16[512,256]{1,0:T(8,128)(2,1)S(1)}, u32[]{:S(2)}, u32[]{:S(2)}) collective-permute-start(bf16[512,256]{1,0:T(8,128)(2,1)S(1)} %get-tuple-element.27), channel_id=1, source_target_pairs={{0,1},{1,0},{2,3},{3,2},{4,5},{5,4},{6,7},{7,6},{8,9},{9,8},{10,11... | collective-permute-start | bytes 786440 | tf_op jit(solution)/shard_map/ppermute | solution.py:525
  5.4 4.6 %collective-permute-start.1 = (bf16[512,256]{1,0:T(8,128)(2,1)S(1)}, bf16[512,256]{1,0:T(8,128)(2,1)S(1)}, u32[]{:S(2)}, u32[]{:S(2)}) collective-permute-start(bf16[512,256]{1,0:T(8,128)(2,1)S(1)} %get-tuple-element.28), channel_id=1, source_target_pairs={{1,2},{2,1},{3,4},{4,3},{5,6},{6,5},{7,8},{8,7},{9,10},{10,9},{11,... | collective-permute-start | bytes 786440 | tf_op jit(solution)/shard_map/ppermute | solution.py:526
  10.0 0.0 copy-start.3
  10.0 0.0 copy-start.8
  10.0 0.0 copy-start.9
  10.0 9.3 %edge_terms.1 = (f32[8192,256]{1,0:T(8,128)S(1)}, f32[2048,256]{1,0:T(8,128)S(1)}, f32[6144,128]{1,0:T(8,128)S(1)}, s32[64,128]{1,0:T(8,128)S(1)}, bf16[2,256,25...) custom-call(s32[64,128]{1,0:T(8,128)} %bitcast.6, s32[1,2048]{1,0:T(1,128)} %bitcast.7, ...), custom_call_target="tpu_custom_call" | custom-call | flops 3000000000 | bytes 8000000 | tf_op jit(solution)/shard_map/edge_terms/pallas_call | solution.py:237
  19.3 0.0 collective-permute-done.low_ref
  19.3 0.0 collective-permute-done.1.high_ref
  19.3 0.0 copy-done.3
  19.3 0.0 copy-done.8
  19.4 0.0 copy-done.9
  19.4 0.0 copy-start.11
  19.4 0.0 copy-start
  19.4 0.0 copy-start.4
  19.4 0.0 copy-start.12
  19.4 0.0 copy-start.1
  19.4 0.0 copy-start.2
  19.4 0.0 copy-start.5
  19.5 0.0 copy-start.6
  19.5 0.0 copy-start.7
  19.5 14.8 %fine_level.1 = (bf16[2048,256]{1,0:T(8,128)(2,1)}, bf16[4,272,256]{2,1,0:T(8,128)(2,1)}, f32[6144,128]{1,0:T(8,128)S(1)}) custom-call(s32[64,128]{1,0:T(8,128)S(1)} %get-tuple-element.20.row_ref, f32[8192,256]{1,0:T(8,128)S(1)} %get-tuple-element.21.pre_ref, f32[2048,256]{1,0:T(8,128)S(1)} %get-tuple-element.22.own_ref, ...), custom_call_target="tpu_custom_call", output_to_operand_aliasing={{2}: (3, {})} | custom-call | flops 4000000000 | bytes 8000000 | tf_op jit(solution)/shard_map/fine_level/pallas_call | solution.py:347
  34.3 0.0 copy-start.10
  34.3 4.2 %all-to-all-start = ((bf16[4,272,256]{2,1,0:T(8,128)(2,1)}), bf16[4,272,256]{2,1,0:T(8,128)(2,1)S(1)}, u32[]{:S(2)}, u32[]{:S(2)}) async-start(bf16[4,272,256]{2,1,0:T(8,128)(2,1)} %get-tuple-element.30), calls=%async_computation | async-start | bytes 1114112 | tf_op jit(solution)/shard_map/all_to_all | solution.py:544
  38.5 0.0 copy-done.11
  38.5 0.1 copy.24.list_ref
  38.7 8.9 %all-to-all-done.parts_ref = bf16[4,272,256]{2,1,0:T(8,128)(2,1)S(1)} async-done(((bf16[4,272,256]{2,1,0:T(8,128)(2,1)}), bf16[4,272,256]{2,1,0:T(8,128)(2,1)S(1)}, u32[]{:S(2)}, u32[]{:S(2)}) %all-to-all-start) | async-done | bytes 557088 | tf_op jit(solution)/shard_map/all_to_all | solution.py:544
  47.6 0.0 copy-done
  47.6 0.0 copy-done.4
  47.6 0.6 %cluster_level.1 = (bf16[256,256]{1,0:T(8,128)(2,1)S(1)}, bf16[256,256]{1,0:T(8,128)(2,1)S(1)}, bf16[128,256]{1,0:T(8,128)(2,1)S(1)}, bf16[128,256]{1,0:T(8,128)(2,1)S(1)}) custom-call(bf16[4,272,256]{2,1,0:T(8,128)(2,1)S(1)} %all-to-all-done.parts_ref, bf16[256,256]{1,0:T(8,128)(2,1)S(1)} %copy-done.4, s32[256,1]{1,0:T(8,128)S(1)} %copy.24.list_ref, ...), custom_call_target="tpu_custom_call" | custom-call | flops 70000000 | bytes 1000000 | tf_op jit(solution)/shard_map/cluster_level/pallas_call | solution.py:404
  48.2 0.1 collective-permute-start.2
  48.3 4.7 %collective-permute-start.3 = (bf16[128,256]{1,0:T(8,128)(2,1)S(1)}, bf16[128,256]{1,0:T(8,128)(2,1)S(1)}, u32[]{:S(2)}, u32[]{:S(2)}) collective-permute-start(bf16[128,256]{1,0:T(8,128)(2,1)S(1)} %get-tuple-element.37), channel_id=1, source_target_pairs={{1,2},{2,1},{3,4},{4,3},{5,6},{6,5},{7,8},{8,7},{9,10},{10,9},{11,... | collective-permute-start | bytes 196616 | tf_op jit(solution)/shard_map/ppermute | solution.py:552
  53.0 0.0 copy-done.12
  53.0 0.2 copy.26.send_ref
  53.3 0.0 copy-done.1
  53.3 0.0 copy-done.2
  53.3 0.0 copy-done.5
  53.3 0.0 copy-done.6
  53.3 0.0 copy-done.7
  53.3 0.8 %coarse_edge_terms.1 = (f32[1024,256]{1,0:T(8,128)S(1)}, f32[256,256]{1,0:T(8,128)S(1)}, bf16[2,256,256]{2,1,0:T(8,128)(2,1)S(1)}) custom-call(s32[1024,1]{1,0:T(8,128)S(1)} %copy.26.send_ref, bf16[1024,256]{1,0:T(8,128)(2,1)S(1)} %copy-done.2, bf16[256,256]{1,0:T(8,128)(2,1)S(1)} %get-tuple-element.31.node_ref, ...), custom_call_target="tpu_custom_call" | custom-call | flops 500000000 | bytes 3000000 | tf_op jit(solution)/shard_map/coarse_edge_terms/pallas_call | solution.py:433
  54.1 0.0 collective-permute-done.2.low_ref
  54.1 3.1 %collective-permute-done.3.high_ref = bf16[128,256]{1,0:T(8,128)(2,1)S(1)} collective-permute-done((bf16[128,256]{1,0:T(8,128)(2,1)S(1)}, bf16[128,256]{1,0:T(8,128)(2,1)S(1)}, u32[]{:S(2)}, u32[]{:S(2)}) %collective-permute-start.3) | collective-permute-done | bytes 65568 | tf_op jit(solution)/shard_map/ppermute | solution.py:552
  57.2 0.0 copy-done.10
  57.2 1.8 %coarse_level.1 = bf16[256,256]{1,0:T(8,128)(2,1)} custom-call(s32[1024,1]{1,0:T(8,128)S(1)} %copy.26.send_ref, f32[1024,256]{1,0:T(8,128)S(1)} %get-tuple-element.33.pre_ref, f32[256,256]{1,0:T(8,128)S(1)} %get-tuple-element.34.own_ref, bf16[2,256,256]{2,1,0:T(8,128)(2,1)S(1)} %get-tuple-element.35.w_ref, bf16[256,256]{1,0:T(8,128)(2,1)S(1)} %get-tuple-element.31.node_ref, ...), custom_call_target="tpu_custom_call" | custom-call | flops 500000000 | bytes 3000000 | tf_op jit(solution)/shard_map/coarse_level/pallas_call | solution.py:468
  (3 shorter events, 0.0 us)
Async XLA Ops:
  4.6 14.7 %collective-permute-start = (bf16[512,256]{1,0:T(8,128)(2,1)S(1)}, bf16[512,256]{1,0:T(8,128)(2,1)S(1)}, u32[]{:S(2)}, u32[]{:S(2)}) collective-permute-start(bf16[512,256]{1,0:T(8,128)(2,1)S(1)} %get-tuple-element.27), channel_id=1, source_target_pairs={{0,1},{1,0},{2,3},{3,2},{4,5},{5,4},{6,7},{7,6},{8,9},{9,8},{10,11... | collective-permute-start | bytes 786440 | tf_op jit(solution)/shard_map/ppermute | solution.py:525
  5.4 13.9 %collective-permute-start.1 = (bf16[512,256]{1,0:T(8,128)(2,1)S(1)}, bf16[512,256]{1,0:T(8,128)(2,1)S(1)}, u32[]{:S(2)}, u32[]{:S(2)}) collective-permute-start(bf16[512,256]{1,0:T(8,128)(2,1)S(1)} %get-tuple-element.28), channel_id=1, source_target_pairs={{1,2},{2,1},{3,4},{4,3},{5,6},{6,5},{7,8},{8,7},{9,10},{10,9},{11,... | collective-permute-start | bytes 786440 | tf_op jit(solution)/shard_map/ppermute | solution.py:526
  10.0 9.3 %copy-start.3 = (bf16[2,256,256]{2,1,0:T(8,128)(2,1)S(1)}, bf16[2,256,256]{2,1,0:T(8,128)(2,1)}, u32[]{:S(2)}) copy-start(bf16[2,256,256]{2,1,0:T(8,128)(2,1)} %node_in.3) | copy-start | bytes 786436
  10.0 9.3 %copy-start.8 = (f32[4,256]{1,0:T(4,128)S(1)}, f32[4,256]{1,0:T(4,128)}, u32[]{:S(2)}) copy-start(f32[4,256]{1,0:T(4,128)} %bias.3) | copy-start | bytes 12292
  10.0 9.3 %copy-start.9 = (f32[2,256]{1,0:T(2,128)S(1)}, f32[2,256]{1,0:T(2,128)}, u32[]{:S(2)}) copy-start(f32[2,256]{1,0:T(2,128)} %gain.2) | copy-start | bytes 6148
  19.4 19.1 %copy-start.11 = (s32[256]{0:T(256)S(1)}, s32[256]{0:T(256)}, u32[]{:S(2)}) copy-start(s32[256]{0:T(256)} %param.29) | copy-start | bytes 3076
  19.4 28.2 %copy-start = (bf16[3,256,256]{2,1,0:T(8,128)(2,1)S(1)}, bf16[3,256,256]{2,1,0:T(8,128)(2,1)}, u32[]{:S(2)}) copy-start(bf16[3,256,256]{2,1,0:T(8,128)(2,1)} %edge_in.1) | copy-start | bytes 1179652
  19.4 28.2 %copy-start.4 = (bf16[256,256]{1,0:T(8,128)(2,1)S(1)}, bf16[256,256]{1,0:T(8,128)(2,1)}, u32[]{:S(2)}) copy-start(bf16[256,256]{1,0:T(8,128)(2,1)} %lat_ref.1) | copy-start | bytes 393220
  19.4 33.6 %copy-start.12 = (s32[1024]{0:T(1024)S(1)}, s32[1024]{0:T(1024)}, u32[]{:S(2)}) copy-start(s32[1024]{0:T(1024)} %param.28) | copy-start | bytes 12292
  19.4 33.8 %copy-start.1 = (bf16[2,256,256]{2,1,0:T(8,128)(2,1)S(1)}, bf16[2,256,256]{2,1,0:T(8,128)(2,1)}, u32[]{:S(2)}) copy-start(bf16[2,256,256]{2,1,0:T(8,128)(2,1)} %node_in.5) | copy-start | bytes 786436
  19.4 33.8 %copy-start.2 = (bf16[1024,256]{1,0:T(8,128)(2,1)S(1)}, bf16[1024,256]{1,0:T(8,128)(2,1)}, u32[]{:S(2)}) copy-start(bf16[1024,256]{1,0:T(8,128)(2,1)} %edge_ref.1) | copy-start | bytes 1572868
  19.4 33.8 %copy-start.5 = (bf16[256,256]{1,0:T(8,128)(2,1)S(1)}, bf16[256,256]{1,0:T(8,128)(2,1)}, u32[]{:S(2)}) copy-start(bf16[256,256]{1,0:T(8,128)(2,1)} %edge_out.1) | copy-start | bytes 393220
  19.5 33.8 %copy-start.6 = (bf16[256,256]{1,0:T(8,128)(2,1)S(1)}, bf16[256,256]{1,0:T(8,128)(2,1)}, u32[]{:S(2)}) copy-start(bf16[256,256]{1,0:T(8,128)(2,1)} %node_out.1) | copy-start | bytes 393220
  19.5 33.8 %copy-start.7 = (f32[4,256]{1,0:T(4,128)S(1)}, f32[4,256]{1,0:T(4,128)}, u32[]{:S(2)}) copy-start(f32[4,256]{1,0:T(4,128)} %bias.5) | copy-start | bytes 12292
  34.3 22.9 %copy-start.10 = (f32[2,256]{1,0:T(2,128)S(1)}, f32[2,256]{1,0:T(2,128)}, u32[]{:S(2)}) copy-start(f32[2,256]{1,0:T(2,128)} %gain.3) | copy-start | bytes 6148
  34.3 13.3 %all-to-all-start = ((bf16[4,272,256]{2,1,0:T(8,128)(2,1)}), bf16[4,272,256]{2,1,0:T(8,128)(2,1)S(1)}, u32[]{:S(2)}, u32[]{:S(2)}) async-start(bf16[4,272,256]{2,1,0:T(8,128)(2,1)} %get-tuple-element.30), calls=%async_computation | async-start | bytes 1114112 | tf_op jit(solution)/shard_map/all_to_all | solution.py:544
  48.2 5.9 %collective-permute-start.2 = (bf16[128,256]{1,0:T(8,128)(2,1)S(1)}, bf16[128,256]{1,0:T(8,128)(2,1)S(1)}, u32[]{:S(2)}, u32[]{:S(2)}) collective-permute-start(bf16[128,256]{1,0:T(8,128)(2,1)S(1)} %get-tuple-element.36), channel_id=1, source_target_pairs={{0,1},{1,0},{2,3},{3,2},{4,5},{5,4},{6,7},{7,6},{8,9},{9,8},{10,11... | collective-permute-start | bytes 196616 | tf_op jit(solution)/shard_map/ppermute | solution.py:551
  48.3 8.9 %collective-permute-start.3 = (bf16[128,256]{1,0:T(8,128)(2,1)S(1)}, bf16[128,256]{1,0:T(8,128)(2,1)S(1)}, u32[]{:S(2)}, u32[]{:S(2)}) collective-permute-start(bf16[128,256]{1,0:T(8,128)(2,1)S(1)} %get-tuple-element.37), channel_id=1, source_target_pairs={{1,2},{2,1},{3,4},{4,3},{5,6},{6,5},{7,8},{8,7},{9,10},{10,9},{11,... | collective-permute-start | bytes 196616 | tf_op jit(solution)/shard_map/ppermute | solution.py:552

commit v3 on v2

--- a/solution.py
+++ b/solution.py
@@ -56,68 +56,97 @@
     )
 
 
+def copy_rows(table, rows, index, count):
+    for u in range(count):
+        row = pl.multiple_of(index[u] * 2, 2)
+        rows[2 * u : 2 * u + 2, :] = table[pl.ds(row, 2), :]
+
+
 def border_kernel(
-    list_ref, node_ref, w_ref, a_ref, b_ref, nodes, w, table, rows, index0, index1, list_sem, w_sem, node_sem
+    list_ref, node_ref, w_ref, b_ref, nodes, w, table, rows, index, list_sem, w_sem, node_sem
 ):
-    rim = a_ref.shape[0]
+    rim = b_ref.shape[0]
     odd = lax.rem(lax.axis_index("dom"), 2)
-    w_copy = pltpu.make_async_copy(w_ref.at[0], w, w_sem)
-    w_copy.start()
     copies = [
         pltpu.make_async_copy(node_ref.at[i : i + TILE, :], nodes.at[i : i + TILE, :], node_sem.at[i // TILE])
         for i in range(0, nodes.shape[0], TILE)
     ]
     for c in copies:
         c.start()
-    lists = []
-    for part, (index, first) in enumerate(((index0, (1 - odd) * rim), (index1, odd * rim))):
-        first = pl.multiple_of(first, rim)
-        lists.append(
-            pltpu.make_async_copy(list_ref.at[pl.ds(first, rim)], index, list_sem.at[part])
-        )
-        lists[-1].start()
-    w_copy.wait()
+    first = pl.multiple_of(odd * rim, rim)
+    list_copy = pltpu.make_async_copy(list_ref.at[pl.ds(first, rim)], index, list_sem)
+    list_copy.start()
+    w_copy = pltpu.make_async_copy(w_ref, w, w_sem)
+    w_copy.start()
     for i, c in enumerate(copies):
         c.wait()
-        p = dot(nodes[i * TILE : (i + 1) * TILE, :], w[...])
-        store_split(table, i * TILE, p.astype(BF16).astype(F32))
-    for part, (index, out) in enumerate(((index1, b_ref), (index0, a_ref))):
-        lists[1 - part].wait()
-        for u in range(rim):
-            row = pl.multiple_of(index[u] * 2, 2)
-            rows[2 * u : 2 * u + 2, :] = table[pl.ds(row, 2), :]
-        out[...] = load_split(rows, 0, rim).astype(BF16)
+        store_split(table, i * TILE, nodes[i * TILE : (i + 1) * TILE, :].astype(F32))
+    list_copy.wait()
+    copy_rows(table, rows, index, rim)
+    w_copy.wait()
+    b_ref[...] = dot(load_split(rows, 0, rim).astype(BF16), w[0]).astype(BF16)
 
 
 def border_rows(lists, nodes, edge_in, rim):
-    shape = jax.ShapeDtypeStruct((rim, 256), BF16)
+    shape = jax.ShapeDtypeStruct
     return pl.pallas_call(
         border_kernel,
-        out_shape=(shape, shape),
+        out_shape=(
+            shape((rim, 256), BF16),
+            shape(nodes.shape, BF16),
+            shape(edge_in.shape, BF16),
+        ),
         in_specs=[HBM_SPEC] * 3,
-        out_specs=(VMEM_SPEC, VMEM_SPEC),
+        out_specs=(VMEM_SPEC,) * 3,
         scratch_shapes=[
-            pltpu.VMEM(nodes.shape, BF16),
-            pltpu.VMEM((256, 256), BF16),
             pltpu.VMEM((2 * nodes.shape[0], 128), F32),
             pltpu.VMEM((2 * rim, 128), F32),
             pltpu.SMEM((rim,), jnp.int32),
-            pltpu.SMEM((rim,), jnp.int32),
-            pltpu.SemaphoreType.DMA((2,)),
+            pltpu.SemaphoreType.DMA,
             pltpu.SemaphoreType.DMA,
             pltpu.SemaphoreType.DMA((nodes.shape[0] // TILE,)),
         ],
-        cost_estimate=pl.CostEstimate(flops=300_000_000, bytes_accessed=2_000_000, transcendentals=0),
+        cost_estimate=pl.CostEstimate(flops=70_000_000, bytes_accessed=2_000_000, transcendentals=0),
         name="border_rows",
-        compiler_params=limit(10),
+        compiler_params=limit(8),
     )(hbm(lists), hbm(nodes), hbm(edge_in))
 
 
+def own_kernel(list_ref, node_ref, w_ref, a_ref, table, rows, index, list_sem):
+    rim = a_ref.shape[0]
+    odd = lax.rem(lax.axis_index("dom"), 2)
+    first = pl.multiple_of((1 - odd) * rim, rim)
+    list_copy = pltpu.make_async_copy(list_ref.at[pl.ds(first, rim)], index, list_sem)
+    list_copy.start()
+    store_split(table, 0, node_ref[...].astype(F32))
+    list_copy.wait()
+    copy_rows(table, rows, index, rim)
+    a_ref[...] = dot(load_split(rows, 0, rim).astype(BF16), w_ref[0]).astype(BF16)
+
+
+def own_rows(lists, nodes, edge_in, rim):
+    return pl.pallas_call(
+        own_kernel,
+        out_shape=jax.ShapeDtypeStruct((rim, 256), BF16),
+        in_specs=[HBM_SPEC] + [VMEM_SPEC] * 2,
+        out_specs=VMEM_SPEC,
+        scratch_shapes=[
+            pltpu.VMEM((2 * nodes.shape[0], 128), F32),
+            pltpu.VMEM((2 * rim, 128), F32),
+            pltpu.SMEM((rim,), jnp.int32),
+            pltpu.SemaphoreType.DMA,
+        ],
+        cost_estimate=pl.CostEstimate(flops=70_000_000, bytes_accessed=2_000_000, transcendentals=0),
+        name="own_rows",
+        compiler_params=limit(8),
+    )(hbm(lists), nodes, edge_in)
+
+
 def edges_kernel(
+    node,
+    edge_in,
     send_hbm,
     pool_hbm,
-    node_hbm,
-    edge_in_hbm,
     edge_out_hbm,
     node_in_hbm,
     node_out_hbm,
@@ -125,15 +154,13 @@
     edge_hbm,
     pre_ref,
     own_ref,
-    table_ref,
     row_ref,
     w_ref,
     member_ref,
     count_ref,
+    table_ref,
     send,
     pool,
-    node,
-    edge_in,
     edge_out,
     node_in,
     node_out,
@@ -152,14 +179,12 @@
         pltpu.make_async_copy(source, target, small_sem.at[i])
         for i, (source, target) in enumerate(
             (
+                (bias_hbm, bias),
+                (pool_hbm, pool),
                 (send_hbm, send),
-                (pool_hbm, pool),
-                (node_hbm, node),
-                (edge_in_hbm, edge_in),
                 (edge_out_hbm, edge_out),
                 (node_in_hbm, node_in),
                 (node_out_hbm, node_out),
-                (bias_hbm, bias),
             )
         )
     ]
@@ -173,28 +198,35 @@
     ]
     for c in small + copies:
         c.start()
-    for c in small:
-        c.wait()
-    odd = lax.rem(lax.axis_index("dom"), 2)
-    sent = send[...]
-    lower = jnp.where(odd == 1, nodes, nodes + rim)
-    upper = jnp.where(odd == 1, nodes + rim, nodes) - (rim + nodes)
-    row_ref[...] = 2 * (
-        sent + jnp.where(sent < rim, lower, jnp.where(sent < rim + nodes, -rim, upper))
-    )
-    w_ref[0] = centred_weight(edge_out[...])
-    w_ref[1] = centred_weight(node_out[...])
+    small[0].wait()
+    small[1].wait()
+
+    me = lax.axis_index("group")
+    owners = member_ref.shape[0]
+    ids = pool[...]
+    row = lax.broadcasted_iota(jnp.int32, (256, 128), 0).astype(F32).astype(BF16)
+    lane = lax.broadcasted_iota(jnp.int32, (256, 128), 1)
+    one = jnp.ones((256, 128), BF16)
+    zero = jnp.zeros((256, 128), BF16)
+    for k, step in enumerate((2, 1, 3, 0)):
+        base = lax.rem(me + step, owners) * 256
+        local = ids - base
+        inside = jnp.logical_and(local >= 0, local < 256)
+        local = jnp.where(inside, local, 256).astype(F32).astype(BF16)
+        total = zero
+        for i in range(0, nodes, 128):
+            here = jnp.broadcast_to(local[:, i : i + 128], (256, 128))
+            member = jnp.where(row == here, one, zero)
+            member_ref[k, :, i : i + 128] = member
+            total = total + member
+        count = jnp.sum(total.astype(F32), axis=1, keepdims=True)
+        high = jnp.floor(count * (1.0 / 64.0))
+        low = count - high * 64.0
+        both = jnp.where(lane == 0, low, jnp.where(lane == 1, high, 0.0))
+        count_ref[k] = both.T[:16, :].astype(BF16)
+
     b_edge = bias[0:1, :]
     b_node = bias[2:3, :]
-
-    def own_terms(k, carry):
-        i = pl.multiple_of(k * CHUNK, CHUNK)
-        own = node[pl.ds(i, CHUNK), :]
-        store_split(table_ref, i, dot(own, edge_in[0]).astype(BF16).astype(F32))
-        own_ref[pl.ds(i, CHUNK), :] = dot(own, node_in[0]) + b_node
-        return carry
-
-    lax.fori_loop(0, nodes // CHUNK, own_terms, 0, unroll=True)
 
     def edge_chunk(c, carry):
         own = node[pl.ds(pl.multiple_of(c * cnodes, cnodes), cnodes), :]
@@ -211,53 +243,52 @@
 
     lax.fori_loop(0, chunks, edge_chunk, 0, unroll=2)
 
-    ids = pool[...]
-    lane = lax.broadcasted_iota(jnp.int32, (256, 128), 1)
-
-    def membership(g, carry):
-        member = (
-            lax.broadcasted_iota(jnp.int32, (256, nodes), 0) + g * 256 == ids
-        ).astype(F32)
-        member_ref[g] = member.astype(BF16)
-        count = jnp.sum(member, axis=1, keepdims=True)
-        high = jnp.floor(count * (1.0 / 256.0))
-        low = count - high * 256.0
-        both = jnp.where(lane == 0, low, jnp.where(lane == 1, high, 0.0))
-        count_ref[g] = both.T[:16, :].astype(BF16)
-        return carry
-
-    lax.fori_loop(0, member_ref.shape[0], membership, 0)
+    for c in small[2:]:
+        c.wait()
+    odd = lax.rem(lax.axis_index("dom"), 2)
+    sent = send[...]
+    lower = jnp.where(odd == 1, nodes, nodes + rim)
+    upper = jnp.where(odd == 1, nodes + rim, nodes) - (rim + nodes)
+    row_ref[...] = 2 * (
+        sent + jnp.where(sent < rim, lower, jnp.where(sent < rim + nodes, -rim, upper))
+    )
+    w_ref[0] = centred_weight(edge_out[...])
+    w_ref[1] = centred_weight(node_out[...])
+    for i in range(0, nodes, CHUNK):
+        own = node[i : i + CHUNK, :]
+        store_split(table_ref, i, dot(own, edge_in[0]).astype(BF16).astype(F32))
+        own_ref[i : i + CHUNK, :] = dot(own, node_in[0]) + b_node
 
 
 def edge_terms(send, pool, edges, nodes, rim, owners, edge_in, edge_out, node_in, node_out, bias):
     n = nodes.shape[0]
     e = edges.shape[0]
     shape = jax.ShapeDtypeStruct
-    operands = (send, pool, nodes, edge_in, edge_out, node_in, node_out, bias, edges)
+    operands = (send, pool, edge_out, node_in, node_out, bias, edges)
     return pl.pallas_call(
         edges_kernel,
         out_shape=(
             shape((e, 256), F32),
             shape((n, 256), F32),
-            shape((2 * (n + 2 * rim), 128), F32),
             shape(send.shape, jnp.int32),
             shape((2, 256, 256), BF16),
             shape((owners, 256, n), BF16),
             shape((owners, 16, 256), BF16),
+            shape((2 * (n + 2 * rim), 128), F32),
         ),
-        in_specs=[HBM_SPEC] * len(operands),
+        in_specs=[VMEM_SPEC] * 2 + [HBM_SPEC] * len(operands),
         out_specs=(VMEM_SPEC,) * 7,
         scratch_shapes=[pltpu.VMEM(x.shape, x.dtype) for x in operands]
         + [
             pltpu.VMEM((CHUNK, 128), F32),
             pltpu.VMEM((CHUNK, 128), F32),
-            pltpu.SemaphoreType.DMA((8,)),
+            pltpu.SemaphoreType.DMA((6,)),
             pltpu.SemaphoreType.DMA((e // CHUNK,)),
         ],
         cost_estimate=pl.CostEstimate(flops=3_000_000_000, bytes_accessed=8_000_000, transcendentals=0),
         name="edge_terms",
         compiler_params=limit(14),
-    )(*(hbm(x) for x in operands))
+    )(nodes, edge_in, *(hbm(x) for x in operands))
 
 
 def fine_kernel(
@@ -270,20 +301,20 @@
     count_ref,
     low_ref,
     high_ref,
-    node_hbm,
+    node,
     node_in,
     bias,
     gain,
     out_hbm,
-    pooled_ref,
+    out,
+    up_ref,
+    down_ref,
     table,
     rows,
-    node,
-    out,
     summed,
-    index,
+    index0,
+    index1,
     index_sem,
-    node_sem,
     out_sem,
 ):
     nodes = node.shape[0]
@@ -292,13 +323,15 @@
     cnodes = GATHER // DEG
     lines = GATHER // 128
 
-    def index_copy(c):
+    def index_copy(c, slot):
+        c = jnp.minimum(c, chunks - 1)
         at = pl.ds(pl.multiple_of(c * lines, lines), lines)
-        return pltpu.make_async_copy(row_ref.at[at, :], index, index_sem)
-
-    index_copy(0).start()
-    node_copy = pltpu.make_async_copy(node_hbm, node, node_sem)
-    node_copy.start()
+        return pltpu.make_async_copy(
+            row_ref.at[at, :], index1 if slot else index0, index_sem.at[slot]
+        )
+
+    index_copy(0, 0).start()
+    index_copy(1, 1).start()
     store_split(table, nodes, low_ref[...].astype(F32))
     store_split(table, nodes + rim, high_ref[...].astype(F32))
     b_message = centred_row(bias[1:2, :])
@@ -311,64 +344,107 @@
         == lax.broadcasted_iota(jnp.int32, (tnodes, TILE), 0)
     ).astype(F32).astype(BF16)
 
-    def chunk(c, carry):
-        index_copy(c).wait()
-        for u in range(GATHER):
-            row = pl.multiple_of(index[u // 128, u % 128], 2)
-            rows[2 * u : 2 * u + 2, :] = table[pl.ds(row, 2), :]
-        index_copy(jnp.minimum(c + 1, chunks - 1)).start()
-        pre = pre_ref[pl.ds(pl.multiple_of(c * GATHER, GATHER), GATHER), :]
-        hidden = jnp.maximum(pre + load_split(rows, 0, GATHER), 0.0).astype(BF16)
-        m = scaled_rows(dot(hidden, w_ref[0]) + b_message).astype(BF16)
-        sums = [dot(collect, m[q : q + TILE, :]) for q in range(0, GATHER, TILE)]
-        summed[pl.ds(pl.multiple_of(c * cnodes, cnodes), cnodes), :] = (
-            jnp.concatenate(sums, axis=0) * g_message
-        ).astype(BF16)
+    def pair(k, carry):
+        for slot, index in enumerate((index0, index1)):
+            c = 2 * k + slot
+            index_copy(c, slot).wait()
+            for u in range(GATHER):
+                row = pl.multiple_of(index[u // 128, u % 128], 2)
+                rows[2 * u : 2 * u + 2, :] = table[pl.ds(row, 2), :]
+            index_copy(c + 2, slot).start()
+            pre = pre_ref[pl.ds(pl.multiple_of(c * GATHER, GATHER), GATHER), :]
+            hidden = jnp.maximum(pre + load_split(rows, 0, GATHER), 0.0).astype(BF16)
+            m = scaled_rows(dot(hidden, w_ref[0]) + b_message).astype(BF16)
+            sums = [dot(collect, m[q : q + TILE, :]) for q in range(0, GATHER, TILE)]
+            summed[pl.ds(pl.multiple_of(c * cnodes, cnodes), cnodes), :] = (
+                jnp.concatenate(sums, axis=0) * g_message
+            ).astype(BF16)
         return carry
 
-    lax.fori_loop(0, chunks, chunk, 0)
-    index_copy(0).wait()
-    node_copy.wait()
+    lax.fori_loop(0, chunks // 2, pair, 0)
+    index_copy(0, 0).wait()
+    index_copy(1, 1).wait()
     hidden = jnp.maximum(own_ref[...] + dot(summed[...], node_in[1]), 0.0).astype(BF16)
     u = scaled_rows(dot(hidden, w_ref[1]) + b_update) * g_update
     out[...] = (node[...].astype(F32) + u).astype(BF16)
     out_copy = pltpu.make_async_copy(out, out_hbm, out_sem)
     out_copy.start()
-    for g in range(pooled_ref.shape[0]):
-        pooled_ref[g, :256, :] = dot(member_ref[g], out[...]).astype(BF16)
-        pooled_ref[g, 256:, :] = count_ref[g]
+    far = dot(member_ref[0], out[...]).astype(BF16)
+    up_ref[:256, :] = far[:, :128]
+    down_ref[:256, :] = far[:, 128:]
+    up_ref[256:, :] = count_ref[0, :, :128]
+    down_ref[256:, :] = count_ref[0, :, 128:]
     out_copy.wait()
 
 
-def fine_level(terms, nodes, low, high, node_in, bias, gain):
+def fine_level(terms, table, nodes, low, high, node_in, bias, gain):
     n = nodes.shape[0]
-    pre, own, table, row, w, member, count = terms
-    owners = member.shape[0]
+    pre, own, row, w, member, count = terms
+    shape = jax.ShapeDtypeStruct
     outs = pl.pallas_call(
         fine_kernel,
         out_shape=(
-            jax.ShapeDtypeStruct((n, 256), BF16),
-            jax.ShapeDtypeStruct((owners, 272, 256), BF16),
-            jax.ShapeDtypeStruct(table.shape, F32),
+            shape((n, 256), BF16),
+            shape((n, 256), BF16),
+            shape((272, 128), BF16),
+            shape((272, 128), BF16),
+            shape(table.shape, F32),
         ),
-        in_specs=[VMEM_SPEC] * 9 + [HBM_SPEC] + [VMEM_SPEC] * 3,
-        out_specs=(HBM_SPEC, VMEM_SPEC, VMEM_SPEC),
+        in_specs=[VMEM_SPEC] * 13,
+        out_specs=(HBM_SPEC,) + (VMEM_SPEC,) * 4,
         scratch_shapes=[
             pltpu.VMEM((2 * GATHER, 128), F32),
             pltpu.VMEM((n, 256), BF16),
-            pltpu.VMEM((n, 256), BF16),
-            pltpu.VMEM((n, 256), BF16),
             pltpu.SMEM((GATHER // 128, 128), jnp.int32),
-            pltpu.SemaphoreType.DMA,
-            pltpu.SemaphoreType.DMA,
+            pltpu.SMEM((GATHER // 128, 128), jnp.int32),
+            pltpu.SemaphoreType.DMA((2,)),
             pltpu.SemaphoreType.DMA,
         ],
-        input_output_aliases={3: 2},
+        input_output_aliases={3: 4},
         cost_estimate=pl.CostEstimate(flops=4_000_000_000, bytes_accessed=8_000_000, transcendentals=0),
         name="fine_level",
-        compiler_params=limit(16),
-    )(row, pre, own, table, w, member, count, low, high, hbm(nodes), node_in, bias, gain)
-    return outs[0], outs[1]
+        compiler_params=limit(14),
+    )(row, pre, own, table, w, member, count, low, high, nodes, node_in, bias, gain)
+    return outs[:4]
+
+
+def pool_kernel(member_ref, count_ref, out_ref, next_ref, prev_ref, mine_ref):
+    for k, ref in enumerate((next_ref, prev_ref, mine_ref)):
+        ref[:256, :] = dot(member_ref[k + 1], out_ref[...]).astype(BF16)
+        ref[256:, :] = count_ref[k + 1]
+
+
+def pool_rows(member, count, out):
+    shape = jax.ShapeDtypeStruct((272, 256), BF16)
+    return pl.pallas_call(
+        pool_kernel,
+        out_shape=(shape,) * 3,
+        in_specs=[VMEM_SPEC] * 3,
+        out_specs=(VMEM_SPEC,) * 3,
+        cost_estimate=pl.CostEstimate(flops=800_000_000, bytes_accessed=4_000_000, transcendentals=0),
+        name="pool_rows",
+        compiler_params=limit(8),
+    )(member, count, out)
+
+
+def relay_kernel(next_ref, prev_ref, up_ref, down_ref, next_out, prev_out):
+    next_out[:, :128] = (next_ref[:, :128].astype(F32) + up_ref[...].astype(F32)).astype(BF16)
+    next_out[:, 128:] = next_ref[:, 128:]
+    prev_out[:, :128] = prev_ref[:, :128]
+    prev_out[:, 128:] = (prev_ref[:, 128:].astype(F32) + down_ref[...].astype(F32)).astype(BF16)
+
+
+def relay_rows(next_rows, prev_rows, up, down):
+    shape = jax.ShapeDtypeStruct((272, 256), BF16)
+    return pl.pallas_call(
+        relay_kernel,
+        out_shape=(shape,) * 2,
+        in_specs=[VMEM_SPEC] * 4,
+        out_specs=(VMEM_SPEC,) * 2,
+        cost_estimate=pl.CostEstimate(flops=200_000, bytes_accessed=1_000_000, transcendentals=0),
+        name="relay_rows",
+        compiler_params=limit(8),
+    )(next_rows, prev_rows, up, down)
 
 
 def one_hot_rows(index_col, count):
@@ -377,15 +453,12 @@
     ).astype(F32).astype(BF16)
 
 
-def cluster_kernel(parts_ref, lat_ref, list_ref, w_ref, in_ref, proj_ref, a_ref, b_ref):
+def cluster_kernel(mine_ref, below_ref, above_ref, lat_ref, list_ref, w_ref, in_ref, proj_ref, a_ref, b_ref):
     clusters = lat_ref.shape[0]
     rim = a_ref.shape[0]
-    total = parts_ref[0, :clusters, :].astype(F32)
-    tail = parts_ref[0, clusters:, :].astype(F32)
-    for g in range(1, parts_ref.shape[0]):
-        total = total + parts_ref[g, :clusters, :].astype(F32)
-        tail = tail + parts_ref[g, clusters:, :].astype(F32)
-    count = tail[0:1, :] + 256.0 * tail[1:2, :]
+    total = mine_ref[...].astype(F32) + below_ref[...].astype(F32) + above_ref[...].astype(F32)
+    count = total[clusters : clusters + 1, :] + 64.0 * total[clusters + 1 : clusters + 2, :]
+    total = total[:clusters, :]
     count = jnp.broadcast_to(count, (8, clusters)).T[:, :1]
     mean = total / jnp.maximum(count, 1.0)
     coarse_in = (lat_ref[...].astype(F32) + mean).astype(BF16)
@@ -397,19 +470,19 @@
     b_ref[...] = border[rim:, :]
 
 
-def cluster_level(parts, lat, lists, edge_in):
+def cluster_level(mine, below, above, lat, lists, edge_in):
     n = lat.shape[0]
     shape = jax.ShapeDtypeStruct((n, 256), BF16)
     rim = jax.ShapeDtypeStruct((lists.shape[0] // 2, 256), BF16)
     return pl.pallas_call(
         cluster_kernel,
         out_shape=(shape, shape, rim, rim),
-        in_specs=[VMEM_SPEC] * 4,
+        in_specs=[VMEM_SPEC] * 6,
         out_specs=(VMEM_SPEC,) * 4,
         cost_estimate=pl.CostEstimate(flops=70_000_000, bytes_accessed=1_000_000, transcendentals=0),
         name="cluster_level",
         compiler_params=limit(16),
-    )(parts, lat, lists, edge_in)
+    )(mine, below, above, lat, lists, edge_in)
 
 
 def coarse_edges_kernel(send_ref, edge_ref, node_ref, proj_ref, edge_in, edge_out, node_in, node_out, bias, pre_ref, own_ref, w_ref):
@@ -521,35 +594,43 @@
             ),
         )
 
-    border_a, border_b = border_rows(halo_list, node_lat, fine_edge_in, rim)
+    border_b, node_near, edge_in_near = border_rows(halo_list, node_lat, fine_edge_in, rim)
+    rim_b = lax.ppermute(border_b, "dom", outer)
+    border_a = own_rows(halo_list, node_near, edge_in_near, rim)
     rim_a = lax.ppermute(border_a, "dom", inner)
-    rim_b = lax.ppermute(border_b, "dom", outer)
     groups = lax.axis_size("group")
-    terms = edge_terms(
+    *terms, table = edge_terms(
         edge_send.reshape(-1, 128),
         pool_id.reshape(1, -1),
         edge_lat,
-        node_lat,
+        node_near,
         rim,
         groups,
-        fine_edge_in,
+        edge_in_near,
         fine_edge_out,
         fine_node_in,
         fine_node_out,
         fine_bias,
     )
-    fine_out, pooled = fine_level(
-        terms, node_lat, rim_a, rim_b, fine_node_in, fine_bias, fine_gain
-    )
-    parts = lax.all_to_all(pooled, "group", 0, 0, tiled=True)
+    fine_out, fine_near, far_up, far_down = fine_level(
+        terms, table, node_near, rim_a, rim_b, fine_node_in, fine_bias, fine_gain
+    )
+    onward = [(i, (i + 1) % groups) for i in range(groups)]
+    back = [(target, source) for source, target in onward]
+    far_up = lax.ppermute(far_up, "group", onward)
+    far_down = lax.ppermute(far_down, "group", back)
+    next_rows, prev_rows, mine = pool_rows(terms[4], terms[5], fine_near)
+    next_rows, prev_rows = relay_rows(next_rows, prev_rows, far_up, far_down)
+    below = lax.ppermute(next_rows, "group", onward)
+    above = lax.ppermute(prev_rows, "group", back)
     crim = chalo_list.shape[0] // 2
     clusters = coarse_lat.shape[0]
     lists = jnp.where(odd == 1, chalo_list, jnp.roll(chalo_list, crim))
     coarse_in, coarse_proj, cborder_a, cborder_b = cluster_level(
-        parts, coarse_lat, lists.reshape(-1, 1), coarse_edge_in
-    )
+        mine, below, above, coarse_lat, lists.reshape(-1, 1), coarse_edge_in
+    )
+    crim_b = lax.ppermute(cborder_b, "dom", outer)
     crim_a = lax.ppermute(cborder_a, "dom", inner)
-    crim_b = lax.ppermute(cborder_b, "dom", outer)
     csend = table_row(cedge_send, clusters, crim).reshape(-1, 1)
     cterms = coarse_edge_terms(
         csend,
@@ -572,6 +653,7 @@
     rows = P(("group", "dom"), None)
     flat = P(("group", "dom"))
     placed = (rows, rows, flat, flat, flat, rows, rows, flat, flat) + (P(),) * 12
+
     return jax.shard_map(
         body,
         mesh=mesh,

time: 59.2 us -> 53.6 us (0.905)
  waiting for transfers between devices: 12 us -> 7.34 us
  Pallas kernels: 31.3 us -> 27.3 us
  starting transfers between devices: 14.3 us -> 16.7 us
  local copies, waits for them, and re-layouts: 0.44 us -> 1.19 us
    all_to_all x1 -> x0, waiting for transfers between devices: 8.92 us -> none  [body(): parts = lax.all_to_all(pooled, 'group', 0, 0, tiled=True)]
    ppermute x0 -> x4, starting transfers between devices: none -> 5.8 us  [the longest x1 1.53 us: body(): far_down = lax.ppermute(far_down, 'group', back)]
    ppermute x0 -> x4, waiting for transfers between devices: none -> 4.56 us  [the longest x1 3.91 us: body(): below = lax.ppermute(next_rows, 'group', onward)]
    all_to_all x1 -> x0, starting transfers between devices: 4.21 us -> none  [body(): parts = lax.all_to_all(pooled, 'group', 0, 0, tiled=True)]
    pallas_call x2 -> x5, Pallas kernels: 18.8 us -> 16.7 us  [the longest x1 12.3 us: fine_level(): pl.pallas_call(fine_kernel, out_shape=(shape((n, 256), BF16), shape((n, 2...]
    pallas_call x1, Pallas kernels: 9.28 us -> 7.36 us  [edge_terms(): pl.pallas_call(edges_kernel, out_shape=(shape((e, 256), F32), shape((n, 2...]
    slice x1, local copies, waits for them, and re-layouts: 0.01 us -> 0.76 us  [body(): lists = jnp.where(odd == 1, chalo_list, jnp.roll(chalo_list, crim))]
  transfers between devices with their start and end apart: 5 -> 8, of which waited for: 2 -> 3; matrix products, arithmetic and copies ran while one was open for 1% -> 2% of each run, Pallas kernels for 17% -> 17%
where the time goes in v3:
time: 53.6 us; the launch traced here: 53.4 us
  Pallas kernels  27.3 us (51%)
  starting transfers between devices  16.7 us (31%)
  waiting for transfers between devices  7.34 us (14%)
  local copies, waits for them, and re-layouts  1.19 us (2%)
  between operations  0.92 us (2%)
    pallas_call x1, Pallas kernels, fine_level(): pl.pallas_call(fine_kernel, out_shape=(shape((n, 256), BF16), shape((n, 2...  12.3 us
    pallas_call x1, Pallas kernels, edge_terms(): pl.pallas_call(edges_kernel, out_shape=(shape((e, 256), F32), shape((n, 2...  7.36 us
    ppermute x1, starting transfers between devices, body(): crim_b = lax.ppermute(cborder_b, 'dom', outer)  4.96 us
    ppermute x1, starting transfers between devices, body(): rim_b = lax.ppermute(border_b, 'dom', outer)  4.57 us
    ppermute x1, waiting for transfers between devices, body(): below = lax.ppermute(next_rows, 'group', onward)  3.91 us
    ppermute x1, waiting for transfers between devices, body(): crim_b = lax.ppermute(cborder_b, 'dom', outer)  2.77 us
    pallas_call x1, Pallas kernels, border_rows(): pl.pallas_call(border_kernel, out_shape=(shape((rim, 256), BF16), shape(n...  2.03 us
    pallas_call x1, Pallas kernels, coarse_level(): pl.pallas_call(coarse_kernel, out_shape=jax.ShapeDtypeStruct(nodes.shape,...  1.8 us
  transfers between devices with their start and end apart: 8, of which 3 were waited for; matrix products, arithmetic and copies ran while one was open for 2% of the time, Pallas kernels for 17%

profile of v3, /device:TPU:103, one launch (start us, length us, event | category | flops | bytes accessed | tf_op | source)
XLA Modules:
  0.0 53.4 jit_solution(13801554859297108768)
XLA Ops:
  0.6 2.0 %border_rows.1 = (bf16[512,256]{1,0:T(8,128)(2,1)S(1)}, bf16[2048,256]{1,0:T(8,128)(2,1)S(1)}, bf16[3,256,256]{2,1,0:T(8,128)(2,1)S(1)}) custom-call(s32[1024]{0:T(1024)} %list_ref.3, bf16[2048,256]{1,0:T(8,128)(2,1)} %node_ref.1, bf16[3,256,256]{2,1,0:T(8,128)(2,1)} %w_ref.2), custom_call_target="tpu_custom_call" | custom-call | flops 70000000 | bytes 2000000 | tf_op jit(solution)/shard_map/border_rows/pallas_call | solution.py:92
  2.7 1.3 %own_rows.1 = bf16[512,256]{1,0:T(8,128)(2,1)S(1)} custom-call(s32[1024]{0:T(1024)} %list_ref.3, bf16[2048,256]{1,0:T(8,128)(2,1)S(1)} %get-tuple-element.28.node.node_ref, bf16[3,256,256]{2,1,0:T(8,128)(2,1)S(1)} %get-tuple-element.29.edge_in.w_ref), custom_call_target="tpu_custom_call" | custom-call | flops 70000000 | bytes 2000000 | tf_op jit(solution)/shard_map/own_rows/pallas_call | solution.py:128
  4.0 0.8 %collective-permute-start = (bf16[512,256]{1,0:T(8,128)(2,1)S(1)}, bf16[512,256]{1,0:T(8,128)(2,1)S(1)}, u32[]{:S(2)}, u32[]{:S(2)}) collective-permute-start(bf16[512,256]{1,0:T(8,128)(2,1)S(1)} %own_rows.1), channel_id=1, source_target_pairs={{0,1},{1,0},{2,3},{3,2},{4,5},{5,4},{6,7},{7,6},{8,9},{9,8},{10,11... | collective-permute-start | bytes 786440 | tf_op jit(solution)/shard_map/ppermute | solution.py:600
  4.8 4.6 %collective-permute-start.1 = (bf16[512,256]{1,0:T(8,128)(2,1)S(1)}, bf16[512,256]{1,0:T(8,128)(2,1)S(1)}, u32[]{:S(2)}, u32[]{:S(2)}) collective-permute-start(bf16[512,256]{1,0:T(8,128)(2,1)S(1)} %get-tuple-element.37), channel_id=1, source_target_pairs={{1,2},{2,1},{3,4},{4,3},{5,6},{6,5},{7,8},{8,7},{9,10},{10,9},{11,... | collective-permute-start | bytes 786440 | tf_op jit(solution)/shard_map/ppermute | solution.py:598
  9.4 0.8 %fusion = (s32[128]{0:T(128)S(1)}, s32[128]{0:T(128)S(1)}) fusion(s32[256]{0:T(256)} %param.29), kind=kLoop, calls=%fused_computation.2 | loop fusion | bytes 2048 | tf_op jit(solution)/shard_map/jit(_roll_static)/slice | solution.py:628
  10.1 7.4 %edge_terms.1 = (f32[8192,256]{1,0:T(8,128)S(1)}, f32[2048,256]{1,0:T(8,128)S(1)}, s32[64,128]{1,0:T(8,128)S(1)}, bf16[2,256,256]{2,1,0:T(8,128)(2,1)S(1)}, bf16...) custom-call(bf16[2048,256]{1,0:T(8,128)(2,1)S(1)} %get-tuple-element.28.node.node_ref, ...), custom_call_target="tpu_custom_call" | custom-call | flops 3000000000 | bytes 8000000 | tf_op jit(solution)/shard_map/edge_terms/pallas_call | solution.py:268
  17.5 0.0 collective-permute-done.low_ref
  17.5 0.0 collective-permute-done.1.high_ref
  17.5 0.0 copy-done.3
  17.5 0.0 copy-done.8
  17.5 0.0 copy-done.9
  17.5 12.3 %fine_level.1 = (bf16[2048,256]{1,0:T(8,128)(2,1)}, bf16[2048,256]{1,0:T(8,128)(2,1)S(1)}, bf16[272,128]{1,0:T(8,128)(2,1)S(1)}, bf16[272,128]{1,0:T(8,128)(2,1)S(1)}, f32[6144,128]{1,0:T(8,128)S(1)}) custom-call(s32[64,128]{1,0:T(8,128)S(1)} %get-tuple-element.30.row_ref, ...), custom_call_target="tpu_custom_call", output_to_operand_aliasing={{4}: (3, {})} | custom-call | flops 4000000000 | bytes 8000000 | tf_op jit(solution)/shard_map/fine_level/pallas_call | solution.py:384
  29.8 0.0 copy-start.11
  29.9 0.0 copy-start
  29.9 0.0 copy-start.6
  29.9 0.0 copy-start.12
  29.9 0.0 copy-start.1
  29.9 0.0 copy-start.2
  29.9 0.0 copy-start.4
  29.9 0.0 copy-start.5
  29.9 0.0 copy-start.7
  30.0 1.4 %collective-permute-start.2 = (bf16[272,128]{1,0:T(8,128)(2,1)S(1)}, bf16[272,128]{1,0:T(8,128)(2,1)S(1)}, u32[]{:S(2)}, u32[]{:S(2)}) collective-permute-start(bf16[272,128]{1,0:T(8,128)(2,1)S(1)} %get-tuple-element.43), channel_id=1, source_target_pairs={{0,64},{64,128},{128,192},{192,0},{1,65},{65,129},{129,193},{193,1... | collective-permute-start | bytes 208904 | tf_op jit(solution)/shard_map/ppermute | solution.py:620
  31.3 1.5 %collective-permute-start.3 = (bf16[272,128]{1,0:T(8,128)(2,1)S(1)}, bf16[272,128]{1,0:T(8,128)(2,1)S(1)}, u32[]{:S(2)}, u32[]{:S(2)}) collective-permute-start(bf16[272,128]{1,0:T(8,128)(2,1)S(1)} %get-tuple-element.44), channel_id=1, source_target_pairs={{64,0},{128,64},{192,128},{0,192},{65,1},{129,65},{193,129},{1,193... | collective-permute-start | bytes 208904 | tf_op jit(solution)/shard_map/ppermute | solution.py:621
  32.9 1.0 %pool_rows.1 = (bf16[272,256]{1,0:T(8,128)(2,1)S(1)}, bf16[272,256]{1,0:T(8,128)(2,1)S(1)}, bf16[272,256]{1,0:T(8,128)(2,1)S(1)}) custom-call(bf16[4,256,2048]{2,1,0:T(8,128)(2,1)S(1)} %get-tuple-element.35.member_ref, bf16[4,16,256]{2,1,0:T(8,128)(2,1)S(1)} %get-tuple-element.36.count_ref, bf16[2048,256]{1,0:T(8,128)(2,1)S(1)} %get-tuple-element.39.out_ref), custom_call_target="tpu_custom_call" | custom-call | flops 800000000 | bytes 4000000 | tf_op jit(solution)/shard_map/pool_rows/pallas_call | solution.py:419
  33.8 0.6 %collective-permute-done.2.up_ref = bf16[272,128]{1,0:T(8,128)(2,1)S(1)} collective-permute-done((bf16[272,128]{1,0:T(8,128)(2,1)S(1)}, bf16[272,128]{1,0:T(8,128)(2,1)S(1)}, u32[]{:S(2)}, u32[]{:S(2)}) %collective-permute-start.2) | collective-permute-done | bytes 69664 | tf_op jit(solution)/shard_map/ppermute | solution.py:620
  34.5 0.0 collective-permute-done.3.down_ref
  34.5 0.1 relay_rows.1
  34.5 1.4 %collective-permute-start.4 = (bf16[272,256]{1,0:T(8,128)(2,1)S(1)}, bf16[272,256]{1,0:T(8,128)(2,1)S(1)}, u32[]{:S(2)}, u32[]{:S(2)}) collective-permute-start(bf16[272,256]{1,0:T(8,128)(2,1)S(1)} %get-tuple-element.45), channel_id=1, source_target_pairs={{0,64},{64,128},{128,192},{192,0},{1,65},{65,129},{129,193},{193,1... | collective-permute-start | bytes 417800 | tf_op jit(solution)/shard_map/ppermute | solution.py:624
  35.9 1.5 %collective-permute-start.5 = (bf16[272,256]{1,0:T(8,128)(2,1)S(1)}, bf16[272,256]{1,0:T(8,128)(2,1)S(1)}, u32[]{:S(2)}, u32[]{:S(2)}) collective-permute-start(bf16[272,256]{1,0:T(8,128)(2,1)S(1)} %get-tuple-element.46), channel_id=1, source_target_pairs={{64,0},{128,64},{192,128},{0,192},{65,1},{129,65},{193,129},{1,193... | collective-permute-start | bytes 417800 | tf_op jit(solution)/shard_map/ppermute | solution.py:625
  37.4 0.0 copy-done.11
  37.5 0.1 copy.24.list_ref
  37.6 3.9 %collective-permute-done.4.below_ref = bf16[272,256]{1,0:T(8,128)(2,1)S(1)} collective-permute-done((bf16[272,256]{1,0:T(8,128)(2,1)S(1)}, bf16[272,256]{1,0:T(8,128)(2,1)S(1)}, u32[]{:S(2)}, u32[]{:S(2)}) %collective-permute-start.4) | collective-permute-done | bytes 139296 | tf_op jit(solution)/shard_map/ppermute | solution.py:624
  41.5 0.0 collective-permute-done.5.above_ref
  41.5 0.0 copy-done
  41.5 0.0 copy-done.6
  41.5 0.6 %cluster_level.1 = (bf16[256,256]{1,0:T(8,128)(2,1)S(1)}, bf16[256,256]{1,0:T(8,128)(2,1)S(1)}, bf16[128,256]{1,0:T(8,128)(2,1)S(1)}, bf16[128,256]{1,0:T(8,128)(2,1)S(1)}) custom-call(bf16[272,256]{1,0:T(8,128)(2,1)S(1)} %get-tuple-element.40.mine_ref, bf16[272,256]{1,0:T(8,128)(2,1)S(1)} %collective-permute-done.4.below_ref, ...), custom_call_target="tpu_custom_call" | custom-call | flops 70000000 | bytes 1000000 | tf_op jit(solution)/shard_map/cluster_level/pallas_call | solution.py:477
  42.1 0.6 %collective-permute-start.6 = (bf16[128,256]{1,0:T(8,128)(2,1)S(1)}, bf16[128,256]{1,0:T(8,128)(2,1)S(1)}, u32[]{:S(2)}, u32[]{:S(2)}) collective-permute-start(bf16[128,256]{1,0:T(8,128)(2,1)S(1)} %get-tuple-element.52), channel_id=1, source_target_pairs={{0,1},{1,0},{2,3},{3,2},{4,5},{5,4},{6,7},{7,6},{8,9},{9,8},{10,11... | collective-permute-start | bytes 196616 | tf_op jit(solution)/shard_map/ppermute | solution.py:633
  42.7 5.0 %collective-permute-start.7 = (bf16[128,256]{1,0:T(8,128)(2,1)S(1)}, bf16[128,256]{1,0:T(8,128)(2,1)S(1)}, u32[]{:S(2)}, u32[]{:S(2)}) collective-permute-start(bf16[128,256]{1,0:T(8,128)(2,1)S(1)} %get-tuple-element.53), channel_id=1, source_target_pairs={{1,2},{2,1},{3,4},{4,3},{5,6},{6,5},{7,8},{8,7},{9,10},{10,9},{11,... | collective-permute-start | bytes 196616 | tf_op jit(solution)/shard_map/ppermute | solution.py:632
  47.7 0.0 copy-done.12
  47.7 0.2 copy.26.send_ref
  47.9 0.0 copy-done.1
  48.0 0.0 copy-done.2
  48.0 0.0 copy-done.4
  48.0 0.0 copy-done.5
  48.0 0.8 %coarse_edge_terms.1 = (f32[1024,256]{1,0:T(8,128)S(1)}, f32[256,256]{1,0:T(8,128)S(1)}, bf16[2,256,256]{2,1,0:T(8,128)(2,1)S(1)}) custom-call(s32[1024,1]{1,0:T(8,128)S(1)} %copy.26.send_ref, bf16[1024,256]{1,0:T(8,128)(2,1)S(1)} %copy-done.2, bf16[256,256]{1,0:T(8,128)(2,1)S(1)} %get-tuple-element.47.node_ref, ...), custom_call_target="tpu_custom_call" | custom-call | flops 500000000 | bytes 3000000 | tf_op jit(solution)/shard_map/coarse_edge_terms/pallas_call | solution.py:506
  48.8 0.0 collective-permute-done.6.low_ref
  48.8 2.8 %collective-permute-done.7.high_ref = bf16[128,256]{1,0:T(8,128)(2,1)S(1)} collective-permute-done((bf16[128,256]{1,0:T(8,128)(2,1)S(1)}, bf16[128,256]{1,0:T(8,128)(2,1)S(1)}, u32[]{:S(2)}, u32[]{:S(2)}) %collective-permute-start.7) | collective-permute-done | bytes 65568 | tf_op jit(solution)/shard_map/ppermute | solution.py:632
  51.6 1.8 %coarse_level.1 = bf16[256,256]{1,0:T(8,128)(2,1)} custom-call(s32[1024,1]{1,0:T(8,128)S(1)} %copy.26.send_ref, f32[1024,256]{1,0:T(8,128)S(1)} %get-tuple-element.49.pre_ref, f32[256,256]{1,0:T(8,128)S(1)} %get-tuple-element.50.own_ref, bf16[2,256,256]{2,1,0:T(8,128)(2,1)S(1)} %get-tuple-element.51.w_ref, bf16[256,256]{1,0:T(8,128)(2,1)S(1)} %get-tuple-element.47.node_ref, ...), custom_call_target="tpu_custom_call" | custom-call | flops 500000000 | bytes 3000000 | tf_op jit(solution)/shard_map/coarse_level/pallas_call | solution.py:541
  (8 shorter events, 0.0 us)
Async XLA Ops:
  4.0 13.5 %collective-permute-start = (bf16[512,256]{1,0:T(8,128)(2,1)S(1)}, bf16[512,256]{1,0:T(8,128)(2,1)S(1)}, u32[]{:S(2)}, u32[]{:S(2)}) collective-permute-start(bf16[512,256]{1,0:T(8,128)(2,1)S(1)} %own_rows.1), channel_id=1, source_target_pairs={{0,1},{1,0},{2,3},{3,2},{4,5},{5,4},{6,7},{7,6},{8,9},{9,8},{10,11... | collective-permute-start | bytes 786440 | tf_op jit(solution)/shard_map/ppermute | solution.py:600
  4.8 12.7 %collective-permute-start.1 = (bf16[512,256]{1,0:T(8,128)(2,1)S(1)}, bf16[512,256]{1,0:T(8,128)(2,1)S(1)}, u32[]{:S(2)}, u32[]{:S(2)}) collective-permute-start(bf16[512,256]{1,0:T(8,128)(2,1)S(1)} %get-tuple-element.37), channel_id=1, source_target_pairs={{1,2},{2,1},{3,4},{4,3},{5,6},{6,5},{7,8},{8,7},{9,10},{10,9},{11,... | collective-permute-start | bytes 786440 | tf_op jit(solution)/shard_map/ppermute | solution.py:598
  10.1 7.4 %copy-start.3 = (bf16[2,256,256]{2,1,0:T(8,128)(2,1)S(1)}, bf16[2,256,256]{2,1,0:T(8,128)(2,1)}, u32[]{:S(2)}) copy-start(bf16[2,256,256]{2,1,0:T(8,128)(2,1)} %node_in.3) | copy-start | bytes 786436
  10.1 7.4 %copy-start.8 = (f32[4,256]{1,0:T(4,128)S(1)}, f32[4,256]{1,0:T(4,128)}, u32[]{:S(2)}) copy-start(f32[4,256]{1,0:T(4,128)} %bias.3) | copy-start | bytes 12292
  10.1 7.4 %copy-start.9 = (f32[2,256]{1,0:T(2,128)S(1)}, f32[2,256]{1,0:T(2,128)}, u32[]{:S(2)}) copy-start(f32[2,256]{1,0:T(2,128)} %gain.2) | copy-start | bytes 6148
  29.8 7.6 %copy-start.11 = (s32[256]{0:T(256)S(1)}, s32[256]{0:T(256)}, u32[]{:S(2)}) copy-start(s32[256]{0:T(256)} %param.29) | copy-start | bytes 3076
  29.9 11.7 %copy-start = (bf16[3,256,256]{2,1,0:T(8,128)(2,1)S(1)}, bf16[3,256,256]{2,1,0:T(8,128)(2,1)}, u32[]{:S(2)}) copy-start(bf16[3,256,256]{2,1,0:T(8,128)(2,1)} %edge_in.1) | copy-start | bytes 1179652
  29.9 11.7 %copy-start.6 = (bf16[256,256]{1,0:T(8,128)(2,1)S(1)}, bf16[256,256]{1,0:T(8,128)(2,1)}, u32[]{:S(2)}) copy-start(bf16[256,256]{1,0:T(8,128)(2,1)} %lat_ref.1) | copy-start | bytes 393220
  29.9 17.8 %copy-start.12 = (s32[1024]{0:T(1024)S(1)}, s32[1024]{0:T(1024)}, u32[]{:S(2)}) copy-start(s32[1024]{0:T(1024)} %param.28) | copy-start | bytes 12292
  29.9 18.1 %copy-start.1 = (bf16[2,256,256]{2,1,0:T(8,128)(2,1)S(1)}, bf16[2,256,256]{2,1,0:T(8,128)(2,1)}, u32[]{:S(2)}) copy-start(bf16[2,256,256]{2,1,0:T(8,128)(2,1)} %node_in.5) | copy-start | bytes 786436
  29.9 18.1 %copy-start.2 = (bf16[1024,256]{1,0:T(8,128)(2,1)S(1)}, bf16[1024,256]{1,0:T(8,128)(2,1)}, u32[]{:S(2)}) copy-start(bf16[1024,256]{1,0:T(8,128)(2,1)} %edge_ref.1) | copy-start | bytes 1572868
  29.9 18.1 %copy-start.4 = (bf16[256,256]{1,0:T(8,128)(2,1)S(1)}, bf16[256,256]{1,0:T(8,128)(2,1)}, u32[]{:S(2)}) copy-start(bf16[256,256]{1,0:T(8,128)(2,1)} %edge_out.1) | copy-start | bytes 393220
  29.9 18.0 %copy-start.5 = (bf16[256,256]{1,0:T(8,128)(2,1)S(1)}, bf16[256,256]{1,0:T(8,128)(2,1)}, u32[]{:S(2)}) copy-start(bf16[256,256]{1,0:T(8,128)(2,1)} %node_out.1) | copy-start | bytes 393220
  29.9 18.0 %copy-start.7 = (f32[4,256]{1,0:T(4,128)S(1)}, f32[4,256]{1,0:T(4,128)}, u32[]{:S(2)}) copy-start(f32[4,256]{1,0:T(4,128)} %bias.5) | copy-start | bytes 12292
  30.0 4.5 %collective-permute-start.2 = (bf16[272,128]{1,0:T(8,128)(2,1)S(1)}, bf16[272,128]{1,0:T(8,128)(2,1)S(1)}, u32[]{:S(2)}, u32[]{:S(2)}) collective-permute-start(bf16[272,128]{1,0:T(8,128)(2,1)S(1)} %get-tuple-element.43), channel_id=1, source_target_pairs={{0,64},{64,128},{128,192},{192,0},{1,65},{65,129},{129,193},{193,1... | collective-permute-start | bytes 208904 | tf_op jit(solution)/shard_map/ppermute | solution.py:620
  31.3 3.2 %collective-permute-start.3 = (bf16[272,128]{1,0:T(8,128)(2,1)S(1)}, bf16[272,128]{1,0:T(8,128)(2,1)S(1)}, u32[]{:S(2)}, u32[]{:S(2)}) collective-permute-start(bf16[272,128]{1,0:T(8,128)(2,1)S(1)} %get-tuple-element.44), channel_id=1, source_target_pairs={{64,0},{128,64},{192,128},{0,192},{65,1},{129,65},{193,129},{1,193... | collective-permute-start | bytes 208904 | tf_op jit(solution)/shard_map/ppermute | solution.py:621
  32.8 18.8 %copy-start.10 = (f32[2,256]{1,0:T(2,128)S(1)}, f32[2,256]{1,0:T(2,128)}, u32[]{:S(2)}) copy-start(f32[2,256]{1,0:T(2,128)} %gain.3) | copy-start | bytes 6148
  34.5 7.0 %collective-permute-start.4 = (bf16[272,256]{1,0:T(8,128)(2,1)S(1)}, bf16[272,256]{1,0:T(8,128)(2,1)S(1)}, u32[]{:S(2)}, u32[]{:S(2)}) collective-permute-start(bf16[272,256]{1,0:T(8,128)(2,1)S(1)} %get-tuple-element.45), channel_id=1, source_target_pairs={{0,64},{64,128},{128,192},{192,0},{1,65},{65,129},{129,193},{193,1... | collective-permute-start | bytes 417800 | tf_op jit(solution)/shard_map/ppermute | solution.py:624
  35.9 5.6 %collective-permute-start.5 = (bf16[272,256]{1,0:T(8,128)(2,1)S(1)}, bf16[272,256]{1,0:T(8,128)(2,1)S(1)}, u32[]{:S(2)}, u32[]{:S(2)}) collective-permute-start(bf16[272,256]{1,0:T(8,128)(2,1)S(1)} %get-tuple-element.46), channel_id=1, source_target_pairs={{64,0},{128,64},{192,128},{0,192},{65,1},{129,65},{193,129},{1,193... | collective-permute-start | bytes 417800 | tf_op jit(solution)/shard_map/ppermute | solution.py:625
  42.1 6.7 %collective-permute-start.6 = (bf16[128,256]{1,0:T(8,128)(2,1)S(1)}, bf16[128,256]{1,0:T(8,128)(2,1)S(1)}, u32[]{:S(2)}, u32[]{:S(2)}) collective-permute-start(bf16[128,256]{1,0:T(8,128)(2,1)S(1)} %get-tuple-element.52), channel_id=1, source_target_pairs={{0,1},{1,0},{2,3},{3,2},{4,5},{5,4},{6,7},{7,6},{8,9},{9,8},{10,11... | collective-permute-start | bytes 196616 | tf_op jit(solution)/shard_map/ppermute | solution.py:633
  42.7 8.9 %collective-permute-start.7 = (bf16[128,256]{1,0:T(8,128)(2,1)S(1)}, bf16[128,256]{1,0:T(8,128)(2,1)S(1)}, u32[]{:S(2)}, u32[]{:S(2)}) collective-permute-start(bf16[128,256]{1,0:T(8,128)(2,1)S(1)} %get-tuple-element.53), channel_id=1, source_target_pairs={{1,2},{2,1},{3,4},{4,3},{5,6},{6,5},{7,8},{8,7},{9,10},{10,9},{11,... | collective-permute-start | bytes 196616 | tf_op jit(solution)/shard_map/ppermute | solution.py:632

commit v4 on v3

--- a/solution.py
+++ b/solution.py
@@ -9,9 +9,10 @@
 F32 = jnp.float32
 BF16 = jnp.bfloat16
 CHUNK = 1024
-GATHER = 1024
+GATHER = 2048
 TILE = 256
 DEG = 4
+PIECE = 512
 
 VMEM_SPEC = pl.BlockSpec(memory_space=pltpu.VMEM)
 HBM_SPEC = pl.BlockSpec(memory_space=pltpu.HBM)
@@ -140,6 +141,29 @@
         name="own_rows",
         compiler_params=limit(8),
     )(hbm(lists), nodes, edge_in)
+
+
+def membership(pool, step, member_ref, k, count_ref, at):
+    nodes = pool.shape[1]
+    owner = lax.rem(lax.axis_index("group") + step, lax.axis_size("group"))
+    row = lax.broadcasted_iota(jnp.int32, (256, 128), 0).astype(F32).astype(BF16)
+    lane = lax.broadcasted_iota(jnp.int32, (256, 128), 1)
+    one = jnp.ones((256, 128), BF16)
+    zero = jnp.zeros((256, 128), BF16)
+    local = pool[...] - owner * 256
+    inside = jnp.logical_and(local >= 0, local < 256)
+    local = jnp.where(inside, local, 256).astype(F32).astype(BF16)
+    total = zero
+    for i in range(0, nodes, 128):
+        here = jnp.broadcast_to(local[:, i : i + 128], (256, 128))
+        member = jnp.where(row == here, one, zero)
+        member_ref[k, :, i : i + 128] = member
+        total = total + member
+    count = jnp.sum(total.astype(F32), axis=1, keepdims=True)
+    high = jnp.floor(count * (1.0 / 64.0))
+    low = count - high * 64.0
+    both = jnp.where(lane == 0, low, jnp.where(lane == 1, high, 0.0))
+    count_ref[at] = both.T[:16, :].astype(BF16)
 
 
 def edges_kernel(
@@ -168,6 +192,8 @@
     edges,
     rep0,
     rep1,
+    rep2,
+    rep3,
     small_sem,
     edge_sem,
 ):
@@ -201,47 +227,36 @@
     small[0].wait()
     small[1].wait()
 
-    me = lax.axis_index("group")
-    owners = member_ref.shape[0]
-    ids = pool[...]
-    row = lax.broadcasted_iota(jnp.int32, (256, 128), 0).astype(F32).astype(BF16)
-    lane = lax.broadcasted_iota(jnp.int32, (256, 128), 1)
-    one = jnp.ones((256, 128), BF16)
-    zero = jnp.zeros((256, 128), BF16)
-    for k, step in enumerate((2, 1, 3, 0)):
-        base = lax.rem(me + step, owners) * 256
-        local = ids - base
-        inside = jnp.logical_and(local >= 0, local < 256)
-        local = jnp.where(inside, local, 256).astype(F32).astype(BF16)
-        total = zero
-        for i in range(0, nodes, 128):
-            here = jnp.broadcast_to(local[:, i : i + 128], (256, 128))
-            member = jnp.where(row == here, one, zero)
-            member_ref[k, :, i : i + 128] = member
-            total = total + member
-        count = jnp.sum(total.astype(F32), axis=1, keepdims=True)
-        high = jnp.floor(count * (1.0 / 64.0))
-        low = count - high * 64.0
-        both = jnp.where(lane == 0, low, jnp.where(lane == 1, high, 0.0))
-        count_ref[k] = both.T[:16, :].astype(BF16)
-
+    membership(pool, 2, member_ref, 0, count_ref, 0)
     b_edge = bias[0:1, :]
     b_node = bias[2:3, :]
 
-    def edge_chunk(c, carry):
+    reps = ((rep0, rep1), (rep2, rep3))
+
+    def spread(c, pair):
+        c = jnp.minimum(c, chunks - 1)
         own = node[pl.ds(pl.multiple_of(c * cnodes, cnodes), cnodes), :]
         receiver = dot(own, edge_in[1]) + b_edge
-        for j in range(DEG):
-            rep0[pl.ds(j, cnodes, stride=DEG), :] = receiver[:, :128]
-            rep1[pl.ds(j, cnodes, stride=DEG), :] = receiver[:, 128:]
-        at = pl.ds(pl.multiple_of(c * CHUNK, CHUNK), CHUNK)
-        pltpu.make_async_copy(edge_hbm.at[at, :], edges.at[at, :], edge_sem.at[c]).wait()
-        pre_ref[at, :] = dot(edges[at, :], edge_in[2]) + jnp.concatenate(
-            [rep0[...], rep1[...]], axis=1
-        )
+        for half, rep in enumerate(pair):
+            for j in range(DEG):
+                rep[pl.ds(j, cnodes, stride=DEG), :] = receiver[:, 128 * half : 128 * half + 128]
+
+    spread(0, reps[0])
+
+    def edge_pair(k, carry):
+        for slot in range(2):
+            c = 2 * k + slot
+            at = pl.ds(pl.multiple_of(c * CHUNK, CHUNK), CHUNK)
+            pltpu.make_async_copy(edge_hbm.at[at, :], edges.at[at, :], edge_sem.at[c]).wait()
+            spread(c + 1, reps[1 - slot])
+            here = reps[slot]
+            for i in range(0, CHUNK, PIECE):
+                at = pl.ds(pl.multiple_of(c * CHUNK + i, PIECE), PIECE)
+                near = [rep[i : i + PIECE, :] for rep in here]
+                pre_ref[at, :] = dot(edges[at, :], edge_in[2]) + jnp.concatenate(near, axis=1)
         return carry
 
-    lax.fori_loop(0, chunks, edge_chunk, 0, unroll=2)
+    lax.fori_loop(0, chunks // 2, edge_pair, 0)
 
     for c in small[2:]:
         c.wait()
@@ -260,7 +275,7 @@
         own_ref[i : i + CHUNK, :] = dot(own, node_in[0]) + b_node
 
 
-def edge_terms(send, pool, edges, nodes, rim, owners, edge_in, edge_out, node_in, node_out, bias):
+def edge_terms(send, pool, edges, nodes, rim, edge_in, edge_out, node_in, node_out, bias):
     n = nodes.shape[0]
     e = edges.shape[0]
     shape = jax.ShapeDtypeStruct
@@ -272,14 +287,16 @@
             shape((n, 256), F32),
             shape(send.shape, jnp.int32),
             shape((2, 256, 256), BF16),
-            shape((owners, 256, n), BF16),
-            shape((owners, 16, 256), BF16),
+            shape((1, 256, n), BF16),
+            shape((1, 16, 256), BF16),
             shape((2 * (n + 2 * rim), 128), F32),
         ),
         in_specs=[VMEM_SPEC] * 2 + [HBM_SPEC] * len(operands),
         out_specs=(VMEM_SPEC,) * 7,
         scratch_shapes=[pltpu.VMEM(x.shape, x.dtype) for x in operands]
         + [
+            pltpu.VMEM((CHUNK, 128), F32),
+            pltpu.VMEM((CHUNK, 128), F32),
             pltpu.VMEM((CHUNK, 128), F32),
             pltpu.VMEM((CHUNK, 128), F32),
             pltpu.SemaphoreType.DMA((6,)),
@@ -403,28 +420,33 @@
         input_output_aliases={3: 4},
         cost_estimate=pl.CostEstimate(flops=4_000_000_000, bytes_accessed=8_000_000, transcendentals=0),
         name="fine_level",
-        compiler_params=limit(14),
+        compiler_params=pltpu.CompilerParams(vmem_limit_bytes=14 * 1024 * 1024),
     )(row, pre, own, table, w, member, count, low, high, nodes, node_in, bias, gain)
     return outs[:4]
 
 
-def pool_kernel(member_ref, count_ref, out_ref, next_ref, prev_ref, mine_ref):
-    for k, ref in enumerate((next_ref, prev_ref, mine_ref)):
-        ref[:256, :] = dot(member_ref[k + 1], out_ref[...]).astype(BF16)
-        ref[256:, :] = count_ref[k + 1]
-
-
-def pool_rows(member, count, out):
+def pool_kernel(pool, out_ref, next_ref, prev_ref, mine_ref, member, count):
+    for k, (step, ref) in enumerate(((1, next_ref), (3, prev_ref), (0, mine_ref))):
+        membership(pool, step, member, k, count, k)
+        ref[:256, :] = dot(member[k], out_ref[...]).astype(BF16)
+        ref[256:, :] = count[k]
+
+
+def pool_rows(pool, out):
     shape = jax.ShapeDtypeStruct((272, 256), BF16)
     return pl.pallas_call(
         pool_kernel,
         out_shape=(shape,) * 3,
-        in_specs=[VMEM_SPEC] * 3,
+        in_specs=[VMEM_SPEC] * 2,
         out_specs=(VMEM_SPEC,) * 3,
+        scratch_shapes=[
+            pltpu.VMEM((3, 256, out.shape[0]), BF16),
+            pltpu.VMEM((3, 16, 256), BF16),
+        ],
         cost_estimate=pl.CostEstimate(flops=800_000_000, bytes_accessed=4_000_000, transcendentals=0),
         name="pool_rows",
-        compiler_params=limit(8),
-    )(member, count, out)
+        compiler_params=limit(10),
+    )(pool, out)
 
 
 def relay_kernel(next_ref, prev_ref, up_ref, down_ref, next_out, prev_out):
@@ -465,9 +487,11 @@
     in_ref[...] = coarse_in
     proj = dot(coarse_in, w_ref[0]).astype(BF16)
     proj_ref[...] = proj
-    border = dot(one_hot_rows(list_ref[...], clusters), proj).astype(BF16)
-    a_ref[...] = border[:rim, :]
-    b_ref[...] = border[rim:, :]
+    border = dot(one_hot_rows(list_ref[...], clusters), proj)
+    low, high = border[:rim, :], border[rim:, :]
+    odd = lax.rem(lax.axis_index("dom"), 2) == 1
+    a_ref[...] = jnp.where(odd, low, high).astype(BF16)
+    b_ref[...] = jnp.where(odd, high, low).astype(BF16)
 
 
 def cluster_level(mine, below, above, lat, lists, edge_in):
@@ -605,7 +629,6 @@
         edge_lat,
         node_near,
         rim,
-        groups,
         edge_in_near,
         fine_edge_out,
         fine_node_in,
@@ -619,15 +642,14 @@
     back = [(target, source) for source, target in onward]
     far_up = lax.ppermute(far_up, "group", onward)
     far_down = lax.ppermute(far_down, "group", back)
-    next_rows, prev_rows, mine = pool_rows(terms[4], terms[5], fine_near)
+    next_rows, prev_rows, mine = pool_rows(pool_id.reshape(1, -1), fine_near)
     next_rows, prev_rows = relay_rows(next_rows, prev_rows, far_up, far_down)
     below = lax.ppermute(next_rows, "group", onward)
     above = lax.ppermute(prev_rows, "group", back)
     crim = chalo_list.shape[0] // 2
     clusters = coarse_lat.shape[0]
-    lists = jnp.where(odd == 1, chalo_list, jnp.roll(chalo_list, crim))
     coarse_in, coarse_proj, cborder_a, cborder_b = cluster_level(
-        mine, below, above, coarse_lat, lists.reshape(-1, 1), coarse_edge_in
+        mine, below, above, coarse_lat, chalo_list.reshape(-1, 1), coarse_edge_in
     )
     crim_b = lax.ppermute(cborder_b, "dom", outer)
     crim_a = lax.ppermute(cborder_a, "dom", inner)

time: 53.6 us -> 50.7 us (0.946)
  the two profiles are of different devices: /device:TPU:103 before, /device:TPU:128 now
where the time goes in v4:
time: 50.7 us; the launch traced here: 50.5 us
  Pallas kernels  24.5 us (48%)
  starting transfers between devices  13.8 us (27%)
  waiting for transfers between devices  10.9 us (21%)
  between operations  0.92 us (2%)
    pallas_call x1, Pallas kernels, fine_level(): pl.pallas_call(fine_kernel, out_shape=(shape((n, 256), BF16), shape((n, 2...  11.1 us
    pallas_call x1, Pallas kernels, edge_terms(): pl.pallas_call(edges_kernel, out_shape=(shape((e, 256), F32), shape((n, 2...  5.43 us
    ppermute x1, waiting for transfers between devices, body(): crim_b = lax.ppermute(cborder_b, 'dom', outer)  5.12 us
    ppermute x1, starting transfers between devices, body(): rim_b = lax.ppermute(border_b, 'dom', outer)  4.31 us
    ppermute x1, waiting for transfers between devices, body(): below = lax.ppermute(next_rows, 'group', onward)  2.89 us
    ppermute x1, starting transfers between devices, body(): crim_b = lax.ppermute(cborder_b, 'dom', outer)  2.64 us
    pallas_call x1, Pallas kernels, border_rows(): pl.pallas_call(border_kernel, out_shape=(shape((rim, 256), BF16), shape(n...  2.03 us
    pallas_call x1, Pallas kernels, coarse_level(): pl.pallas_call(coarse_kernel, out_shape=jax.ShapeDtypeStruct(nodes.shape,...  1.8 us
  transfers between devices with their start and end apart: 8, of which 6 were waited for; matrix products, arithmetic and copies ran while one was open for 1% of the time, Pallas kernels for 15%

profile of v4, /device:TPU:128, one launch (start us, length us, event | category | flops | bytes accessed | tf_op | source)
XLA Modules:
  0.0 50.5 jit_solution(5458110043029680342)
XLA Ops:
  0.6 2.0 %border_rows.1 = (bf16[512,256]{1,0:T(8,128)(2,1)S(1)}, bf16[2048,256]{1,0:T(8,128)(2,1)S(1)}, bf16[3,256,256]{2,1,0:T(8,128)(2,1)S(1)}) custom-call(s32[1024]{0:T(1024)} %list_ref.3, bf16[2048,256]{1,0:T(8,128)(2,1)} %node_ref.1, bf16[3,256,256]{2,1,0:T(8,128)(2,1)} %w_ref.2), custom_call_target="tpu_custom_call" | custom-call | flops 70000000 | bytes 2000000 | tf_op jit(solution)/shard_map/border_rows/pallas_call | solution.py:93
  2.7 1.3 %own_rows.1 = bf16[512,256]{1,0:T(8,128)(2,1)S(1)} custom-call(s32[1024]{0:T(1024)} %list_ref.3, bf16[2048,256]{1,0:T(8,128)(2,1)S(1)} %get-tuple-element.28.node.node_ref, bf16[3,256,256]{2,1,0:T(8,128)(2,1)S(1)} %get-tuple-element.29.edge_in.w_ref), custom_call_target="tpu_custom_call" | custom-call | flops 70000000 | bytes 2000000 | tf_op jit(solution)/shard_map/own_rows/pallas_call | solution.py:129
  4.0 0.1 collective-permute-start
  4.1 4.3 %collective-permute-start.1 = (bf16[512,256]{1,0:T(8,128)(2,1)S(1)}, bf16[512,256]{1,0:T(8,128)(2,1)S(1)}, u32[]{:S(2)}, u32[]{:S(2)}) collective-permute-start(bf16[512,256]{1,0:T(8,128)(2,1)S(1)} %get-tuple-element.37), channel_id=1, source_target_pairs={{1,2},{2,1},{3,4},{4,3},{5,6},{6,5},{7,8},{8,7},{9,10},{10,9},{11,... | collective-permute-start | bytes 786440 | tf_op jit(solution)/shard_map/ppermute | solution.py:622
  8.4 0.0 copy-start.3
  8.4 0.0 copy-start.8
  8.4 0.0 copy-start.9
  8.5 5.4 %edge_terms.1 = (f32[8192,256]{1,0:T(8,128)S(1)}, f32[2048,256]{1,0:T(8,128)S(1)}, s32[64,128]{1,0:T(8,128)S(1)}, bf16[2,256,256]{2,1,0:T(8,128)(2,1)S(1)}, bf16...) custom-call(bf16[2048,256]{1,0:T(8,128)(2,1)S(1)} %get-tuple-element.28.node.node_ref, ...), custom_call_target="tpu_custom_call" | custom-call | flops 3000000000 | bytes 8000000 | tf_op jit(solution)/shard_map/edge_terms/pallas_call | solution.py:283
  13.9 0.0 collective-permute-done.low_ref
  13.9 1.2 %collective-permute-done.1.high_ref = bf16[512,256]{1,0:T(8,128)(2,1)S(1)} collective-permute-done((bf16[512,256]{1,0:T(8,128)(2,1)S(1)}, bf16[512,256]{1,0:T(8,128)(2,1)S(1)}, u32[]{:S(2)}, u32[]{:S(2)}) %collective-permute-start.1) | collective-permute-done | bytes 262176 | tf_op jit(solution)/shard_map/ppermute | solution.py:622
  15.1 0.0 copy-done.3
  15.1 0.0 copy-done.8
  15.1 0.0 copy-done.9
  15.1 0.0 copy-start.11
  15.1 11.1 %fine_level.1 = (bf16[2048,256]{1,0:T(8,128)(2,1)}, bf16[2048,256]{1,0:T(8,128)(2,1)S(1)}, bf16[272,128]{1,0:T(8,128)(2,1)S(1)}, bf16[272,128]{1,0:T(8,128)(2,1)S(1)}, f32[6144,128]{1,0:T(8,128)S(1)}) custom-call(s32[64,128]{1,0:T(8,128)S(1)} %get-tuple-element.30.row_ref, ...), custom_call_target="tpu_custom_call", output_to_operand_aliasing={{4}: (3, {})} | custom-call | flops 4000000000 | bytes 8000000 | tf_op jit(solution)/shard_map/fine_level/pallas_call | solution.py:401
  26.3 0.0 copy-start.13
  26.3 0.0 copy-start
  26.3 0.0 copy-start.6
  26.3 0.0 copy-start.12
  26.3 0.0 copy-start.1
  26.3 0.0 copy-start.2
  26.4 0.0 copy-start.4
  26.4 0.0 copy-start.5
  26.4 0.0 copy-start.7
  26.4 1.7 %collective-permute-start.2 = (bf16[272,128]{1,0:T(8,128)(2,1)S(1)}, bf16[272,128]{1,0:T(8,128)(2,1)S(1)}, u32[]{:S(2)}, u32[]{:S(2)}) collective-permute-start(bf16[272,128]{1,0:T(8,128)(2,1)S(1)} %get-tuple-element.43), channel_id=1, source_target_pairs={{0,64},{64,128},{128,192},{192,0},{1,65},{65,129},{129,193},{193,1... | collective-permute-start | bytes 208904 | tf_op jit(solution)/shard_map/ppermute | solution.py:643
  28.0 1.7 %collective-permute-start.3 = (bf16[272,128]{1,0:T(8,128)(2,1)S(1)}, bf16[272,128]{1,0:T(8,128)(2,1)S(1)}, u32[]{:S(2)}, u32[]{:S(2)}) collective-permute-start(bf16[272,128]{1,0:T(8,128)(2,1)S(1)} %get-tuple-element.44), channel_id=1, source_target_pairs={{64,0},{128,64},{192,128},{0,192},{65,1},{129,65},{193,129},{1,193... | collective-permute-start | bytes 208904 | tf_op jit(solution)/shard_map/ppermute | solution.py:644
  29.7 0.0 copy-done.11
  29.7 1.3 %pool_rows.1 = (bf16[272,256]{1,0:T(8,128)(2,1)S(1)}, bf16[272,256]{1,0:T(8,128)(2,1)S(1)}, bf16[272,256]{1,0:T(8,128)(2,1)S(1)}) custom-call(s32[1,2048]{1,0:T(1,128)S(1)} %bitcast.5, bf16[2048,256]{1,0:T(8,128)(2,1)S(1)} %get-tuple-element.39.out_ref), custom_call_target="tpu_custom_call" | custom-call | flops 800000000 | bytes 4000000 | tf_op jit(solution)/shard_map/pool_rows/pallas_call | solution.py:437
  31.0 1.0 %collective-permute-done.2.up_ref = bf16[272,128]{1,0:T(8,128)(2,1)S(1)} collective-permute-done((bf16[272,128]{1,0:T(8,128)(2,1)S(1)}, bf16[272,128]{1,0:T(8,128)(2,1)S(1)}, u32[]{:S(2)}, u32[]{:S(2)}) %collective-permute-start.2) | collective-permute-done | bytes 69664 | tf_op jit(solution)/shard_map/ppermute | solution.py:643
  32.0 0.4 collective-permute-done.3.down_ref
  32.4 0.1 relay_rows.1
  32.4 1.7 %collective-permute-start.4 = (bf16[272,256]{1,0:T(8,128)(2,1)S(1)}, bf16[272,256]{1,0:T(8,128)(2,1)S(1)}, u32[]{:S(2)}, u32[]{:S(2)}) collective-permute-start(bf16[272,256]{1,0:T(8,128)(2,1)S(1)} %get-tuple-element.45), channel_id=1, source_target_pairs={{0,64},{64,128},{128,192},{192,0},{1,65},{65,129},{129,193},{193,1... | collective-permute-start | bytes 417800 | tf_op jit(solution)/shard_map/ppermute | solution.py:647
  34.1 1.7 %collective-permute-start.5 = (bf16[272,256]{1,0:T(8,128)(2,1)S(1)}, bf16[272,256]{1,0:T(8,128)(2,1)S(1)}, u32[]{:S(2)}, u32[]{:S(2)}) collective-permute-start(bf16[272,256]{1,0:T(8,128)(2,1)S(1)} %get-tuple-element.46), channel_id=1, source_target_pairs={{64,0},{128,64},{192,128},{0,192},{65,1},{129,65},{193,129},{1,193... | collective-permute-start | bytes 417800 | tf_op jit(solution)/shard_map/ppermute | solution.py:648
  35.7 0.0 copy-done.13
  35.7 0.1 copy.24.list_ref
  35.9 2.9 %collective-permute-done.4.below_ref = bf16[272,256]{1,0:T(8,128)(2,1)S(1)} collective-permute-done((bf16[272,256]{1,0:T(8,128)(2,1)S(1)}, bf16[272,256]{1,0:T(8,128)(2,1)S(1)}, u32[]{:S(2)}, u32[]{:S(2)}) %collective-permute-start.4) | collective-permute-done | bytes 139296 | tf_op jit(solution)/shard_map/ppermute | solution.py:647
  38.8 0.4 collective-permute-done.5.above_ref
  39.1 0.0 copy-done
  39.1 0.0 copy-done.6
  39.1 0.6 %cluster_level.1 = (bf16[256,256]{1,0:T(8,128)(2,1)S(1)}, bf16[256,256]{1,0:T(8,128)(2,1)S(1)}, bf16[128,256]{1,0:T(8,128)(2,1)S(1)}, bf16[128,256]{1,0:T(8,128)(2,1)S(1)}) custom-call(bf16[272,256]{1,0:T(8,128)(2,1)S(1)} %get-tuple-element.40.mine_ref, bf16[272,256]{1,0:T(8,128)(2,1)S(1)} %collective-permute-done.4.below_ref, ...), custom_call_target="tpu_custom_call" | custom-call | flops 70000000 | bytes 1000000 | tf_op jit(solution)/shard_map/cluster_level/pallas_call | solution.py:501
  39.7 0.1 collective-permute-start.6
  39.8 2.6 %collective-permute-start.7 = (bf16[128,256]{1,0:T(8,128)(2,1)S(1)}, bf16[128,256]{1,0:T(8,128)(2,1)S(1)}, u32[]{:S(2)}, u32[]{:S(2)}) collective-permute-start(bf16[128,256]{1,0:T(8,128)(2,1)S(1)} %get-tuple-element.53), channel_id=1, source_target_pairs={{1,2},{2,1},{3,4},{4,3},{5,6},{6,5},{7,8},{8,7},{9,10},{10,9},{11,... | collective-permute-start | bytes 196616 | tf_op jit(solution)/shard_map/ppermute | solution.py:654
  42.5 0.0 copy-done.12
  42.5 0.2 copy.26.send_ref
  42.8 0.8 %coarse_edge_terms.1 = (f32[1024,256]{1,0:T(8,128)S(1)}, f32[256,256]{1,0:T(8,128)S(1)}, bf16[2,256,256]{2,1,0:T(8,128)(2,1)S(1)}) custom-call(s32[1024,1]{1,0:T(8,128)S(1)} %copy.26.send_ref, bf16[1024,256]{1,0:T(8,128)(2,1)S(1)} %copy-done.2, bf16[256,256]{1,0:T(8,128)(2,1)S(1)} %get-tuple-element.47.node_ref, ...), custom_call_target="tpu_custom_call" | custom-call | flops 500000000 | bytes 3000000 | tf_op jit(solution)/shard_map/coarse_edge_terms/pallas_call | solution.py:530
  43.6 0.0 collective-permute-done.6.low_ref
  43.6 5.1 %collective-permute-done.7.high_ref = bf16[128,256]{1,0:T(8,128)(2,1)S(1)} collective-permute-done((bf16[128,256]{1,0:T(8,128)(2,1)S(1)}, bf16[128,256]{1,0:T(8,128)(2,1)S(1)}, u32[]{:S(2)}, u32[]{:S(2)}) %collective-permute-start.7) | collective-permute-done | bytes 65568 | tf_op jit(solution)/shard_map/ppermute | solution.py:654
  48.8 1.8 %coarse_level.1 = bf16[256,256]{1,0:T(8,128)(2,1)} custom-call(s32[1024,1]{1,0:T(8,128)S(1)} %copy.26.send_ref, f32[1024,256]{1,0:T(8,128)S(1)} %get-tuple-element.49.pre_ref, f32[256,256]{1,0:T(8,128)S(1)} %get-tuple-element.50.own_ref, bf16[2,256,256]{2,1,0:T(8,128)(2,1)S(1)} %get-tuple-element.51.w_ref, bf16[256,256]{1,0:T(8,128)(2,1)S(1)} %get-tuple-element.47.node_ref, ...), custom_call_target="tpu_custom_call" | custom-call | flops 500000000 | bytes 3000000 | tf_op jit(solution)/shard_map/coarse_level/pallas_call | solution.py:565
  (8 shorter events, 0.0 us)
Async XLA Ops:
  4.0 9.9 %collective-permute-start = (bf16[512,256]{1,0:T(8,128)(2,1)S(1)}, bf16[512,256]{1,0:T(8,128)(2,1)S(1)}, u32[]{:S(2)}, u32[]{:S(2)}) collective-permute-start(bf16[512,256]{1,0:T(8,128)(2,1)S(1)} %own_rows.1), channel_id=1, source_target_pairs={{0,1},{1,0},{2,3},{3,2},{4,5},{5,4},{6,7},{7,6},{8,9},{9,8},{10,11... | collective-permute-start | bytes 786440 | tf_op jit(solution)/shard_map/ppermute | solution.py:624
  4.1 11.0 %collective-permute-start.1 = (bf16[512,256]{1,0:T(8,128)(2,1)S(1)}, bf16[512,256]{1,0:T(8,128)(2,1)S(1)}, u32[]{:S(2)}, u32[]{:S(2)}) collective-permute-start(bf16[512,256]{1,0:T(8,128)(2,1)S(1)} %get-tuple-element.37), channel_id=1, source_target_pairs={{1,2},{2,1},{3,4},{4,3},{5,6},{6,5},{7,8},{8,7},{9,10},{10,9},{11,... | collective-permute-start | bytes 786440 | tf_op jit(solution)/shard_map/ppermute | solution.py:622
  8.4 6.7 %copy-start.3 = (bf16[2,256,256]{2,1,0:T(8,128)(2,1)S(1)}, bf16[2,256,256]{2,1,0:T(8,128)(2,1)}, u32[]{:S(2)}) copy-start(bf16[2,256,256]{2,1,0:T(8,128)(2,1)} %node_in.3) | copy-start | bytes 786436
  8.4 6.7 %copy-start.8 = (f32[4,256]{1,0:T(4,128)S(1)}, f32[4,256]{1,0:T(4,128)}, u32[]{:S(2)}) copy-start(f32[4,256]{1,0:T(4,128)} %bias.3) | copy-start | bytes 12292
  8.4 6.7 %copy-start.9 = (f32[2,256]{1,0:T(2,128)S(1)}, f32[2,256]{1,0:T(2,128)}, u32[]{:S(2)}) copy-start(f32[2,256]{1,0:T(2,128)} %gain.2) | copy-start | bytes 6148
  15.1 14.6 %copy-start.11 = (s32[2048]{0:T(1024)S(1)}, s32[2048]{0:T(1024)}, u32[]{:S(2)}) copy-start(s32[2048]{0:T(1024)} %param.25) | copy-start | bytes 24580
  26.3 9.5 %copy-start.13 = (s32[256]{0:T(256)S(1)}, s32[256]{0:T(256)}, u32[]{:S(2)}) copy-start(s32[256]{0:T(256)} %param.29) | copy-start | bytes 3076
  26.3 12.8 %copy-start = (bf16[3,256,256]{2,1,0:T(8,128)(2,1)S(1)}, bf16[3,256,256]{2,1,0:T(8,128)(2,1)}, u32[]{:S(2)}) copy-start(bf16[3,256,256]{2,1,0:T(8,128)(2,1)} %edge_in.1) | copy-start | bytes 1179652
  26.3 12.8 %copy-start.6 = (bf16[256,256]{1,0:T(8,128)(2,1)S(1)}, bf16[256,256]{1,0:T(8,128)(2,1)}, u32[]{:S(2)}) copy-start(bf16[256,256]{1,0:T(8,128)(2,1)} %lat_ref.1) | copy-start | bytes 393220
  26.3 16.2 %copy-start.12 = (s32[1024]{0:T(1024)S(1)}, s32[1024]{0:T(1024)}, u32[]{:S(2)}) copy-start(s32[1024]{0:T(1024)} %param.28) | copy-start | bytes 12292
  26.3 16.4 %copy-start.1 = (bf16[2,256,256]{2,1,0:T(8,128)(2,1)S(1)}, bf16[2,256,256]{2,1,0:T(8,128)(2,1)}, u32[]{:S(2)}) copy-start(bf16[2,256,256]{2,1,0:T(8,128)(2,1)} %node_in.5) | copy-start | bytes 786436
  26.3 16.4 %copy-start.2 = (bf16[1024,256]{1,0:T(8,128)(2,1)S(1)}, bf16[1024,256]{1,0:T(8,128)(2,1)}, u32[]{:S(2)}) copy-start(bf16[1024,256]{1,0:T(8,128)(2,1)} %edge_ref.1) | copy-start | bytes 1572868
  26.4 16.4 %copy-start.4 = (bf16[256,256]{1,0:T(8,128)(2,1)S(1)}, bf16[256,256]{1,0:T(8,128)(2,1)}, u32[]{:S(2)}) copy-start(bf16[256,256]{1,0:T(8,128)(2,1)} %edge_out.1) | copy-start | bytes 393220
  26.4 16.4 %copy-start.5 = (bf16[256,256]{1,0:T(8,128)(2,1)S(1)}, bf16[256,256]{1,0:T(8,128)(2,1)}, u32[]{:S(2)}) copy-start(bf16[256,256]{1,0:T(8,128)(2,1)} %node_out.1) | copy-start | bytes 393220
  26.4 16.4 %copy-start.7 = (f32[4,256]{1,0:T(4,128)S(1)}, f32[4,256]{1,0:T(4,128)}, u32[]{:S(2)}) copy-start(f32[4,256]{1,0:T(4,128)} %bias.5) | copy-start | bytes 12292
  26.4 5.6 %collective-permute-start.2 = (bf16[272,128]{1,0:T(8,128)(2,1)S(1)}, bf16[272,128]{1,0:T(8,128)(2,1)S(1)}, u32[]{:S(2)}, u32[]{:S(2)}) collective-permute-start(bf16[272,128]{1,0:T(8,128)(2,1)S(1)} %get-tuple-element.43), channel_id=1, source_target_pairs={{0,64},{64,128},{128,192},{192,0},{1,65},{65,129},{129,193},{193,1... | collective-permute-start | bytes 208904 | tf_op jit(solution)/shard_map/ppermute | solution.py:643
  28.0 4.3 %collective-permute-start.3 = (bf16[272,128]{1,0:T(8,128)(2,1)S(1)}, bf16[272,128]{1,0:T(8,128)(2,1)S(1)}, u32[]{:S(2)}, u32[]{:S(2)}) collective-permute-start(bf16[272,128]{1,0:T(8,128)(2,1)S(1)} %get-tuple-element.44), channel_id=1, source_target_pairs={{64,0},{128,64},{192,128},{0,192},{65,1},{129,65},{193,129},{1,193... | collective-permute-start | bytes 208904 | tf_op jit(solution)/shard_map/ppermute | solution.py:644
  29.7 19.0 %copy-start.10 = (f32[2,256]{1,0:T(2,128)S(1)}, f32[2,256]{1,0:T(2,128)}, u32[]{:S(2)}) copy-start(f32[2,256]{1,0:T(2,128)} %gain.3) | copy-start | bytes 6148
  32.4 6.3 %collective-permute-start.4 = (bf16[272,256]{1,0:T(8,128)(2,1)S(1)}, bf16[272,256]{1,0:T(8,128)(2,1)S(1)}, u32[]{:S(2)}, u32[]{:S(2)}) collective-permute-start(bf16[272,256]{1,0:T(8,128)(2,1)S(1)} %get-tuple-element.45), channel_id=1, source_target_pairs={{0,64},{64,128},{128,192},{192,0},{1,65},{65,129},{129,193},{193,1... | collective-permute-start | bytes 417800 | tf_op jit(solution)/shard_map/ppermute | solution.py:647
  34.1 5.1 %collective-permute-start.5 = (bf16[272,256]{1,0:T(8,128)(2,1)S(1)}, bf16[272,256]{1,0:T(8,128)(2,1)S(1)}, u32[]{:S(2)}, u32[]{:S(2)}) collective-permute-start(bf16[272,256]{1,0:T(8,128)(2,1)S(1)} %get-tuple-element.46), channel_id=1, source_target_pairs={{64,0},{128,64},{192,128},{0,192},{65,1},{129,65},{193,129},{1,193... | collective-permute-start | bytes 417800 | tf_op jit(solution)/shard_map/ppermute | solution.py:648
  39.7 3.9 %collective-permute-start.6 = (bf16[128,256]{1,0:T(8,128)(2,1)S(1)}, bf16[128,256]{1,0:T(8,128)(2,1)S(1)}, u32[]{:S(2)}, u32[]{:S(2)}) collective-permute-start(bf16[128,256]{1,0:T(8,128)(2,1)S(1)} %get-tuple-element.52), channel_id=1, source_target_pairs={{0,1},{1,0},{2,3},{3,2},{4,5},{5,4},{6,7},{7,6},{8,9},{9,8},{10,11... | collective-permute-start | bytes 196616 | tf_op jit(solution)/shard_map/ppermute | solution.py:655
  39.8 8.9 %collective-permute-start.7 = (bf16[128,256]{1,0:T(8,128)(2,1)S(1)}, bf16[128,256]{1,0:T(8,128)(2,1)S(1)}, u32[]{:S(2)}, u32[]{:S(2)}) collective-permute-start(bf16[128,256]{1,0:T(8,128)(2,1)S(1)} %get-tuple-element.53), channel_id=1, source_target_pairs={{1,2},{2,1},{3,4},{4,3},{5,6},{6,5},{7,8},{8,7},{9,10},{10,9},{11,... | collective-permute-start | bytes 196616 | tf_op jit(solution)/shard_map/ppermute | solution.py:654

commit v5 on v4

--- a/solution.py
+++ b/solution.py
@@ -322,7 +322,6 @@
     node_in,
     bias,
     gain,
-    out_hbm,
     out,
     up_ref,
     down_ref,
@@ -332,7 +331,6 @@
     index0,
     index1,
     index_sem,
-    out_sem,
 ):
     nodes = node.shape[0]
     chunks = pre_ref.shape[0] // GATHER
@@ -384,14 +382,11 @@
     hidden = jnp.maximum(own_ref[...] + dot(summed[...], node_in[1]), 0.0).astype(BF16)
     u = scaled_rows(dot(hidden, w_ref[1]) + b_update) * g_update
     out[...] = (node[...].astype(F32) + u).astype(BF16)
-    out_copy = pltpu.make_async_copy(out, out_hbm, out_sem)
-    out_copy.start()
     far = dot(member_ref[0], out[...]).astype(BF16)
     up_ref[:256, :] = far[:, :128]
     down_ref[:256, :] = far[:, 128:]
     up_ref[256:, :] = count_ref[0, :, :128]
     down_ref[256:, :] = count_ref[0, :, 128:]
-    out_copy.wait()
 
 
 def fine_level(terms, table, nodes, low, high, node_in, bias, gain):
@@ -402,46 +397,48 @@
         fine_kernel,
         out_shape=(
             shape((n, 256), BF16),
-            shape((n, 256), BF16),
             shape((272, 128), BF16),
             shape((272, 128), BF16),
             shape(table.shape, F32),
         ),
         in_specs=[VMEM_SPEC] * 13,
-        out_specs=(HBM_SPEC,) + (VMEM_SPEC,) * 4,
+        out_specs=(VMEM_SPEC,) * 4,
         scratch_shapes=[
             pltpu.VMEM((2 * GATHER, 128), F32),
             pltpu.VMEM((n, 256), BF16),
             pltpu.SMEM((GATHER // 128, 128), jnp.int32),
             pltpu.SMEM((GATHER // 128, 128), jnp.int32),
             pltpu.SemaphoreType.DMA((2,)),
-            pltpu.SemaphoreType.DMA,
         ],
-        input_output_aliases={3: 4},
+        input_output_aliases={3: 3},
         cost_estimate=pl.CostEstimate(flops=4_000_000_000, bytes_accessed=8_000_000, transcendentals=0),
         name="fine_level",
         compiler_params=pltpu.CompilerParams(vmem_limit_bytes=14 * 1024 * 1024),
     )(row, pre, own, table, w, member, count, low, high, nodes, node_in, bias, gain)
-    return outs[:4]
-
-
-def pool_kernel(pool, out_ref, next_ref, prev_ref, mine_ref, member, count):
+    return outs[:3]
+
+
+def pool_kernel(pool, out_ref, out_hbm, next_ref, prev_ref, mine_ref, member, count, sem):
+    out_copy = pltpu.make_async_copy(out_ref, out_hbm, sem)
+    out_copy.start()
     for k, (step, ref) in enumerate(((1, next_ref), (3, prev_ref), (0, mine_ref))):
         membership(pool, step, member, k, count, k)
         ref[:256, :] = dot(member[k], out_ref[...]).astype(BF16)
         ref[256:, :] = count[k]
+    out_copy.wait()
 
 
 def pool_rows(pool, out):
     shape = jax.ShapeDtypeStruct((272, 256), BF16)
     return pl.pallas_call(
         pool_kernel,
-        out_shape=(shape,) * 3,
+        out_shape=(jax.ShapeDtypeStruct(out.shape, BF16),) + (shape,) * 3,
         in_specs=[VMEM_SPEC] * 2,
-        out_specs=(VMEM_SPEC,) * 3,
+        out_specs=(HBM_SPEC,) + (VMEM_SPEC,) * 3,
         scratch_shapes=[
             pltpu.VMEM((3, 256, out.shape[0]), BF16),
             pltpu.VMEM((3, 16, 256), BF16),
+            pltpu.SemaphoreType.DMA,
         ],
         cost_estimate=pl.CostEstimate(flops=800_000_000, bytes_accessed=4_000_000, transcendentals=0),
         name="pool_rows",
@@ -635,14 +632,14 @@
         fine_node_out,
         fine_bias,
     )
-    fine_out, fine_near, far_up, far_down = fine_level(
+    fine_near, far_up, far_down = fine_level(
         terms, table, node_near, rim_a, rim_b, fine_node_in, fine_bias, fine_gain
     )
     onward = [(i, (i + 1) % groups) for i in range(groups)]
     back = [(target, source) for source, target in onward]
     far_up = lax.ppermute(far_up, "group", onward)
     far_down = lax.ppermute(far_down, "group", back)
-    next_rows, prev_rows, mine = pool_rows(pool_id.reshape(1, -1), fine_near)
+    fine_out, next_rows, prev_rows, mine = pool_rows(pool_id.reshape(1, -1), fine_near)
     next_rows, prev_rows = relay_rows(next_rows, prev_rows, far_up, far_down)
     below = lax.ppermute(next_rows, "group", onward)
     above = lax.ppermute(prev_rows, "group", back)

time: 50.7 us -> 49.9 us (0.984)
  Pallas kernels: 24.5 us -> 23.7 us
    pallas_call x2, Pallas kernels: 12.4 us -> 11.7 us  [the longest x1 10.3 us: fine_level(): pl.pallas_call(fine_kernel, out_shape=(shape((n, 256), BF16), shape((272,...]
where the time goes in v5:
time: 49.9 us; the launch traced here: 49.8 us
  Pallas kernels  23.7 us (47%)
  starting transfers between devices  13.8 us (28%)
  waiting for transfers between devices  10.9 us (22%)
  between operations  0.92 us (2%)
    pallas_call x1, Pallas kernels, fine_level(): pl.pallas_call(fine_kernel, out_shape=(shape((n, 256), BF16), shape((272,...  10.3 us
    pallas_call x1, Pallas kernels, edge_terms(): pl.pallas_call(edges_kernel, out_shape=(shape((e, 256), F32), shape((n, 2...  5.43 us
    ppermute x1, waiting for transfers between devices, body(): crim_b = lax.ppermute(cborder_b, 'dom', outer)  5.12 us
    ppermute x1, starting transfers between devices, body(): rim_b = lax.ppermute(border_b, 'dom', outer)  4.31 us
    ppermute x1, waiting for transfers between devices, body(): below = lax.ppermute(next_rows, 'group', onward)  2.89 us
    ppermute x1, starting transfers between devices, body(): crim_b = lax.ppermute(cborder_b, 'dom', outer)  2.64 us
    pallas_call x1, Pallas kernels, border_rows(): pl.pallas_call(border_kernel, out_shape=(shape((rim, 256), BF16), shape(n...  2.03 us
    pallas_call x1, Pallas kernels, coarse_level(): pl.pallas_call(coarse_kernel, out_shape=jax.ShapeDtypeStruct(nodes.shape,...  1.8 us
  transfers between devices with their start and end apart: 8, of which 6 were waited for; matrix products, arithmetic and copies ran while one was open for 1% of the time, Pallas kernels for 15%

profile of v5, /device:TPU:128, one launch (start us, length us, event | category | flops | bytes accessed | tf_op | source)
XLA Modules:
  0.0 49.8 jit_solution(3810582277548208631)
XLA Ops:
  0.6 2.0 %border_rows.1 = (bf16[512,256]{1,0:T(8,128)(2,1)S(1)}, bf16[2048,256]{1,0:T(8,128)(2,1)S(1)}, bf16[3,256,256]{2,1,0:T(8,128)(2,1)S(1)}) custom-call(s32[1024]{0:T(1024)} %list_ref.3, bf16[2048,256]{1,0:T(8,128)(2,1)} %node_ref.1, bf16[3,256,256]{2,1,0:T(8,128)(2,1)} %w_ref.2), custom_call_target="tpu_custom_call" | custom-call | flops 70000000 | bytes 2000000 | tf_op jit(solution)/shard_map/border_rows/pallas_call | solution.py:93
  2.7 1.3 %own_rows.1 = bf16[512,256]{1,0:T(8,128)(2,1)S(1)} custom-call(s32[1024]{0:T(1024)} %list_ref.3, bf16[2048,256]{1,0:T(8,128)(2,1)S(1)} %get-tuple-element.28.node.node_ref, bf16[3,256,256]{2,1,0:T(8,128)(2,1)S(1)} %get-tuple-element.29.edge_in.w_ref), custom_call_target="tpu_custom_call" | custom-call | flops 70000000 | bytes 2000000 | tf_op jit(solution)/shard_map/own_rows/pallas_call | solution.py:129
  4.0 0.1 collective-permute-start
  4.1 4.3 %collective-permute-start.1 = (bf16[512,256]{1,0:T(8,128)(2,1)S(1)}, bf16[512,256]{1,0:T(8,128)(2,1)S(1)}, u32[]{:S(2)}, u32[]{:S(2)}) collective-permute-start(bf16[512,256]{1,0:T(8,128)(2,1)S(1)} %get-tuple-element.37), channel_id=1, source_target_pairs={{1,2},{2,1},{3,4},{4,3},{5,6},{6,5},{7,8},{8,7},{9,10},{10,9},{11,... | collective-permute-start | bytes 786440 | tf_op jit(solution)/shard_map/ppermute | solution.py:619
  8.4 0.0 copy-start.3
  8.4 0.0 copy-start.8
  8.4 0.0 copy-start.9
  8.5 5.4 %edge_terms.1 = (f32[8192,256]{1,0:T(8,128)S(1)}, f32[2048,256]{1,0:T(8,128)S(1)}, s32[64,128]{1,0:T(8,128)S(1)}, bf16[2,256,256]{2,1,0:T(8,128)(2,1)S(1)}, bf16...) custom-call(bf16[2048,256]{1,0:T(8,128)(2,1)S(1)} %get-tuple-element.28.node.node_ref, ...), custom_call_target="tpu_custom_call" | custom-call | flops 3000000000 | bytes 8000000 | tf_op jit(solution)/shard_map/edge_terms/pallas_call | solution.py:283
  13.9 0.0 collective-permute-done.low_ref
  13.9 1.2 %collective-permute-done.1.high_ref = bf16[512,256]{1,0:T(8,128)(2,1)S(1)} collective-permute-done((bf16[512,256]{1,0:T(8,128)(2,1)S(1)}, bf16[512,256]{1,0:T(8,128)(2,1)S(1)}, u32[]{:S(2)}, u32[]{:S(2)}) %collective-permute-start.1) | collective-permute-done | bytes 262176 | tf_op jit(solution)/shard_map/ppermute | solution.py:619
  15.1 0.0 copy-done.3
  15.1 0.0 copy-done.8
  15.1 0.0 copy-done.9
  15.1 0.0 copy-start.11
  15.1 10.3 %fine_level.1 = (bf16[2048,256]{1,0:T(8,128)(2,1)S(1)}, bf16[272,128]{1,0:T(8,128)(2,1)S(1)}, bf16[272,128]{1,0:T(8,128)(2,1)S(1)}, f32[6144,128]{1,0:T(8,128)S(1)}) custom-call(s32[64,128]{1,0:T(8,128)S(1)} %get-tuple-element.30.row_ref, f32[8192,256]{1,0:T(8,128)S(1)} %get-tuple-element.31.pre_ref, ...), custom_call_target="tpu_custom_call", output_to_operand_aliasing={{3}: (3, {})} | custom-call | flops 4000000000 | bytes 8000000 | tf_op jit(solution)/shard_map/fine_level/pallas_call | solution.py:396
  25.5 0.0 copy-start.13
  25.5 0.0 copy-start
  25.5 0.0 copy-start.6
  25.5 0.0 copy-start.12
  25.5 0.0 copy-start.1
  25.6 0.0 copy-start.2
  25.6 0.0 copy-start.4
  25.6 0.0 copy-start.5
  25.6 0.0 copy-start.7
  25.6 1.7 %collective-permute-start.2 = (bf16[272,128]{1,0:T(8,128)(2,1)S(1)}, bf16[272,128]{1,0:T(8,128)(2,1)S(1)}, u32[]{:S(2)}, u32[]{:S(2)}) collective-permute-start(bf16[272,128]{1,0:T(8,128)(2,1)S(1)} %get-tuple-element.43), channel_id=1, source_target_pairs={{0,64},{64,128},{128,192},{192,0},{1,65},{65,129},{129,193},{193,1... | collective-permute-start | bytes 208904 | tf_op jit(solution)/shard_map/ppermute | solution.py:640
  27.3 1.7 %collective-permute-start.3 = (bf16[272,128]{1,0:T(8,128)(2,1)S(1)}, bf16[272,128]{1,0:T(8,128)(2,1)S(1)}, u32[]{:S(2)}, u32[]{:S(2)}) collective-permute-start(bf16[272,128]{1,0:T(8,128)(2,1)S(1)} %get-tuple-element.44), channel_id=1, source_target_pairs={{64,0},{128,64},{192,128},{0,192},{65,1},{129,65},{193,129},{1,193... | collective-permute-start | bytes 208904 | tf_op jit(solution)/shard_map/ppermute | solution.py:641
  28.9 0.0 copy-done.11
  28.9 1.3 %pool_rows.1 = (bf16[2048,256]{1,0:T(8,128)(2,1)}, bf16[272,256]{1,0:T(8,128)(2,1)S(1)}, bf16[272,256]{1,0:T(8,128)(2,1)S(1)}, bf16[272,256]{1,0:T(8,128)(2,1)S(1)}) custom-call(s32[1,2048]{1,0:T(1,128)S(1)} %bitcast.5, bf16[2048,256]{1,0:T(8,128)(2,1)S(1)} %get-tuple-element.38.out_ref), custom_call_target="tpu_custom_call" | custom-call | flops 800000000 | bytes 4000000 | tf_op jit(solution)/shard_map/pool_rows/pallas_call | solution.py:433
  30.3 0.9 %collective-permute-done.2.up_ref = bf16[272,128]{1,0:T(8,128)(2,1)S(1)} collective-permute-done((bf16[272,128]{1,0:T(8,128)(2,1)S(1)}, bf16[272,128]{1,0:T(8,128)(2,1)S(1)}, u32[]{:S(2)}, u32[]{:S(2)}) %collective-permute-start.2) | collective-permute-done | bytes 69664 | tf_op jit(solution)/shard_map/ppermute | solution.py:640
  31.2 0.4 collective-permute-done.3.down_ref
  31.6 0.1 relay_rows.1
  31.6 1.7 %collective-permute-start.4 = (bf16[272,256]{1,0:T(8,128)(2,1)S(1)}, bf16[272,256]{1,0:T(8,128)(2,1)S(1)}, u32[]{:S(2)}, u32[]{:S(2)}) collective-permute-start(bf16[272,256]{1,0:T(8,128)(2,1)S(1)} %get-tuple-element.45), channel_id=1, source_target_pairs={{0,64},{64,128},{128,192},{192,0},{1,65},{65,129},{129,193},{193,1... | collective-permute-start | bytes 417800 | tf_op jit(solution)/shard_map/ppermute | solution.py:644
  33.3 1.7 %collective-permute-start.5 = (bf16[272,256]{1,0:T(8,128)(2,1)S(1)}, bf16[272,256]{1,0:T(8,128)(2,1)S(1)}, u32[]{:S(2)}, u32[]{:S(2)}) collective-permute-start(bf16[272,256]{1,0:T(8,128)(2,1)S(1)} %get-tuple-element.46), channel_id=1, source_target_pairs={{64,0},{128,64},{192,128},{0,192},{65,1},{129,65},{193,129},{1,193... | collective-permute-start | bytes 417800 | tf_op jit(solution)/shard_map/ppermute | solution.py:645
  34.9 0.0 copy-done.13
  34.9 0.1 copy.24.list_ref
  35.1 2.9 %collective-permute-done.4.below_ref = bf16[272,256]{1,0:T(8,128)(2,1)S(1)} collective-permute-done((bf16[272,256]{1,0:T(8,128)(2,1)S(1)}, bf16[272,256]{1,0:T(8,128)(2,1)S(1)}, u32[]{:S(2)}, u32[]{:S(2)}) %collective-permute-start.4) | collective-permute-done | bytes 139296 | tf_op jit(solution)/shard_map/ppermute | solution.py:644
  38.0 0.4 collective-permute-done.5.above_ref
  38.3 0.0 copy-done
  38.3 0.0 copy-done.6
  38.3 0.6 %cluster_level.1 = (bf16[256,256]{1,0:T(8,128)(2,1)S(1)}, bf16[256,256]{1,0:T(8,128)(2,1)S(1)}, bf16[128,256]{1,0:T(8,128)(2,1)S(1)}, bf16[128,256]{1,0:T(8,128)(2,1)S(1)}) custom-call(bf16[272,256]{1,0:T(8,128)(2,1)S(1)} %get-tuple-element.40.mine_ref, bf16[272,256]{1,0:T(8,128)(2,1)S(1)} %collective-permute-done.4.below_ref, ...), custom_call_target="tpu_custom_call" | custom-call | flops 70000000 | bytes 1000000 | tf_op jit(solution)/shard_map/cluster_level/pallas_call | solution.py:498
  39.0 0.1 collective-permute-start.6
  39.1 2.6 %collective-permute-start.7 = (bf16[128,256]{1,0:T(8,128)(2,1)S(1)}, bf16[128,256]{1,0:T(8,128)(2,1)S(1)}, u32[]{:S(2)}, u32[]{:S(2)}) collective-permute-start(bf16[128,256]{1,0:T(8,128)(2,1)S(1)} %get-tuple-element.53), channel_id=1, source_target_pairs={{1,2},{2,1},{3,4},{4,3},{5,6},{6,5},{7,8},{8,7},{9,10},{10,9},{11,... | collective-permute-start | bytes 196616 | tf_op jit(solution)/shard_map/ppermute | solution.py:651
  41.7 0.0 copy-done.12
  41.7 0.2 copy.26.send_ref
  42.0 0.8 %coarse_edge_terms.1 = (f32[1024,256]{1,0:T(8,128)S(1)}, f32[256,256]{1,0:T(8,128)S(1)}, bf16[2,256,256]{2,1,0:T(8,128)(2,1)S(1)}) custom-call(s32[1024,1]{1,0:T(8,128)S(1)} %copy.26.send_ref, bf16[1024,256]{1,0:T(8,128)(2,1)S(1)} %copy-done.2, bf16[256,256]{1,0:T(8,128)(2,1)S(1)} %get-tuple-element.47.node_ref, ...), custom_call_target="tpu_custom_call" | custom-call | flops 500000000 | bytes 3000000 | tf_op jit(solution)/shard_map/coarse_edge_terms/pallas_call | solution.py:527
  42.8 0.0 collective-permute-done.6.low_ref
  42.8 5.1 %collective-permute-done.7.high_ref = bf16[128,256]{1,0:T(8,128)(2,1)S(1)} collective-permute-done((bf16[128,256]{1,0:T(8,128)(2,1)S(1)}, bf16[128,256]{1,0:T(8,128)(2,1)S(1)}, u32[]{:S(2)}, u32[]{:S(2)}) %collective-permute-start.7) | collective-permute-done | bytes 65568 | tf_op jit(solution)/shard_map/ppermute | solution.py:651
  48.0 1.8 %coarse_level.1 = bf16[256,256]{1,0:T(8,128)(2,1)} custom-call(s32[1024,1]{1,0:T(8,128)S(1)} %copy.26.send_ref, f32[1024,256]{1,0:T(8,128)S(1)} %get-tuple-element.49.pre_ref, f32[256,256]{1,0:T(8,128)S(1)} %get-tuple-element.50.own_ref, bf16[2,256,256]{2,1,0:T(8,128)(2,1)S(1)} %get-tuple-element.51.w_ref, bf16[256,256]{1,0:T(8,128)(2,1)S(1)} %get-tuple-element.47.node_ref, ...), custom_call_target="tpu_custom_call" | custom-call | flops 500000000 | bytes 3000000 | tf_op jit(solution)/shard_map/coarse_level/pallas_call | solution.py:562
  (8 shorter events, 0.0 us)
Async XLA Ops:
  4.0 9.9 %collective-permute-start = (bf16[512,256]{1,0:T(8,128)(2,1)S(1)}, bf16[512,256]{1,0:T(8,128)(2,1)S(1)}, u32[]{:S(2)}, u32[]{:S(2)}) collective-permute-start(bf16[512,256]{1,0:T(8,128)(2,1)S(1)} %own_rows.1), channel_id=1, source_target_pairs={{0,1},{1,0},{2,3},{3,2},{4,5},{5,4},{6,7},{7,6},{8,9},{9,8},{10,11... | collective-permute-start | bytes 786440 | tf_op jit(solution)/shard_map/ppermute | solution.py:621
  4.1 11.0 %collective-permute-start.1 = (bf16[512,256]{1,0:T(8,128)(2,1)S(1)}, bf16[512,256]{1,0:T(8,128)(2,1)S(1)}, u32[]{:S(2)}, u32[]{:S(2)}) collective-permute-start(bf16[512,256]{1,0:T(8,128)(2,1)S(1)} %get-tuple-element.37), channel_id=1, source_target_pairs={{1,2},{2,1},{3,4},{4,3},{5,6},{6,5},{7,8},{8,7},{9,10},{10,9},{11,... | collective-permute-start | bytes 786440 | tf_op jit(solution)/shard_map/ppermute | solution.py:619
  8.4 6.7 %copy-start.3 = (bf16[2,256,256]{2,1,0:T(8,128)(2,1)S(1)}, bf16[2,256,256]{2,1,0:T(8,128)(2,1)}, u32[]{:S(2)}) copy-start(bf16[2,256,256]{2,1,0:T(8,128)(2,1)} %node_in.3) | copy-start | bytes 786436
  8.4 6.7 %copy-start.8 = (f32[4,256]{1,0:T(4,128)S(1)}, f32[4,256]{1,0:T(4,128)}, u32[]{:S(2)}) copy-start(f32[4,256]{1,0:T(4,128)} %bias.3) | copy-start | bytes 12292
  8.4 6.7 %copy-start.9 = (f32[2,256]{1,0:T(2,128)S(1)}, f32[2,256]{1,0:T(2,128)}, u32[]{:S(2)}) copy-start(f32[2,256]{1,0:T(2,128)} %gain.2) | copy-start | bytes 6148
  15.1 13.8 %copy-start.11 = (s32[2048]{0:T(1024)S(1)}, s32[2048]{0:T(1024)}, u32[]{:S(2)}) copy-start(s32[2048]{0:T(1024)} %param.25) | copy-start | bytes 24580
  25.5 9.5 %copy-start.13 = (s32[256]{0:T(256)S(1)}, s32[256]{0:T(256)}, u32[]{:S(2)}) copy-start(s32[256]{0:T(256)} %param.29) | copy-start | bytes 3076
  25.5 12.8 %copy-start = (bf16[3,256,256]{2,1,0:T(8,128)(2,1)S(1)}, bf16[3,256,256]{2,1,0:T(8,128)(2,1)}, u32[]{:S(2)}) copy-start(bf16[3,256,256]{2,1,0:T(8,128)(2,1)} %edge_in.1) | copy-start | bytes 1179652
  25.5 12.8 %copy-start.6 = (bf16[256,256]{1,0:T(8,128)(2,1)S(1)}, bf16[256,256]{1,0:T(8,128)(2,1)}, u32[]{:S(2)}) copy-start(bf16[256,256]{1,0:T(8,128)(2,1)} %lat_ref.1) | copy-start | bytes 393220
  25.5 16.2 %copy-start.12 = (s32[1024]{0:T(1024)S(1)}, s32[1024]{0:T(1024)}, u32[]{:S(2)}) copy-start(s32[1024]{0:T(1024)} %param.28) | copy-start | bytes 12292
  25.5 16.4 %copy-start.1 = (bf16[2,256,256]{2,1,0:T(8,128)(2,1)S(1)}, bf16[2,256,256]{2,1,0:T(8,128)(2,1)}, u32[]{:S(2)}) copy-start(bf16[2,256,256]{2,1,0:T(8,128)(2,1)} %node_in.5) | copy-start | bytes 786436
  25.6 16.4 %copy-start.2 = (bf16[1024,256]{1,0:T(8,128)(2,1)S(1)}, bf16[1024,256]{1,0:T(8,128)(2,1)}, u32[]{:S(2)}) copy-start(bf16[1024,256]{1,0:T(8,128)(2,1)} %edge_ref.1) | copy-start | bytes 1572868
  25.6 16.4 %copy-start.4 = (bf16[256,256]{1,0:T(8,128)(2,1)S(1)}, bf16[256,256]{1,0:T(8,128)(2,1)}, u32[]{:S(2)}) copy-start(bf16[256,256]{1,0:T(8,128)(2,1)} %edge_out.1) | copy-start | bytes 393220
  25.6 16.4 %copy-start.5 = (bf16[256,256]{1,0:T(8,128)(2,1)S(1)}, bf16[256,256]{1,0:T(8,128)(2,1)}, u32[]{:S(2)}) copy-start(bf16[256,256]{1,0:T(8,128)(2,1)} %node_out.1) | copy-start | bytes 393220
  25.6 16.4 %copy-start.7 = (f32[4,256]{1,0:T(4,128)S(1)}, f32[4,256]{1,0:T(4,128)}, u32[]{:S(2)}) copy-start(f32[4,256]{1,0:T(4,128)} %bias.5) | copy-start | bytes 12292
  25.6 5.6 %collective-permute-start.2 = (bf16[272,128]{1,0:T(8,128)(2,1)S(1)}, bf16[272,128]{1,0:T(8,128)(2,1)S(1)}, u32[]{:S(2)}, u32[]{:S(2)}) collective-permute-start(bf16[272,128]{1,0:T(8,128)(2,1)S(1)} %get-tuple-element.43), channel_id=1, source_target_pairs={{0,64},{64,128},{128,192},{192,0},{1,65},{65,129},{129,193},{193,1... | collective-permute-start | bytes 208904 | tf_op jit(solution)/shard_map/ppermute | solution.py:640
  27.3 4.3 %collective-permute-start.3 = (bf16[272,128]{1,0:T(8,128)(2,1)S(1)}, bf16[272,128]{1,0:T(8,128)(2,1)S(1)}, u32[]{:S(2)}, u32[]{:S(2)}) collective-permute-start(bf16[272,128]{1,0:T(8,128)(2,1)S(1)} %get-tuple-element.44), channel_id=1, source_target_pairs={{64,0},{128,64},{192,128},{0,192},{65,1},{129,65},{193,129},{1,193... | collective-permute-start | bytes 208904 | tf_op jit(solution)/shard_map/ppermute | solution.py:641
  28.9 19.0 %copy-start.10 = (f32[2,256]{1,0:T(2,128)S(1)}, f32[2,256]{1,0:T(2,128)}, u32[]{:S(2)}) copy-start(f32[2,256]{1,0:T(2,128)} %gain.3) | copy-start | bytes 6148
  31.6 6.3 %collective-permute-start.4 = (bf16[272,256]{1,0:T(8,128)(2,1)S(1)}, bf16[272,256]{1,0:T(8,128)(2,1)S(1)}, u32[]{:S(2)}, u32[]{:S(2)}) collective-permute-start(bf16[272,256]{1,0:T(8,128)(2,1)S(1)} %get-tuple-element.45), channel_id=1, source_target_pairs={{0,64},{64,128},{128,192},{192,0},{1,65},{65,129},{129,193},{193,1... | collective-permute-start | bytes 417800 | tf_op jit(solution)/shard_map/ppermute | solution.py:644
  33.3 5.1 %collective-permute-start.5 = (bf16[272,256]{1,0:T(8,128)(2,1)S(1)}, bf16[272,256]{1,0:T(8,128)(2,1)S(1)}, u32[]{:S(2)}, u32[]{:S(2)}) collective-permute-start(bf16[272,256]{1,0:T(8,128)(2,1)S(1)} %get-tuple-element.46), channel_id=1, source_target_pairs={{64,0},{128,64},{192,128},{0,192},{65,1},{129,65},{193,129},{1,193... | collective-permute-start | bytes 417800 | tf_op jit(solution)/shard_map/ppermute | solution.py:645
  39.0 3.9 %collective-permute-start.6 = (bf16[128,256]{1,0:T(8,128)(2,1)S(1)}, bf16[128,256]{1,0:T(8,128)(2,1)S(1)}, u32[]{:S(2)}, u32[]{:S(2)}) collective-permute-start(bf16[128,256]{1,0:T(8,128)(2,1)S(1)} %get-tuple-element.52), channel_id=1, source_target_pairs={{0,1},{1,0},{2,3},{3,2},{4,5},{5,4},{6,7},{7,6},{8,9},{9,8},{10,11... | collective-permute-start | bytes 196616 | tf_op jit(solution)/shard_map/ppermute | solution.py:652
  39.1 8.9 %collective-permute-start.7 = (bf16[128,256]{1,0:T(8,128)(2,1)S(1)}, bf16[128,256]{1,0:T(8,128)(2,1)S(1)}, u32[]{:S(2)}, u32[]{:S(2)}) collective-permute-start(bf16[128,256]{1,0:T(8,128)(2,1)S(1)} %get-tuple-element.53), channel_id=1, source_target_pairs={{1,2},{2,1},{3,4},{4,3},{5,6},{6,5},{7,8},{8,7},{9,10},{10,9},{11,... | collective-permute-start | bytes 196616 | tf_op jit(solution)/shard_map/ppermute | solution.py:651
